TPU v7x, 32 devices: a whole 2x2x4 slice. The times are simulated.
32 devices in a mesh: ctx: 16 (over z, y, x), fsdp: 2 (over core).
Axes of the slice: x: 2, y: 2, z: 4, core: 2. Of those that a mesh axis runs over, the one named last changes fastest.
Arguments:
- layer_input: bfloat16 [2, 2048, 4544], P('fsdp', 'ctx'), may hold values from -6 to 6
- cotangent: bfloat16 [2, 2048, 4544], P('fsdp', 'ctx'), may hold values from -6 to 6
- norm_gain: float32 [4544], replicated, may hold values from 0.5 to 1.5
- norm_bias: float32 [4544], replicated, may hold values from -3 to 3
- qkv_weight: bfloat16 [4544, 4672], P('ctx', 'fsdp'), may hold values from -1 to 1
- up_weight: bfloat16 [4544, 18176], P('ctx', 'fsdp'), may hold values from -0.09375 to 0.09375
- dense_weight: bfloat16 [4544, 4544], P('ctx', 'fsdp'), may hold values from -0.75 to 0.75
- down_weight: bfloat16 [4544, 18176], P('ctx', 'fsdp'), may hold values from -0.046875 to 0.046875
Outputs:
- layer_output: bfloat16 [2, 2048, 4544], P('fsdp', 'ctx')
- input_grad: float32 [2, 2048, 4544], P('fsdp', 'ctx')
- gain_grad: float32 [4544], replicated
- bias_grad: float32 [4544], replicated
- qkv_grad: float32 [4544, 4672], P('ctx', 'fsdp')
- up_grad: float32 [4544, 18176], P('ctx', 'fsdp')
- dense_grad: float32 [4544, 4544], P('ctx', 'fsdp')
- down_grad: float32 [4544, 18176], P('ctx', 'fsdp')
All inputs are finite; a program needn't handle non-finite values.
Results may differ from a plain program's by a relative error of at most 0.04.
Values may be sent and summed in bfloat16 or wider, within the bound.
A program may use at most 1.625 GiB of HBM per device.

v0:
```python
import math

import jax
import jax.numpy as jnp
from jax import lax
from jax.sharding import PartitionSpec as P

HEADS = 71
HEAD = 64


epsilon = 1e-05
rope_base = 10000.0
masked_score = -1e30


def in_blocks(shard, dim, size):
    shape = shard.shape
    blocks = shard.reshape(*shape[:dim], size, shape[dim] // size, *shape[dim + 1 :])
    return jnp.moveaxis(blocks, dim, 0)


def sent_and_summed(shard, axis, dim):
    size = lax.axis_size(axis)
    blocks = lax.all_to_all(in_blocks(shard, dim, size), axis, 0, 0, tiled=True)
    return jnp.sum(blocks.astype(jnp.float32), axis=0)


def layer_norm(values, gain_vec, bias_vec):
    center = values - jnp.mean(values, -1, keepdims=True)
    spread = jnp.mean(center * center, -1, keepdims=True)
    return center * lax.rsqrt(spread + epsilon) * gain_vec + bias_vec


def rotate(values, cosines, sines):
    middle = values.shape[-1] // 2
    turned = jnp.concatenate([-values[..., middle:], values[..., :middle]], -1)
    return values * cosines + turned * sines


def angles(positions, head_size):
    inverse_freq = rope_base ** (-jnp.arange(0, head_size, 2).astype(jnp.float32) / head_size)
    phases = positions.astype(jnp.float32)[:, None] * inverse_freq[None, :]
    phases = jnp.concatenate([phases, phases], -1)
    return (jnp.cos(phases), jnp.sin(phases))


def gather_halves(first, second):
    return (
        lax.all_gather(first, "fsdp", axis=1, tiled=True),
        lax.all_gather(second, "fsdp", axis=1, tiled=True),
    )


def grad_halves(partial_grad):
    return lax.psum_scatter(
        partial_grad.astype(jnp.bfloat16), "fsdp", scatter_dimension=1, tiled=True
    ).astype(jnp.float32)


def fold_inputs(left, first, second):
    return (
        jnp.dot(
            left,
            lax.all_gather(first, "ctx", axis=0, tiled=True),
            preferred_element_type=jnp.float32,
        ),
        jnp.dot(
            left,
            lax.all_gather(second, "ctx", axis=0, tiled=True),
            preferred_element_type=jnp.float32,
        ),
    )


def fold_outputs(first_left, second_left, first, second):
    contract = (((1,), (1,)), ((), ()))
    partial_term = lax.dot_general(
        first_left,
        lax.all_gather(first, "ctx", axis=0, tiled=True),
        contract,
        preferred_element_type=jnp.float32,
    )
    return partial_term + lax.dot_general(
        second_left,
        lax.all_gather(second, "ctx", axis=0, tiled=True),
        contract,
        preferred_element_type=jnp.float32,
    )


def grad_blocks(left, right):
    left_columns = lax.all_to_all(left, "ctx", split_axis=1, concat_axis=0, tiled=True)
    across = (((0,), (0,)), ((), ()))
    return lax.dot_general(
        left_columns,
        lax.all_gather(right, "ctx", axis=0, tiled=True),
        across,
        preferred_element_type=jnp.float32,
    )


def alternate(first, second, pair_count):
    row_total = first.shape[0]
    first_parts = first.reshape(row_total, pair_count, first.shape[1] // pair_count)
    second_parts = second.reshape(row_total, pair_count, second.shape[1] // pair_count)
    return jnp.concatenate([first_parts, second_parts], 2).reshape(row_total, -1)


def block_scores(query_block, keyvals, key_index, key_rows, query_pos, head_size):
    key_block = lax.dynamic_slice_in_dim(keyvals, key_index * key_rows, key_rows, 0)
    raw_scores = lax.dot_general(
        query_block,
        key_block[:, :head_size],
        (((1,), (1,)), ((), ())),
        preferred_element_type=jnp.float32,
    ) * head_size ** (-0.5)
    key_pos = key_index * key_rows + lax.iota(jnp.int32, key_rows)
    return (jnp.where(key_pos[None, :] <= query_pos[:, None], raw_scores, masked_score), key_block)


def attend_forward(queries, keyvals, offset, head_count, head_size):
    row_total = queries.shape[0]
    tokens = row_total // head_count
    query_tokens = math.gcd(32, tokens)
    key_rows = math.gcd(1024, keyvals.shape[0])
    block_rows = query_tokens * head_count
    blocks = queries.reshape(tokens // query_tokens, block_rows, head_size)
    numbers = jnp.arange(tokens // query_tokens, dtype=jnp.int32)

    def one_block(operands):
        query_block, number = operands
        query_pos = offset + number * query_tokens + lax.iota(jnp.int32, block_rows) // head_count
        key_blocks = (offset + (number + 1) * query_tokens + key_rows - 1) // key_rows

        def statistics(key_index, state_pair):
            row_max, exp_sum = state_pair
            scores, key_block = block_scores(
                query_block, keyvals, key_index, key_rows, query_pos, head_size
            )
            new_max = jnp.maximum(row_max, jnp.max(scores, 1))
            exp_sum = exp_sum * jnp.exp(row_max - new_max) + jnp.sum(
                jnp.exp(scores - new_max[:, None]), 1
            )
            return (new_max, exp_sum)

        start_state = (
            jnp.full((block_rows,), masked_score, jnp.float32),
            jnp.zeros((block_rows,), jnp.float32),
        )
        row_max, exp_sum = lax.fori_loop(0, key_blocks, statistics, start_state)

        def one_accumulate(key_index, output_sum):
            scores, key_block = block_scores(
                query_block, keyvals, key_index, key_rows, query_pos, head_size
            )
            probabilities = (jnp.exp(scores - row_max[:, None]) / exp_sum[:, None]).astype(
                jnp.bfloat16
            )
            return output_sum + jnp.dot(
                probabilities, key_block[:, head_size:], preferred_element_type=jnp.float32
            )

        output_sum = lax.fori_loop(
            0, key_blocks, one_accumulate, jnp.zeros((block_rows, head_size), jnp.float32)
        )
        return (output_sum, row_max, exp_sum)

    outputs, row_max, exp_sum = lax.map(one_block, (blocks, numbers))
    return (
        outputs.reshape(row_total, head_size),
        row_max.reshape(row_total),
        exp_sum.reshape(row_total),
    )


def attend_backward(
    queries, keyvals, grad_heads, delta, row_max, exp_sum, offset, head_count, head_size
):
    row_total = queries.shape[0]
    tokens = row_total // head_count
    query_tokens = math.gcd(32, tokens)
    key_rows = math.gcd(1024, keyvals.shape[0])
    block_rows = query_tokens * head_count
    block_count = tokens // query_tokens
    numbers = jnp.arange(block_count, dtype=jnp.int32)
    scale = head_size ** (-0.5)
    across = (((0,), (0,)), ((), ()))

    def one_block(keyval_grad, operands):
        query_block, grad_block, delta_block, max_block, sum_block, number = operands
        query_pos = offset + number * query_tokens + lax.iota(jnp.int32, block_rows) // head_count
        key_blocks = (offset + (number + 1) * query_tokens + key_rows - 1) // key_rows

        def step_back(key_index, state_pair):
            query_grad, keyval_grad = state_pair
            scores, key_block = block_scores(
                query_block, keyvals, key_index, key_rows, query_pos, head_size
            )
            probabilities = jnp.exp(scores - max_block[:, None]) / sum_block[:, None]
            prob_low = probabilities.astype(jnp.bfloat16)
            prob_grad = lax.dot_general(
                grad_block,
                key_block[:, head_size:],
                (((1,), (1,)), ((), ())),
                preferred_element_type=jnp.float32,
            )
            score_grad = (probabilities * (prob_grad - delta_block[:, None])).astype(jnp.bfloat16)
            query_grad = (
                query_grad
                + jnp.dot(score_grad, key_block[:, :head_size], preferred_element_type=jnp.float32)
                * scale
            )
            key_grad = (
                lax.dot_general(score_grad, query_block, across, preferred_element_type=jnp.float32)
                * scale
            )
            value_grad = lax.dot_general(
                prob_low, grad_block, across, preferred_element_type=jnp.float32
            )
            first_row = key_index * key_rows
            current = lax.dynamic_slice_in_dim(keyval_grad, first_row, key_rows, 0)
            keyval_grad = lax.dynamic_update_slice_in_dim(
                keyval_grad, current + jnp.concatenate([key_grad, value_grad], 1), first_row, 0
            )
            return (query_grad, keyval_grad)

        start_state = (jnp.zeros((block_rows, head_size), jnp.float32), keyval_grad)
        query_grad, keyval_grad = lax.fori_loop(0, key_blocks, step_back, start_state)
        return (keyval_grad, query_grad)

    operands = (
        queries.reshape(block_count, block_rows, head_size),
        grad_heads.reshape(block_count, block_rows, head_size),
        delta.reshape(block_count, block_rows),
        row_max.reshape(block_count, block_rows),
        exp_sum.reshape(block_count, block_rows),
        numbers,
    )
    start_grad = jnp.zeros((keyvals.shape[0], 2 * head_size), jnp.float32)
    keyval_grad, query_grads = lax.scan(one_block, start_grad, operands)
    return (query_grads.reshape(row_total, head_size), keyval_grad)


def body(
    layer_input, cotangent, norm_gain, norm_bias, qkv_weight, up_weight, dense_weight, down_weight
):
    head_size = HEAD
    head_count = HEADS
    inputs = layer_input[0].astype(jnp.float32)
    tokens = inputs.shape[0]
    features = inputs.shape[1]
    offset = lax.axis_index("ctx") * tokens
    pair_count = lax.axis_size("fsdp")
    normed = layer_norm(inputs, norm_gain, norm_bias)
    normed_low = normed.astype(jnp.bfloat16)
    whole_qkv, whole_up = gather_halves(qkv_weight, up_weight)
    joined_out, up_raw = fold_inputs(normed_low, whole_qkv, whole_up)
    cosines, sines = angles(offset + lax.iota(jnp.int32, tokens), head_size)
    query_raw = joined_out[:, :features].reshape(tokens, head_count, head_size)
    key_raw = joined_out[:, features : features + head_size]
    value_raw = joined_out[:, features + head_size :]
    query_rot = rotate(query_raw, cosines[:, None, :], sines[:, None, :]).astype(jnp.bfloat16)
    key_rot = rotate(key_raw, cosines, sines).astype(jnp.bfloat16)
    keyvals_mine = jnp.concatenate([key_rot, value_raw.astype(jnp.bfloat16)], 1)
    keyvals = lax.all_gather(keyvals_mine, "ctx", axis=0, tiled=True)
    queries = query_rot.reshape(tokens * head_count, head_size)
    attention, row_max, exp_sum = attend_forward(queries, keyvals, offset, head_count, head_size)
    attended_low = attention.reshape(tokens, features).astype(jnp.bfloat16)
    hidden_low = jax.nn.gelu(up_raw, approximate=False).astype(jnp.bfloat16)
    whole_dense, whole_down = gather_halves(dense_weight, down_weight)
    branch = fold_outputs(attended_low, hidden_low, whole_dense, whole_down)
    layer_output = (inputs + branch).astype(jnp.bfloat16)
    grad_low = cotangent[0]
    whole_dense, whole_down = gather_halves(dense_weight, down_weight)
    grad_attended, grad_hidden = fold_inputs(grad_low, whole_dense, whole_down)
    late_grads = grad_halves(grad_blocks(grad_low, alternate(attended_low, hidden_low, pair_count)))
    dense_cols = dense_weight.shape[1]
    dense_grad = late_grads[:, :dense_cols]
    down_grad = late_grads[:, dense_cols:]
    grad_heads = grad_attended.astype(jnp.bfloat16).reshape(tokens * head_count, head_size)
    delta = jnp.sum(grad_heads.astype(jnp.float32) * attention, 1)
    query_grad, keyval_grad = attend_backward(
        queries, keyvals, grad_heads, delta, row_max, exp_sum, offset, head_count, head_size
    )
    keyval_mine = sent_and_summed(keyval_grad.astype(jnp.bfloat16), "ctx", 0)
    _, query_back = jax.vjp(
        lambda vector: rotate(vector, cosines[:, None, :], sines[:, None, :]), query_raw
    )
    query_unrot = query_back(query_grad.reshape(tokens, head_count, head_size))[0]
    _, key_back = jax.vjp(lambda vector: rotate(vector, cosines, sines), key_raw)
    key_unrot = key_back(keyval_mine[:, :head_size])[0]
    grad_joined = jnp.concatenate(
        [query_unrot.reshape(tokens, features), key_unrot, keyval_mine[:, head_size:]], 1
    ).astype(jnp.bfloat16)
    _, gelu_back = jax.vjp(lambda vector: jax.nn.gelu(vector, approximate=False), up_raw)
    grad_up = gelu_back(grad_hidden)[0].astype(jnp.bfloat16)
    whole_qkv, whole_up = gather_halves(qkv_weight, up_weight)
    grad_normed = fold_outputs(grad_joined, grad_up, whole_qkv, whole_up)
    early_grads = grad_halves(grad_blocks(normed_low, alternate(grad_joined, grad_up, pair_count)))
    qkv_cols = qkv_weight.shape[1]
    qkv_grad = early_grads[:, :qkv_cols]
    up_grad = early_grads[:, qkv_cols:]
    _, norm_back = jax.vjp(layer_norm, inputs, norm_gain, norm_bias)
    input_part, gain_part, bias_part = norm_back(grad_normed)
    gain_grad, bias_grad = lax.psum((gain_part, bias_part), ("ctx", "fsdp"))
    input_grad = grad_low.astype(jnp.float32) + input_part
    return (
        layer_output[None],
        input_grad[None],
        gain_grad,
        bias_grad,
        qkv_grad,
        up_grad,
        dense_grad,
        down_grad,
    )


def solution(mesh):
    return jax.shard_map(
        body,
        mesh=mesh,
        in_specs=(
            P("fsdp", "ctx", None),
            P("fsdp", "ctx", None),
            P(),
            P(),
            P("ctx", "fsdp"),
            P("ctx", "fsdp"),
            P("ctx", "fsdp"),
            P("ctx", "fsdp"),
        ),
        out_specs=(
            P("fsdp", "ctx", None),
            P("fsdp", "ctx", None),
            P(),
            P(),
            P("ctx", "fsdp"),
            P("ctx", "fsdp"),
            P("ctx", "fsdp"),
            P("ctx", "fsdp"),
        ),
        check_vma=False,
    )
```

profile of v0, /device:TPU:15, one launch (start us, length us, event | category | flops | bytes accessed | tf_op | source)
XLA Modules:
  0.0 8371.7 jit_solution(7402094966194372725)
XLA Ops:
  10.0 13.0 all-gather.25.cloned.1.call-done
  30.7 17.7 all-gather.17.cloned.1.call-done
  48.5 14.1 all-gather.29.cloned.1.call-done
  75.6 12.4 all-gather.19.cloned.1.call-done
  94.0 440.7 %all-gather.27.cloned.1.call-done = bf16[16,284,4672]{2,1,0:T(8,128)(2,1)} async-done(((bf16[1,284,4672]{2,1,0:T(8,128)(2,1)}), bf16[16,284,4672]{2,1,0:T(8,128)(2,1)}) %all-gather.27.cloned.1.call-update) | async-done | bytes 42459152 | tf_op jit(solution)/shard_map/all_gather | solution.py:65
  534.7 63.6 reshape.226
  598.3 26.0 fusion.70
  629.3 46.5 all_gather.43
  732.2 9.0 fusion.57
  741.2 72.4 while.146
  831.0 1327.0 %all-gather.33.cloned.1.call-done = bf16[16,284,18176]{2,1,0:T(8,128)(2,1)} async-done(((bf16[1,284,18176]{2,1,0:T(8,128)(2,1)}), bf16[16,284,18176]{2,1,0:T(8,128)(2,1)}) %all-gather.33.cloned.1.call-update) | async-done | bytes 165183504 | tf_op jit(solution)/shard_map/all_gather | solution.py:70
  2157.9 152.7 %reshape.232 = bf16[4544,18176]{1,0:T(8,128)(2,1)} reshape(bf16[16,284,18176]{2,1,0:T(8,128)(2,1)} %all-gather.33.cloned.1.call-done) | data formatting | bytes 330366976
  2310.7 60.7 multiply_convert_fusion
  2378.2 7.6 pad_maximum_fusion.1
  2385.9 208.7 %all-gather.31.cloned.1.call-done = bf16[16,284,4544]{2,1,0:T(8,128)(2,1)} async-done(((bf16[1,284,4544]{2,1,0:T(8,128)(2,1)}), bf16[16,284,4544]{2,1,0:T(8,128)(2,1)}) %all-gather.31.cloned.1.call-update) | async-done | bytes 41295888 | tf_op jit(solution)/shard_map/all_gather | solution.py:80
  2594.6 62.2 reshape.230
  2656.8 22.0 convolution_convert_fusion.2
  2693.4 97.4 %while.148 = (s32[]{:T(128)}, f32[2048,128]{0,1:T(8,128)S(1)}, f32[4,2272,64]{1,0,2:T(4,128)}, s32[4]{0:T(128)S(1)}, s32[]{:T(128)}, /*index=5*/bf16[4,2272,64]{...) while((s32[]{:T(128)}, f32[2048,128]{0,1:T(8,128)S(1)}, ...), condition=%wide.region_14.15_spmd, body=%wide.region_11.14_spmd.sunk | while | flops 1510556672 | bytes 51870676 | solution.py:241
  2698.4 8.3 while.151
  2707.3 10.6 dynamic_update_slice.56
  2722.7 8.3 while.151
  2731.6 10.6 dynamic_update_slice.56
  2747.1 8.3 while.151
  2756.0 10.5 dynamic_update_slice.56
  2771.4 8.3 while.151
  2780.3 10.5 dynamic_update_slice.56
  2792.1 40.1 all-to-all-start
  2832.3 9.4 reshape_reshape.10
  2859.1 1364.5 %all-gather.35.cloned.1.call-done = bf16[16,284,18176]{2,1,0:T(8,128)(2,1)} async-done(((bf16[1,284,18176]{2,1,0:T(8,128)(2,1)}), bf16[16,284,18176]{2,1,0:T(8,128)(2,1)}) %all-gather.35.cloned.1.call-update) | async-done | bytes 165183504 | tf_op jit(solution)/shard_map/all_gather | solution.py:86
  4223.6 150.9 %reshape.234 = bf16[4544,18176]{1,0:T(8,128)(2,1)} reshape(bf16[16,284,18176]{2,1,0:T(8,128)(2,1)} %all-gather.35.cloned.1.call-done) | data formatting | bytes 330366976
  4374.5 61.1 add_convert_fusion
  4450.1 62.0 all_to_all.40
  4513.0 1602.7 %all-gather.23.cloned.1.call-done = bf16[2048,22720]{0,1:T(8,128)(2,1)} async-done(((bf16[128,22720]{0,1:T(8,128)(2,1)}), bf16[2048,22720]{0,1:T(8,128)(2,1)}) %all-gather.23.cloned.1.call-update) | async-done | bytes 93061136 | tf_op jit(solution)/shard_map/all_gather | solution.py:97
  6115.7 42.6 fusion.46
  6158.3 19.1 copy.97
  6181.7 100.1 %all_to_all.41 = bf16[128,16,284]{0,2,1:T(8,128)(2,1)S(1)} all-to-all(bf16[128,16,284]{0,2,1:T(8,128)(2,1)S(1)} %add_convert_fusion.1), channel_id=1, replica_groups=mesh['ctx'=16,'fsdp'=2] {'ctx'}, dimensions={1} | all-to-all | bytes 2326528 | tf_op jit(solution)/shard_map/all_to_all | solution.py:93
  6282.8 1740.0 %all-gather.21.cloned.1.call-done = bf16[2048,22848]{0,1:T(8,128)(2,1)} async-done(((bf16[128,22848]{0,1:T(8,128)(2,1)}), bf16[2048,22848]{0,1:T(8,128)(2,1)}) %all-gather.21.cloned.1.call-update) | async-done | bytes 93585424 | tf_op jit(solution)/shard_map/all_gather | solution.py:97
  8022.8 47.2 convolution_convert_fusion.1
  8070.0 19.0 copy.95
  8091.9 20.9 fusion.75
  8112.8 62.9 fusion.76
  8175.8 22.7 fusion.71
  8203.1 44.7 all-reduce.4
  8252.1 59.2 fusion.55
  8313.0 8.0 slice.88
  8323.4 12.4 copy.124
  8339.3 8.0 slice.86
  8352.0 12.4 copy.122
  (334 shorter events, 354.9 us)
Async XLA Ops:
  7.2 15.8 all-gather.25.cloned.1.call-start
  7.9 40.6 all-gather.17.cloned.1.call-start
  8.6 54.0 all-gather.29.cloned.1.call-start
  9.4 78.6 all-gather.19.cloned.1.call-start
  10.0 524.7 %all-gather.27.cloned.1.call-start = ((), (), s32[]{:S(2)}) async-start(), calls=%async_computation.10 | async-start | bytes 46374912 | tf_op jit(solution)/shard_map/all_gather | solution.py:65
  30.7 2127.3 %all-gather.33.cloned.1.call-start = ((), (), s32[]{:S(2)}) async-start(), calls=%async_computation.13 | async-start | bytes 177979392 | tf_op jit(solution)/shard_map/all_gather | solution.py:70
  48.5 2546.1 %all-gather.31.cloned.1.call-start = ((), (), s32[]{:S(2)}) async-start(), calls=%async_computation.12 | async-start | bytes 45121536 | tf_op jit(solution)/shard_map/all_gather | solution.py:80
  68.6 19.7 copy-start.2
  75.5 15.2 copy-start.18
  75.5 15.2 copy-start.25
  75.5 4148.1 %all-gather.35.cloned.1.call-start = ((), (), s32[]{:S(2)}) async-start(), calls=%async_computation.14 | async-start | bytes 177979392 | tf_op jit(solution)/shard_map/all_gather | solution.py:86
  88.0 6027.7 %all-gather.23.cloned.1.call-start = ((), (), s32[]{:S(2)}) async-start(), calls=%async_computation.8 | async-start | bytes 98877440 | tf_op jit(solution)/shard_map/all_gather | solution.py:97
  88.9 1.8 copy-start.32
  624.4 1.4 copy-start.12
  629.3 79.5 copy-start.23
  629.3 91.1 %copy-start.21 = (f32[128,64]{0,1:T(8,128)}, f32[128,64]{0,1:T(8,128)S(1)}, u32[]{:S(2)}) copy-start(f32[128,64]{0,1:T(8,128)S(1)} %get-tuple-element.858) | copy-start | bytes 98308
  680.0 17.1 copy-start.13
  813.7 1497.0 %copy-start = (bf16[2048,128]{1,0:T(8,128)(2,1)}, bf16[2048,128]{1,0:T(8,128)(2,1)S(1)}, u32[]{:S(2)}) copy-start(bf16[2048,128]{1,0:T(8,128)(2,1)S(1)} %get-tuple-element.1500) | copy-start | bytes 1572868
  813.7 1497.0 %copy-start.6 = (bf16[4,2272,64]{2,1,0:T(8,128)(2,1)}, bf16[4,2272,64]{2,1,0:T(8,128)(2,1)S(1)}, u32[]{:S(2)}) copy-start(bf16[4,2272,64]{2,1,0:T(8,128)(2,1)S(1)} %get-tuple-element.1535) | copy-start | bytes 3489796
  2371.4 6.8 copy-start.17
  2385.9 270.9 %copy-start.9 = (bf16[1,128,4544]{1,2,0:T(8,128)(2,1)S(1)}, bf16[1,128,4544]{1,2,0:T(8,128)(2,1)}, u32[]{:S(2)}) copy-start(bf16[1,128,4544]{1,2,0:T(8,128)(2,1)} %param.19) | copy-start | bytes 3489796
  2680.7 12.7 copy-start.1
  2684.0 9.3 copy-start.7
  2790.8 50.9 copy-start.24
  2792.1 63.9 all-to-all-start
  2832.3 5190.5 %all-gather.21.cloned.1.call-start = ((), (), s32[]{:S(2)}) async-start(), calls=%async_computation.7 | async-start | bytes 99434496 | tf_op jit(solution)/shard_map/all_gather | solution.py:97
  2841.8 4.5 copy-start.5
  2841.8 4.5 copy-start.22
  2846.2 11.0 copy-start.27
  2849.6 1525.0 %copy-start.15 = (bf16[128,71,64]{0,2,1:T(8,128)(2,1)}, bf16[128,71,64]{0,2,1:T(8,128)(2,1)S(1)}, u32[]{:S(2)}) copy-start(bf16[128,71,64]{0,2,1:T(8,128)(2,1)S(1)} %copy.84) | copy-start | bytes 3489796
  2859.1 1515.4 %copy-start.10 = (bf16[1,128,4544]{1,2,0:T(8,128)(2,1)S(1)}, bf16[1,128,4544]{1,2,0:T(8,128)(2,1)}, u32[]{:S(2)}) copy-start(bf16[1,128,4544]{1,2,0:T(8,128)(2,1)} %param.19) | copy-start | bytes 3489796
  4435.7 6.7 copy-start.14
  4449.7 3861.5 %reduce-scatter.9.cloned.1.call-start = ((), (), s32[]{:S(2)}) async-start(), calls=%async_computation.16 | async-start | bytes 26173440
  6177.4 0.8 copy-start.19
  6177.4 1.5 copy-start.3
  6177.4 1.8 copy-start.33
  6177.4 1.8 copy-start.36
  6177.5 2158.3 %reduce-scatter.7.cloned.1.call-start = ((), (), s32[]{:S(2)}) async-start(), calls=%async_computation.15 | async-start | bytes 26320896
  8088.9 1.7 copy-start.8
  8112.7 63.0 copy-start.4
  8112.7 63.0 copy-start.16
  8112.7 63.0 copy-start.20
  8112.7 63.0 copy-start.29
  8112.8 63.0 copy-start.31
  8112.8 63.0 copy-start.34
  8175.7 22.8 copy-start.39
  8175.8 23.4 copy-start.37
  8175.8 72.1 copy-start.11
  (5 other events, 3.1 us)
Sparse Core Ops, SparseCore 0:
  9.5 13.4 all-gather.24
  24.6 23.8 all-gather.16
  50.0 12.5 all-gather.28
  64.0 23.8 all-gather.18
  91.2 443.4 all-gather.26
  537.5 1620.4 all-gather.32
  2161.3 433.2 all-gather.30
  2597.5 1626.0 all-gather.34
  4225.6 1890.0 all-gather.22
  6117.6 1905.1 all-gather.20
  8025.1 34.3 reduce-scatter.8
  8089.1 35.0 reduce-scatter.6
where the time goes:
time: 8390 us; the launch traced here: 8370 us
  waiting for transfers between devices  6750 us (80%)
  local copies, waits for them, and re-layouts  736 us (9%)
  matrix products  491 us (6%)
  blocking collectives  253 us (3%)
    all_gather x2, waiting for transfers between devices, grad_blocks(): lax.all_gather(right, 'ctx', axis=0, tiled=True)  3340 us
    all_gather x1, waiting for transfers between devices, fold_outputs(): lax.all_gather(second, 'ctx', axis=0, tiled=True)  1360 us
    all_gather x1, waiting for transfers between devices, fold_inputs(): lax.all_gather(second, 'ctx', axis=0, tiled=True)  1330 us
    unnamed x98, local copies, waits for them, and re-layouts  522 us
    all_gather x1, waiting for transfers between devices, fold_inputs(): lax.all_gather(first, 'ctx', axis=0, tiled=True)  441 us
    all_gather x1, waiting for transfers between devices, fold_outputs(): lax.all_gather(first, 'ctx', axis=0, tiled=True)  209 us
  transfers between devices with their start and end apart: 13, of which 11 were waited for; matrix products, arithmetic and copies ran while one was open for 15% of the time, Pallas kernels for 0%

commit v1 on v0

v1 whole, which is shorter than its diff:
```python
import functools

import jax
import jax.numpy as jnp
from jax import lax
from jax.experimental import pallas as pl
from jax.experimental.pallas import tpu as pltpu
from jax.sharding import PartitionSpec as P

HEADS = 71
HEAD = 64
EPS = 1e-05
ROPE_BASE = 10000.0
MASKED = -1e30
F32 = jnp.float32
BF16 = jnp.bfloat16
ROWS_COLS = (((1,), (1,)), ((), ()))
ROWS_ROWS = (((0,), (0,)), ((), ()))


def dot(a, b, dims=None):
    if dims is None:
        return jnp.dot(a, b, preferred_element_type=F32)
    return lax.dot_general(a, b, dims, preferred_element_type=F32)


def attend_forward_kernel(q_ref, k_ref, v_ref, o_ref, lse_ref, acc, top):
    index = pl.program_id(1)
    rows = q_ref.shape[1]
    q = q_ref[0]
    acc[...] = jnp.zeros_like(acc)
    top[...] = jnp.full_like(top, MASKED)

    def block(start, masked):
        s = dot(q, k_ref[pl.ds(start, rows), :], ROWS_COLS)
        if masked:
            key = lax.broadcasted_iota(jnp.int32, s.shape, 1)
            query = lax.broadcasted_iota(jnp.int32, s.shape, 0)
            s = jnp.where(key <= query, s, MASKED)
        old = top[...]
        new = jnp.maximum(old, jnp.max(s, 1, keepdims=True))
        p = jnp.exp(s - new).astype(BF16)
        acc[...] = acc[...] * jnp.exp(old - new) + dot(p, v_ref[pl.ds(start, rows), :])
        top[...] = new

    def full(i, carry):
        block(pl.multiple_of(i * rows, rows), False)
        return carry

    lax.fori_loop(0, index, full, 0)
    block(pl.multiple_of(index * rows, rows), True)
    total = acc[...]
    norm = total[:, HEAD : HEAD + 1]
    o_ref[0] = total[:, :HEAD] / norm
    lse_ref[0] = top[...] + jnp.log(norm)


def attend_forward(q, k, v):
    heads, length, _ = q.shape
    rows = min(512, length)
    wide = jnp.concatenate([v, jnp.ones_like(v)], 1)
    return pl.pallas_call(
        attend_forward_kernel,
        grid=(heads, length // rows),
        in_specs=[
            pl.BlockSpec((1, rows, HEAD), lambda h, i: (h, i, 0)),
            pl.BlockSpec((length, HEAD), lambda h, i: (0, 0)),
            pl.BlockSpec((length, 2 * HEAD), lambda h, i: (0, 0)),
        ],
        out_specs=[
            pl.BlockSpec((1, rows, HEAD), lambda h, i: (h, i, 0)),
            pl.BlockSpec((1, rows, 1), lambda h, i: (h, i, 0)),
        ],
        out_shape=[
            jax.ShapeDtypeStruct((heads, length, HEAD), F32),
            jax.ShapeDtypeStruct((heads, length, 1), F32),
        ],
        scratch_shapes=[pltpu.VMEM((rows, 2 * HEAD), F32), pltpu.VMEM((rows, 1), F32)],
        compiler_params=pltpu.CompilerParams(vmem_limit_bytes=40 << 20),
        cost_estimate=pl.CostEstimate(
            flops=2 * heads * length * length * HEAD,
            transcendentals=heads * length * length // 2,
            bytes_accessed=8 * heads * length * HEAD,
        ),
        name="attend_forward",
    )(q, k, wide)


def attend_backward_kernel(q_ref, k_ref, v_ref, g_ref, lse_ref, delta_ref, dq_ref, dk_ref, dv_ref, acc):
    index = pl.program_id(1)
    rows = q_ref.shape[1]

    @pl.when((pl.program_id(0) == 0) & (index == 0))
    def _():
        dk_ref[...] = jnp.zeros_like(dk_ref)
        dv_ref[...] = jnp.zeros_like(dv_ref)

    q = q_ref[0]
    g = g_ref[0]
    lse = lse_ref[0]
    delta = delta_ref[0]
    acc[...] = jnp.zeros_like(acc)

    def block(start, masked):
        at = pl.ds(start, rows)
        k = k_ref[at, :]
        s = dot(k, q, ROWS_COLS)
        p = jnp.exp(s - lse)
        if masked:
            key = lax.broadcasted_iota(jnp.int32, s.shape, 0)
            query = lax.broadcasted_iota(jnp.int32, s.shape, 1)
            p = jnp.where(key <= query, p, 0.0)
        dp = dot(v_ref[at, :], g, ROWS_COLS)
        ds = (p * (dp - delta)).astype(BF16)
        dv_ref[at, :] += dot(p.astype(BF16), g)
        dk_ref[at, :] += dot(ds, q)
        acc[...] += dot(ds, k, ROWS_ROWS)

    def full(i, carry):
        block(pl.multiple_of(i * rows, rows), False)
        return carry

    lax.fori_loop(0, index, full, 0)
    block(pl.multiple_of(index * rows, rows), True)
    dq_ref[0] = acc[...]


def attend_backward(q, k, v, g, lse, delta):
    heads, length, _ = q.shape
    rows = min(512, length)
    per_query = pl.BlockSpec((1, rows, HEAD), lambda h, i: (h, i, 0))
    per_row = pl.BlockSpec((1, 1, rows), lambda h, i: (h, 0, i))
    whole = pl.BlockSpec((length, HEAD), lambda h, i: (0, 0))
    return pl.pallas_call(
        attend_backward_kernel,
        grid=(heads, length // rows),
        in_specs=[per_query, whole, whole, per_query, per_row, per_row],
        out_specs=[per_query, whole, whole],
        out_shape=[
            jax.ShapeDtypeStruct((heads, length, HEAD), F32),
            jax.ShapeDtypeStruct((length, HEAD), F32),
            jax.ShapeDtypeStruct((length, HEAD), F32),
        ],
        scratch_shapes=[pltpu.VMEM((rows, HEAD), F32)],
        compiler_params=pltpu.CompilerParams(vmem_limit_bytes=48 << 20),
        cost_estimate=pl.CostEstimate(
            flops=5 * heads * length * length * HEAD,
            transcendentals=heads * length * length // 2,
            bytes_accessed=12 * heads * length * HEAD,
        ),
        name="attend_backward",
    )(q, k, v, g, lse, delta)


def share_heads(columns, chips):
    rows, width = columns.shape
    heads = width // HEAD
    most = -(-heads // chips)
    richer = heads - chips * (most - 1)
    cut = richer * most * HEAD
    first = jnp.moveaxis(columns[:, :cut].reshape(rows, richer, most * HEAD), 1, 0)
    if richer == chips:
        return first
    rest = jnp.moveaxis(columns[:, cut:].reshape(rows, chips - richer, (most - 1) * HEAD), 1, 0)
    return jnp.concatenate([first, jnp.pad(rest, ((0, 0), (0, 0), (0, HEAD)))], 0)


def join_heads(parts, heads):
    chips, rows, width = parts.shape
    most = width // HEAD
    richer = heads - chips * (most - 1)
    first = jnp.moveaxis(parts[:richer], 0, 1).reshape(rows, -1)
    if richer == chips:
        return first
    rest = jnp.moveaxis(parts[richer:, :, : width - HEAD], 0, 1).reshape(rows, -1)
    return jnp.concatenate([first, rest], 1)


def swap(values):
    return lax.ppermute(values, "fsdp", [(0, 1), (1, 0)])


def in_order(mine, other, core, axis):
    return jnp.where(
        core == 0,
        jnp.concatenate([mine, other], axis),
        jnp.concatenate([other, mine], axis),
    )


def half_of(values, core, axis):
    first, second = jnp.split(values, 2, axis)
    return jnp.where(core == 0, first, second), jnp.where(core == 0, second, first)


def to_columns(shard, chips):
    rows, columns = shard.shape
    blocks = jnp.moveaxis(shard.reshape(rows, chips, columns // chips), 1, 0)
    blocks = lax.all_to_all(blocks, "ctx", 0, 0, tiled=True)
    return blocks.reshape(chips * rows, columns // chips)


def to_rows(shard, chips):
    rows, columns = shard.shape
    blocks = lax.all_to_all(shard.reshape(chips, rows // chips, columns), "ctx", 0, 0, tiled=True)
    return jnp.moveaxis(blocks, 0, 1).reshape(rows // chips, chips * columns)


def rotate(values, cosines, sines):
    middle = values.shape[-1] // 2
    turned = jnp.concatenate([-values[..., middle:], values[..., :middle]], -1)
    return values * cosines + turned * sines


def rotate_back(values, cosines, sines):
    middle = values.shape[-1] // 2
    turned = jnp.concatenate([values[..., middle:], -values[..., :middle]], -1)
    return values * cosines + turned * sines


def angles(length):
    inverse_freq = ROPE_BASE ** (-jnp.arange(0, HEAD, 2).astype(F32) / HEAD)
    phases = jnp.arange(length, dtype=jnp.int32).astype(F32)[:, None] * inverse_freq[None, :]
    phases = jnp.concatenate([phases, phases], -1)
    return jnp.cos(phases), jnp.sin(phases)


def gelu(values):
    return jax.nn.gelu(values, approximate=False)


def body(layer_input, cotangent, norm_gain, norm_bias, qkv_weight, up_weight, dense_weight, down_weight):
    chips = lax.axis_size("ctx")
    core = lax.axis_index("fsdp")
    inputs = layer_input[0].astype(F32)
    tokens, features = inputs.shape
    length = tokens * chips
    heads = features // HEAD
    most = -(-heads // chips)
    qwide = most * HEAD
    shard_rows = qkv_weight.shape[0]
    half_rows = -(-shard_rows // 2)

    center = inputs - jnp.mean(inputs, -1, keepdims=True)
    inverse = lax.rsqrt(jnp.mean(center * center, -1, keepdims=True) + EPS)
    xhat = center * inverse
    normed_low = (xhat * norm_gain + norm_bias).astype(BF16)
    grad_low = cotangent[0]

    qkv_rows = in_order(qkv_weight, swap(qkv_weight), core, 1)
    dense_rows = in_order(dense_weight, swap(dense_weight), core, 1)
    joint = jnp.concatenate([qkv_rows, dense_rows], 1)
    joint = jnp.pad(joint, ((0, 2 * half_rows - shard_rows), (0, 0)))
    joint, _ = half_of(joint, core, 0)
    query_cols, kv_cols, dense_cols = jnp.split(joint, [features, features + 2 * HEAD], 1)
    blocks = jnp.concatenate(
        [
            share_heads(query_cols, chips),
            jnp.broadcast_to(kv_cols, (chips, half_rows, 2 * HEAD)),
            share_heads(dense_cols, chips),
        ],
        2,
    )
    blocks = lax.all_to_all(blocks, "ctx", 0, 0, tiled=True)
    small = in_order(blocks, swap(blocks), core, 1)[:, :shard_rows].reshape(features, -1)
    qkv_cols, dense_cols = small[:, : qwide + 2 * HEAD], small[:, qwide + 2 * HEAD :]
    up_mine = to_columns(up_weight, chips)
    up_cols = jnp.concatenate([up_mine, swap(up_mine)], 1)
    down_mine = to_columns(down_weight, chips)
    down_cols = jnp.concatenate([down_mine, swap(down_mine)], 1)

    normed_all = lax.all_gather(normed_low, "ctx", axis=0, tiled=True)
    grad_all = lax.all_gather(grad_low, "ctx", axis=0, tiled=True)
    joined = dot(normed_all, qkv_cols)
    up_raw = dot(normed_all, up_cols)
    cosines, sines = angles(length)
    scale = HEAD ** (-0.5)
    query_raw = jnp.moveaxis(joined[:, :qwide].reshape(length, most, HEAD), 1, 0)
    queries = (rotate(query_raw, cosines, sines).astype(BF16) * scale).astype(BF16)
    keys = rotate(joined[:, qwide : qwide + HEAD], cosines, sines).astype(BF16)
    values = joined[:, qwide + HEAD :].astype(BF16)
    attention, log_sum = attend_forward(queries, keys, values)
    attended_low = jnp.moveaxis(attention.astype(BF16), 0, 1).reshape(length, qwide)
    hidden_low = gelu(up_raw).astype(BF16)
    branch = dot(attended_low, dense_cols, ROWS_COLS) + dot(hidden_low, down_cols, ROWS_COLS)
    branch = lax.psum_scatter(branch.astype(BF16), "ctx", scatter_dimension=0, tiled=True)
    layer_output = (inputs + branch.astype(F32)).astype(BF16)

    grad_heads = dot(grad_all, dense_cols).astype(BF16)
    grad_heads = jnp.moveaxis(grad_heads.reshape(length, most, HEAD), 1, 0)
    grad_hidden = dot(grad_all, down_cols)
    dense_part = dot(grad_all, attended_low, ROWS_ROWS)
    down_part = dot(grad_all, hidden_low, ROWS_ROWS)
    delta = jnp.sum(grad_heads.astype(F32) * attention, 2)
    query_grad, key_grad, value_grad = attend_backward(
        queries, keys, values, grad_heads, log_sum.reshape(most, 1, length), delta.reshape(most, 1, length)
    )
    query_grad = rotate_back(query_grad * scale, cosines, sines).astype(BF16)
    grad_joined = jnp.concatenate(
        [
            jnp.moveaxis(query_grad, 0, 1).reshape(length, qwide),
            rotate_back(key_grad, cosines, sines).astype(BF16),
            value_grad.astype(BF16),
        ],
        1,
    )
    _, gelu_back = jax.vjp(gelu, up_raw)
    grad_up = gelu_back(grad_hidden)[0].astype(BF16)
    grad_normed = dot(grad_joined, qkv_cols, ROWS_COLS) + dot(grad_up, up_cols, ROWS_COLS)
    grad_normed = lax.psum_scatter(
        grad_normed.astype(BF16), "ctx", scatter_dimension=0, tiled=True
    ).astype(F32)
    qkv_part = dot(normed_all, grad_joined, ROWS_ROWS)
    up_part = dot(normed_all, grad_up, ROWS_ROWS)

    def wide_grad(part):
        mine, other = jnp.split(part, 2, 1)
        total = mine + swap(other.astype(BF16)).astype(F32)
        return to_rows(total.astype(BF16), chips).astype(F32)

    down_grad = wide_grad(down_part)
    up_grad = wide_grad(up_part)
    small_part = jnp.concatenate([qkv_part, dense_part], 1).reshape(chips, shard_rows, -1)
    small_part = jnp.pad(small_part, ((0, 0), (0, 2 * half_rows - shard_rows), (0, 0)))
    mine, other = half_of(small_part, core, 1)
    total = (mine + swap(other.astype(BF16)).astype(F32)).astype(BF16)
    total = lax.all_to_all(total, "ctx", 0, 0, tiled=True)
    qkv_rows = jnp.concatenate(
        [
            join_heads(total[:, :, :qwide], heads),
            jnp.sum(total[:, :, qwide : qwide + 2 * HEAD].astype(F32), 0).astype(BF16),
        ],
        1,
    )
    dense_rows = join_heads(total[:, :, qwide + 2 * HEAD :], heads)

    def own_columns(rows):
        mine, other = half_of(rows, core, 1)
        return in_order(mine, swap(other), core, 0)[:shard_rows].astype(F32)

    qkv_grad = own_columns(qkv_rows)
    dense_grad = own_columns(dense_rows)

    gain_part = jnp.sum(grad_normed * xhat, 0)
    bias_part = jnp.sum(grad_normed, 0)
    gain_grad, bias_grad = lax.psum((gain_part, bias_part), ("ctx", "fsdp"))
    scaled = grad_normed * norm_gain
    input_part = (
        scaled
        - jnp.mean(scaled, -1, keepdims=True)
        - xhat * jnp.mean(scaled * xhat, -1, keepdims=True)
    ) * inverse
    input_grad = grad_low.astype(F32) + input_part
    return (
        layer_output[None],
        input_grad[None],
        gain_grad,
        bias_grad,
        qkv_grad,
        up_grad,
        dense_grad,
        down_grad,
    )


def solution(mesh):
    split = P("ctx", "fsdp")
    stream = P("fsdp", "ctx", None)
    return jax.shard_map(
        body,
        mesh=mesh,
        in_specs=(stream, stream, P(), P(), split, split, split, split),
        out_specs=(stream, stream, P(), P(), split, split, split, split),
        check_vma=False,
    )
```

time: 8390 us -> 2220 us (0.26)
  waiting for transfers between devices: 6750 us -> 1130 us
  local copies, waits for them, and re-layouts: 736 us -> 387 us
  blocking collectives: 253 us -> 39.9 us
  matrix products: 491 us -> 310 us
  Pallas kernels: 0 us -> 99.4 us
    all_gather x10 -> x2, waiting for transfers between devices: 6740 us -> 391 us  [the longest x1 383 us: body(): grad_all = lax.all_gather(grad_low, 'ctx', axis=0, tiled=True)]
    all_to_all x1 -> x6, waiting for transfers between devices: 6.49 us -> 695 us  [the longest x2 332 us: to_columns(): blocks = lax.all_to_all(blocks, 'ctx', 0, 0, tiled=True)]
    unnamed x98 -> x70, local copies, waits for them, and re-layouts: 522 us -> 89.8 us
    dot_general x38 -> x12, matrix products: 491 us -> 310 us  [the longest x8 189 us: dot(): return lax.dot_general(a, b, dims, preferred_element_type=F32)]
    all_to_all x2 -> x0, blocking collectives: 162 us -> none  [grad_blocks(): lax.all_to_all(left, 'ctx', split_axis=1, concat_axis=0, tiled=True)]
    reshape x4 -> x23, local copies, waits for them, and re-layouts: 17.4 us -> 157 us  [the longest x4 47.7 us: to_rows(): shard.reshape(chips, rows // chips, columns)]
    pallas_call x0 -> x2, Pallas kernels: none -> 99.4 us  [the longest x1 51.8 us: attend_forward(): pl.pallas_call(attend_forward_kernel, grid=(heads, length // rows), in_sp...]
  transfers between devices with their start and end apart: 13 -> 20, of which waited for: 11 -> 12; matrix products, arithmetic and copies ran while one was open for 15% -> 26% of each run, Pallas kernels for 0% -> 0%
where the time goes in v1:
time: 2220 us; the launch traced here: 2200 us
  waiting for transfers between devices  1130 us (51%)
  local copies, waits for them, and re-layouts  387 us (17%)
  matrix products  310 us (14%)
  other arithmetic  142 us (6%)
  Pallas kernels  99.4 us (4%)
  starting transfers between devices  79.6 us (4%)
  blocking collectives  39.9 us (2%)
    all_gather x1, waiting for transfers between devices, body(): grad_all = lax.all_gather(grad_low, 'ctx', axis=0, tiled=True)  383 us
    all_to_all x2, waiting for transfers between devices, to_columns(): blocks = lax.all_to_all(blocks, 'ctx', 0, 0, tiled=True)  332 us
    all_to_all x2, waiting for transfers between devices, to_rows(): lax.all_to_all(shard.reshape(chips, rows // chips, columns), 'ctx', 0, 0,...  229 us
    dot_general x8, matrix products, dot(): return lax.dot_general(a, b, dims, preferred_element_type=F32)  189 us
    dot_general x4, matrix products, dot(): return jnp.dot(a, b, preferred_element_type=F32)  122 us
    unnamed x70, local copies, waits for them, and re-layouts  89.8 us
    all_to_all x1, waiting for transfers between devices, body(): total = lax.all_to_all(total, 'ctx', 0, 0, tiled=True)  70.4 us
    all_to_all x1, waiting for transfers between devices, body(): blocks = lax.all_to_all(blocks, 'ctx', 0, 0, tiled=True)  63.5 us
  transfers between devices with their start and end apart: 20, of which 12 were waited for; matrix products, arithmetic and copies ran while one was open for 26% of the time, Pallas kernels for 0%

profile of v1, /device:TPU:15, one launch (start us, length us, event | category | flops | bytes accessed | tf_op | source)
XLA Modules:
  0.0 2204.2 jit_solution(6683267490580159545)
XLA Ops:
  16.6 12.7 reshape.184
  42.3 12.7 reshape.186
  61.5 189.1 %all-to-all-done.1 = bf16[16,284,568]{2,1,0:T(8,128)(2,1)} async-done(((bf16[16,284,568]{2,1,0:T(8,128)(2,1)}), bf16[16,284,568]{2,1,0:T(8,128)(2,1)}, u32[]{:S(2)}, u32[]{:S(2)}) %all-to-all-start.1) | async-done | bytes 5162016 | tf_op jit(solution)/shard_map/all_to_all | solution.py:199
  293.8 143.0 %all-to-all-done.2 = bf16[16,284,568]{2,1,0:T(8,128)(2,1)} async-done(((bf16[16,284,568]{2,1,0:T(8,128)(2,1)}), bf16[16,284,568]{2,1,0:T(8,128)(2,1)}, u32[]{:S(2)}, u32[]{:S(2)}) %all-to-all-start.2) | async-done | bytes 5162016 | tf_op jit(solution)/shard_map/all_to_all | solution.py:199
  436.8 30.7 %all-to-all-start = ((bf16[16,142,768]{2,1,0:T(8,128)(2,1)}), bf16[16,142,768]{2,1,0:T(8,128)(2,1)S(1)}, u32[]{:S(2)}, u32[]{:S(2)}) async-start(bf16[16,142,768]{2,1,0:T(8,128)(2,1)} %copy.154), calls=%async_computation | async-start | bytes 7077888 | tf_op jit(solution)/shard_map/all_to_all | solution.py:264
  467.7 8.5 reshape.185
  503.1 63.5 %all-to-all-done = bf16[16,142,768]{2,1,0:T(8,128)(2,1)S(1)} async-done(((bf16[16,142,768]{2,1,0:T(8,128)(2,1)}), bf16[16,142,768]{2,1,0:T(8,128)(2,1)S(1)}, u32[]{:S(2)}, u32[]{:S(2)}) %all-to-all-start) | async-done | bytes 3489824 | tf_op jit(solution)/shard_map/all_to_all | solution.py:264
  583.1 8.6 select_n.96
  591.7 8.4 copy.166
  616.6 13.2 fusion.40
  632.4 382.5 %all-gather.6.cloned.1.call-done = bf16[1,2048,4544]{1,2,0:T(8,128)(2,1)} async-done(((bf16[1,128,4544]{1,2,0:T(8,128)(2,1)}), bf16[1,2048,4544]{1,2,0:T(8,128)(2,1)}) %all-gather.6.cloned.1.call-update) | async-done | bytes 18612240 | tf_op jit(solution)/shard_map/all_gather | solution.py:273
  1014.9 13.4 fusion.58
  1057.6 51.8 %attend_forward.1 = (f32[5,2048,64]{2,1,0:T(8,128)S(1)}, f32[5,2048,1]{2,1,0:T(8,128)S(1)}) custom-call(bf16[5,2048,64]{2,1,0:T(8,128)(2,1)S(1)} %fusion.66.q_ref, bf16[2048,64]{1,0:T(8,128)(2,1)S(1)} %get-tuple-element.51.k_ref, bf16[2048,128]{1,0:T(8,128)(2,1)S(1)} %concatenate.104.v_ref), custom_call_target="tpu_custom_call" | custom-call | flops 2684354560 | bytes 5242880 | tf_op jit(solution)/shard_map/attend_forward/pallas_call | solution.py:62
  1118.3 47.6 %attend_backward.1 = (f32[5,2048,64]{2,1,0:T(8,128)}, f32[2048,64]{1,0:T(8,128)S(1)}, f32[2048,64]{1,0:T(8,128)S(1)}) custom-call(bf16[5,2048,64]{2,1,0:T(8,128)(2,1)S(1)} %copy-done.2, bf16[2048,64]{1,0:T(8,128)(2,1)S(1)} %get-tuple-element.51.k_ref, bf16[2048,64]{1,0:T(8,128)(2,1)S(1)} %copy.197.v_ref, bf16[5,2048,64]{2,1,0:T(8,128)(2,1)} %bitcast.150, ...), custom_call_target="tpu_custom_call" | custom-call | flops 6710886400 | bytes 7864320 | tf_op jit(solution)/shard_map/attend_backward/pallas_call | solution.py:134
  1186.9 18.9 fusion.38
  1205.8 54.5 %multiply_convert_fusion = (bf16[2048,1136]{0,1:T(8,128)(2,1)}, f32[2048,1136]{0,1:T(8,128)}, f32[2048,1136]{0,1:T(8,128)}) fusion(bf16[2048,4544]{0,1:T(8,128)(2,1)} %all-gather.4.cloned.1.call-done, bf16[4544,568]{1,0:T(8,128)(2,1)} %copy.166, bf16[4544,568]{1,0:T(8,128)(2,1)} %reshape.185), kind=kOutput, calls=%fused_computation.32 | convolution fusion | flops 21315358720 | bytes 52201472 | tf_op jit(solution)/shard_map/dot_general | solution.py:23
  1260.3 40.5 %fusion.15 = bf16[2048,1136]{0,1:T(8,128)(2,1)} fusion(f32[2048,1136]{0,1:T(8,128)} %get-tuple-element.25, bf16[1,2048,4544]{1,2,0:T(8,128)(2,1)} %all-gather.6.cloned.1.call-done, f32[2048,1136]{0,1:T(8,128)} %get-tuple-element.56, bf16[4544,568]{1,0:T(8,128)(2,1)} %copy.169, bf16[4544,568]{1,0:T(8,128)(2,1)} %reshape.187), kind=kOutput, calls=%fused_computation.30 | convolution fusion | flops 21196705792 | bytes 52201472 | tf_op jit(solution)/shard_map/dot_general | solution.py:23
  1300.9 33.0 %add_convert_fusion = bf16[2048,4544]{0,1:T(8,128)(2,1)} fusion(f32[2048,4544]{0,1:T(8,128)} %fusion.38, bf16[2048,1136]{0,1:T(8,128)(2,1)} %fusion.15, bf16[4544,568]{1,0:T(8,128)(2,1)} %copy.166, bf16[4544,568]{1,0:T(8,128)(2,1)} %reshape.185), kind=kOutput, calls=%fused_computation | convolution fusion | flops 21182746624 | bytes 70813696 | tf_op jit(solution)/shard_map/dot_general | solution.py:24
  1333.9 24.9 %copy.190 = bf16[2048,4544]{1,0:T(8,128)(2,1)} copy(bf16[2048,4544]{0,1:T(8,128)(2,1)} %add_convert_fusion) | data formatting | bytes 37224448
  1363.2 20.0 fusion.50
  1383.2 33.7 %add_convert_fusion.1 = bf16[2048,4544]{0,1:T(8,128)(2,1)} fusion(f32[2048,4544]{0,1:T(8,128)} %fusion.50, bf16[2048,1136]{0,1:T(8,128)(2,1)} %get-tuple-element.24, bf16[4544,568]{1,0:T(8,128)(2,1)} %copy.169, bf16[4544,568]{1,0:T(8,128)(2,1)} %reshape.187), kind=kOutput, calls=%fused_computation.1 | convolution fusion | flops 21182746624 | bytes 70813696 | tf_op jit(solution)/shard_map/dot_general | solution.py:24
  1416.8 24.1 %copy.188 = bf16[2048,4544]{1,0:T(8,128)(2,1)} copy(bf16[2048,4544]{0,1:T(8,128)(2,1)} %add_convert_fusion.1) | data formatting | bytes 37224448
  1442.3 10.7 fusion.24
  1453.1 12.0 fusion.86
  1470.7 20.3 reshape.209
  1491.0 19.4 fusion.94
  1510.3 11.4 copy.198
  1521.8 11.4 copy.199
  1537.8 30.1 %fusion.100 = f32[4544,1136]{0,1:T(8,128)} fusion(bf16[2048,4544]{0,1:T(8,128)(2,1)} %all-gather.4.cloned.1.call-done, bf16[2048,1136]{0,1:T(8,128)(2,1)} %fusion.15), kind=kOutput, calls=%fused_computation.168 | convolution fusion | flops 21143486464 | bytes 43913216 | tf_op jit(solution)/shard_map/dot_general | solution.py:24
  1588.0 11.7 all-to-all-start.3
  1599.7 9.3 fusion.8
  1609.0 13.7 reshape.203
  1622.7 10.0 copy.186
  1632.7 70.4 %all-to-all-done.3 = bf16[16,142,768]{2,1,0:T(8,128)(2,1)S(1)} async-done(((bf16[16,142,768]{2,1,0:T(8,128)(2,1)}), bf16[16,142,768]{2,1,0:T(8,128)(2,1)S(1)}, u32[]{:S(2)}, u32[]{:S(2)}) %all-to-all-start.3) | async-done | bytes 3489824 | tf_op jit(solution)/shard_map/all_to_all | solution.py:327
  1709.0 30.2 %convolution_bitcast_fusion = f32[4544,1136]{0,1:T(8,128)} fusion(bf16[2048,1136]{0,1:T(8,128)(2,1)} %get-tuple-element.24, bf16[1,2048,4544]{1,2,0:T(8,128)(2,1)} %all-gather.6.cloned.1.call-done), kind=kOutput, calls=%fused_computation.2 | convolution fusion | flops 21143486464 | bytes 43913216 | tf_op jit(solution)/shard_map/dot_general | solution.py:24
  1743.9 8.8 collective-permute-done.9
  1752.7 9.3 fusion.7
  1762.0 13.7 reshape.204
  1775.7 10.3 copy.187
  1786.0 154.2 %all-to-all-done.4 = bf16[16,284,568]{2,1,0:T(8,128)(2,1)} async-done(((bf16[16,284,568]{2,1,0:T(8,128)(2,1)}), bf16[16,284,568]{2,1,0:T(8,128)(2,1)}, u32[]{:S(2)}, u32[]{:S(2)}) %all-to-all-start.4) | async-done | bytes 5162016 | tf_op jit(solution)/shard_map/all_to_all | solution.py:205
  1974.0 15.5 copy.181
  1989.5 13.6 reshape.199
  2003.1 74.6 %all-to-all-done.5 = bf16[16,284,568]{2,1,0:T(8,128)(2,1)} async-done(((bf16[16,284,568]{2,1,0:T(8,128)(2,1)}), bf16[16,284,568]{2,1,0:T(8,128)(2,1)}, u32[]{:S(2)}, u32[]{:S(2)}) %all-to-all-start.5) | async-done | bytes 5162016 | tf_op jit(solution)/shard_map/all_to_all | solution.py:205
  2077.7 8.8 convert_bitcast_fusion
  2086.5 15.4 copy.185
  2101.9 13.7 reshape.200
  2122.1 39.9 %all-reduce.3 = (f32[4544]{0:T(1024)}, f32[4544]{0:T(1024)}) all-reduce(f32[4544]{0:T(1024)S(1)} %get-tuple-element.18, f32[4544]{0:T(1024)S(1)} %get-tuple-element.21), channel_id=1, replica_groups=mesh['ctx'=16,'fsdp'=2] {'ctx','fsdp'}, use_global_device_ids=true, to_apply=%region_8.9 | all-reduce | flops 9088 | bytes 72704 | tf_op jit(solution)/shard_map/psum | solution.py:346
  2162.7 28.2 %reduce-scatter.7.cloned.1.call-done = bf16[128,4544]{1,0:T(8,128)(2,1)} async-done(((bf16[2048,4544]{1,0:T(8,128)(2,1)}), bf16[128,4544]{1,0:T(8,128)(2,1)}) %reduce-scatter.7.cloned.1.call-update) | async-done | bytes 1163280
  (180 shorter events, 287.8 us)
Async XLA Ops:
  7.2 609.4 %all-gather.4.cloned.1.call-start = ((), (), s32[]{:S(2)}) async-start(), calls=%async_computation.8 | async-start | bytes 19775488 | tf_op jit(solution)/shard_map/all_gather | solution.py:272
  9.1 1.9 copy-start.23
  15.9 999.0 %all-gather.6.cloned.1.call-start = ((), (), s32[]{:S(2)}) async-start(), calls=%async_computation.9 | async-start | bytes 19775488 | tf_op jit(solution)/shard_map/all_gather | solution.py:273
  35.7 214.8 %all-to-all-start.1 = ((bf16[16,284,568]{2,1,0:T(8,128)(2,1)}), bf16[16,284,568]{2,1,0:T(8,128)(2,1)}, u32[]{:S(2)}, u32[]{:S(2)}) async-start(bf16[16,284,568]{2,1,0:T(8,128)(2,1)} %bitcast.149), calls=%async_computation.1 | async-start | bytes 11796480 | tf_op jit(solution)/shard_map/all_to_all | solution.py:199
  250.6 10.3 copy-start.15
  250.6 186.2 %all-to-all-start.2 = ((bf16[16,284,568]{2,1,0:T(8,128)(2,1)}), bf16[16,284,568]{2,1,0:T(8,128)(2,1)}, u32[]{:S(2)}, u32[]{:S(2)}) async-start(bf16[16,284,568]{2,1,0:T(8,128)(2,1)} %bitcast.148), calls=%async_computation.2 | async-start | bytes 11796480 | tf_op jit(solution)/shard_map/all_to_all | solution.py:199
  258.4 6.6 collective-permute-start.1
  260.9 8.7 collective-permute-start
  436.8 129.8 %all-to-all-start = ((bf16[16,142,768]{2,1,0:T(8,128)(2,1)}), bf16[16,142,768]{2,1,0:T(8,128)(2,1)S(1)}, u32[]{:S(2)}, u32[]{:S(2)}) async-start(bf16[16,142,768]{2,1,0:T(8,128)(2,1)} %copy.154), calls=%async_computation | async-start | bytes 7077888 | tf_op jit(solution)/shard_map/all_to_all | solution.py:264
  467.4 1648.1 %reduce-scatter.9.cloned.1.call-start = ((), (), s32[]{:S(2)}) async-start(), calls=%async_computation.11 | async-start | bytes 20054016
  484.5 107.3 %collective-permute-start.3 = (bf16[4544,568]{0,1:T(8,128)(2,1)}, bf16[4544,568]{0,1:T(8,128)(2,1)}, u32[]{:S(2)}, u32[]{:S(2)}) collective-permute-start(bf16[4544,568]{0,1:T(8,128)(2,1)} %copy.165), channel_id=1, source_target_pairs={{0,1},{1,0},{2,3},{3,2},{4,5},{5,4},{6,7},{7,6},{8,9},{9,8},{10,11... | collective-permute-start | bytes 15485960 | tf_op jit(solution)/shard_map/ppermute | solution.py:180
  503.1 97.0 %collective-permute-start.4 = (bf16[4544,568]{0,1:T(8,128)(2,1)}, bf16[4544,568]{0,1:T(8,128)(2,1)}, u32[]{:S(2)}, u32[]{:S(2)}) collective-permute-start(bf16[4544,568]{0,1:T(8,128)(2,1)} %copy.168), channel_id=1, source_target_pairs={{0,1},{1,0},{2,3},{3,2},{4,5},{5,4},{6,7},{7,6},{8,9},{9,8},{10,11... | collective-permute-start | bytes 15485960 | tf_op jit(solution)/shard_map/ppermute | solution.py:180
  567.7 9.4 collective-permute-start.2
  629.8 1.8 copy-start.7
  632.4 399.0 %slice-start.2 = ((f32[2048,448]{0,1:T(8,128)}), f32[2048,64]{0,1:T(8,128)S(1)}, s32[]{:S(2)}) async-start(f32[2048,448]{0,1:T(8,128)} %copy-done.7), calls=%async_computation.14 | async-start | bytes 1048576 | tf_op jit(solution)/shard_map/slice | solution.py:280
  1032.7 6.0 slice-start.3
  1042.4 6.0 copy-start.9
  1048.2 7.5 copy-start.3
  1055.7 1.8 copy-start.8
  1057.5 51.8 %copy-start.1 = (bf16[5,2048,64]{2,1,0:T(8,128)(2,1)}, bf16[5,2048,64]{2,1,0:T(8,128)(2,1)S(1)}, u32[]{:S(2)}) copy-start(bf16[5,2048,64]{2,1,0:T(8,128)(2,1)S(1)} %fusion.66.q_ref) | copy-start | bytes 3932164
  1057.6 51.8 %copy-start.6 = (bf16[2048,5,64]{2,0,1:T(8,128)(2,1)S(1)}, bf16[2048,5,64]{2,0,1:T(8,128)(2,1)}, u32[]{:S(2)}) copy-start(bf16[2048,5,64]{2,0,1:T(8,128)(2,1)} %copy.170) | copy-start | bytes 3932164
  1109.4 3.2 copy-start
  1116.5 1.7 copy-start.2
  1166.2 20.7 copy-start.17
  1171.9 15.0 copy-start.19
  1358.8 1.7 copy-start.5
  1358.9 832.1 %reduce-scatter.7.cloned.1.call-start = ((), (), s32[]{:S(2)}) async-start(), calls=%async_computation.10 | async-start | bytes 20054016
  1442.3 10.8 copy-start.16
  1442.3 10.8 copy-start.18
  1442.3 10.8 copy-start.20
  1533.1 41.9 %slice-start = ((s8[6979584]{0:T(1024)(128)(4,1)}), s8[4194304]{0:T(1024)(128)(4,1)S(1)}, s32[]{:S(2)}) async-start(s8[6979584]{0:T(1024)(128)(4,1)} %bitcast.146), calls=%async_computation.12 | async-start | bytes 8388608
  1537.7 37.3 %slice-start.1 = ((s8[6979584]{0:T(1024)(128)(4,1)}), s8[2785280]{0:T(1024)(128)(4,1)S(1)}, s32[]{:S(2)}) async-start(s8[6979584]{0:T(1024)(128)(4,1)} %bitcast.146), calls=%async_computation.13 | async-start | bytes 5570560
  1537.7 37.3 %collective-permute-start.5 = (bf16[16,142,768]{2,0,1:T(8,128)(2,1)S(1)}, bf16[16,142,768]{2,0,1:T(8,128)(2,1)}, u32[]{:S(2)}, u32[]{:S(2)}) collective-permute-start(bf16[16,142,768]{2,0,1:T(8,128)(2,1)S(1)} %select_convert_fusion), channel_id=1, source_target_pairs={{0,1},{1,0},{2,3},{3,2},{4,5},{5,4},{6,7},{7,6},{8,9},{9,8},{10,11... | collective-permute-start | bytes 10469384 | tf_op jit(solution)/shard_map/ppermute | solution.py:180
  1574.8 24.9 %collective-permute-start.7 = (bf16[4544,568]{0,1:T(8,128)(2,1)}, bf16[4544,568]{0,1:T(8,128)(2,1)}, u32[]{:S(2)}, u32[]{:S(2)}) collective-permute-start(bf16[4544,568]{0,1:T(8,128)(2,1)} %split.85), channel_id=1, source_target_pairs={{0,1},{1,0},{2,3},{3,2},{4,5},{5,4},{6,7},{7,6},{8,9},{9,8},{10,11... | collective-permute-start | bytes 15485960 | tf_op jit(solution)/shard_map/ppermute | solution.py:180
  1588.0 115.1 %all-to-all-start.3 = ((bf16[16,142,768]{2,1,0:T(8,128)(2,1)}), bf16[16,142,768]{2,1,0:T(8,128)(2,1)S(1)}, u32[]{:S(2)}, u32[]{:S(2)}) async-start(bf16[16,142,768]{2,1,0:T(8,128)(2,1)} %copy.177), calls=%async_computation.3 | async-start | bytes 7077888 | tf_op jit(solution)/shard_map/all_to_all | solution.py:327
  1703.1 237.1 %all-to-all-start.4 = ((bf16[16,284,568]{2,1,0:T(8,128)(2,1)}), bf16[16,284,568]{2,1,0:T(8,128)(2,1)}, u32[]{:S(2)}, u32[]{:S(2)}) async-start(bf16[16,284,568]{2,1,0:T(8,128)(2,1)} %copy.186), calls=%async_computation.4 | async-start | bytes 11796480 | tf_op jit(solution)/shard_map/all_to_all | solution.py:205
  1743.8 8.8 collective-permute-start.9
  1940.2 137.5 %all-to-all-start.5 = ((bf16[16,284,568]{2,1,0:T(8,128)(2,1)}), bf16[16,284,568]{2,1,0:T(8,128)(2,1)}, u32[]{:S(2)}, u32[]{:S(2)}) async-start(bf16[16,284,568]{2,1,0:T(8,128)(2,1)} %copy.187), calls=%async_computation.5 | async-start | bytes 11796480 | tf_op jit(solution)/shard_map/all_to_all | solution.py:205
  1951.8 1.9 copy-start.14
  1953.0 4.4 copy-start.12
  1955.2 5.4 collective-permute-start.8
  1957.3 2.7 copy-start.22
  1957.5 3.1 copy-start.13
  1960.5 3.3 collective-permute-start.6
  2101.9 15.9 copy-start.4
  2101.9 15.9 copy-start.21
  2101.9 15.9 copy-start.24
  2115.6 77.7 %copy-start.11 = (bf16[1,128,4544]{1,2,0:T(8,128)(2,1)S(1)}, bf16[1,128,4544]{1,2,0:T(8,128)(2,1)}, u32[]{:S(2)}) copy-start(bf16[1,128,4544]{1,2,0:T(8,128)(2,1)} %param.9) | copy-start | bytes 3489796
  (2 other events, 1.9 us)
Sparse Core Ops, SparseCore 0:
  16.0 600.5 all-gather.3
  618.1 396.7 all-gather.5
  1359.0 335.0 reduce-scatter.8
  1699.8 491.1 reduce-scatter.6

commit v2 on v1

v2 whole, which is shorter than its diff:
```python
import functools

import jax
import jax.numpy as jnp
from jax import lax
from jax.experimental import pallas as pl
from jax.experimental.pallas import tpu as pltpu
from jax.sharding import PartitionSpec as P

HEADS = 71
HEAD = 64
EPS = 1e-05
ROPE_BASE = 10000.0
MASKED = -1e30
LANES = 128
F32 = jnp.float32
BF16 = jnp.bfloat16
ROWS_COLS = (((1,), (1,)), ((), ()))
ROWS_ROWS = (((0,), (0,)), ((), ()))
MESH = pl.DeviceIdType.MESH
ANY = pl.BlockSpec(memory_space=pl.ANY)
WHOLE = pl.BlockSpec(memory_space=pltpu.VMEM)
DMA = pltpu.SemaphoreType.DMA


def dot(a, b, dims=None):
    if dims is None:
        return jnp.dot(a, b, preferred_element_type=F32)
    return lax.dot_general(a, b, dims, preferred_element_type=F32)


def grid_of(chips):
    return (4, 4, 4) if chips == 64 else (chips // 4, 2, 2)


def padded_rows(rows):
    return -(-rows // 16) * 16


def tile_share(tiles, chips):
    return tiles // chips, tiles % chips


class Place:
    def __init__(self, chips):
        self.chips = chips
        self.nz, self.ny, self.nx = grid_of(chips)
        self.me = lax.axis_index("ctx")
        self.core = lax.axis_index("fsdp")
        self.z = self.me // (self.ny * self.nx)
        self.y = lax.rem(self.me // self.nx, self.ny)
        self.x = lax.rem(self.me, self.nx)

    def at(self, dz, dy, dx):
        z = lax.rem(self.z + dz + self.nz, self.nz)
        y = lax.rem(self.y + dy + self.ny, self.ny)
        x = lax.rem(self.x + dx + self.nx, self.nx)
        return (z * self.ny + y) * self.nx + x

    def pair(self, i):
        return self.me ^ i


def enter(place):
    barrier = pltpu.get_barrier_semaphore()

    def greet(i):
        pl.semaphore_signal(barrier, 1, device_id=(place.pair(i), place.core), device_id_type=MESH)

    each(1, place.chips, greet)
    pl.semaphore_signal(barrier, 1, device_id=(place.me, 1 - place.core), device_id_type=MESH)
    pl.semaphore_wait(barrier, place.chips)


def remote(src, dst, send, recv, chip, core):
    return pltpu.make_async_remote_copy(
        src_ref=src, dst_ref=dst, send_sem=send, recv_sem=recv, device_id=(chip, core), device_id_type=MESH
    )


def each(first, last, do):
    def step(i, carry):
        do(i)
        return carry

    lax.fori_loop(first, last, step, 0)


def when(condition, do):
    if condition is None:
        do()
    else:
        pl.when(condition)(do)


def rows_at(start, count):
    return pl.ds(pl.multiple_of(start, 8), count)


def lanes_at(tile, count):
    return pl.ds(pl.multiple_of(tile * LANES, LANES), count * LANES)


def move(src, dst, sem):
    copy = pltpu.make_async_copy(src, dst, sem)
    copy.start()
    copy.wait()


class Tiles:
    def __init__(self, columns, chips):
        self.chips = chips
        self.least, self.richer = tile_share(columns // LANES, chips)
        assert 0 < self.least and 2 * self.richer <= chips

    def more(self, chip, core):
        return jnp.where(core == 0, chip < self.richer, chip >= self.chips - self.richer)

    def first(self, chip, core):
        late = jnp.maximum(chip - (self.chips - self.richer), 0)
        return self.least * chip + jnp.where(core == 0, jnp.minimum(chip, self.richer), late)

    def cut(self, ref, chip, core):
        start = self.first(chip, core)
        return (
            ref.at[:, lanes_at(start, self.least)],
            ref.at[:, lanes_at(jnp.minimum(start + self.least, self.first(self.chips, core) - 1), 1)],
        )


class Gather:
    @staticmethod
    def shape(chips, a):
        return (chips, *a.shape)

    @staticmethod
    def scratch(chips, a):
        nz, ny, nx = grid_of(chips)
        return [DMA((nz,))] * 2 + [DMA((nz, nx))] * 2 + [DMA((nz, ny))] * 2 + [DMA((nz, nx, ny))] * 4 + [DMA]

    def __init__(self, place, mine, out, sems):
        self.p, self.mine, self.out = place, mine, out
        (self.sl, self.rl, self.sx, self.rx, self.sy, self.ry, self.s1, self.r1, self.s2, self.r2, self.own) = sems
        self.half = mine.shape[0] // 2

    def line(self, k):
        p = self.p
        return remote(self.mine, self.out.at[p.me], self.sl.at[k], self.rl.at[k], p.at(k, 0, 0), p.core)

    def across(self, k, i):
        p = self.p
        b = p.at(-k, 0, 0)
        src = self.mine if k == 0 else self.out.at[b]
        return remote(src, self.out.at[b], self.sx.at[k, i], self.rx.at[k, i], p.at(0, 0, i), p.core)

    def along(self, k, j):
        p = self.p
        b = p.at(-k, 0, 0)
        src = self.mine if k == 0 else self.out.at[b]
        return remote(src, self.out.at[b], self.sy.at[k, j], self.ry.at[k, j], p.at(0, j, 0), p.core)

    def corner1(self, k, i, j):
        p = self.p
        part = self.out.at[p.at(-k, 0, -i), pl.ds(0, self.half)]
        return remote(part, part, self.s1.at[k, i, j], self.r1.at[k, i, j], p.at(0, j, 0), p.core)

    def corner2(self, k, i, j):
        p = self.p
        part = self.out.at[p.at(-k, -j, 0), pl.ds(self.half, self.half)]
        return remote(part, part, self.s2.at[k, i, j], self.r2.at[k, i, j], p.at(0, 0, i), p.core)

    def spread(self, k):
        for i in range(1, self.p.nx):
            self.across(k, i).start()
        for j in range(1, self.p.ny):
            self.along(k, j).start()

    def begin(self):
        for k in range(1, self.p.nz):
            self.line(k).start()
        self.spread(0)
        pltpu.make_async_copy(self.mine, self.out.at[self.p.me], self.own).start()

    def turn(self, k):
        p = self.p
        for i in range(1, p.nx):
            self.across(k, i).wait_recv()
            for j in range(1, p.ny):
                self.corner1(k, i, j).start()
        for j in range(1, p.ny):
            self.along(k, j).wait_recv()
            for i in range(1, p.nx):
                self.corner2(k, i, j).start()

    def steps(self):
        nz = self.p.nz
        order = [1, nz - 1] + list(range(2, nz - 1))

        def come(k):
            self.line(k).wait_recv()
            self.spread(k)

        return (
            [functools.partial(self.turn, 0)]
            + [functools.partial(come, k) for k in order]
            + [functools.partial(self.turn, k) for k in order]
        )

    def end(self):
        p = self.p
        pltpu.make_async_copy(self.mine, self.out.at[p.me], self.own).wait()
        for k in range(p.nz):
            if k:
                self.line(k).wait_send()
            for i in range(1, p.nx):
                self.across(k, i).wait_send()
            for j in range(1, p.ny):
                self.along(k, j).wait_send()
            for i in range(1, p.nx):
                for j in range(1, p.ny):
                    self.corner1(k, i, j).wait()
                    self.corner2(k, i, j).wait()


class Columns:
    @staticmethod
    def shape(chips, a):
        least, _ = tile_share(a.shape[1] // LANES, chips)
        return (chips * a.shape[0], (2 * least + 1) * LANES)

    @staticmethod
    def scratch(chips, a):
        return [DMA((chips,))] * 8 + [pltpu.VMEM((a.shape[0], LANES), a.dtype)]

    def __init__(self, place, weight, out, sems):
        self.p, self.w, self.out = place, weight, out
        self.ms, self.mr, self.es, self.er, self.fs, self.fr, self.gs, self.gr, self.nought = sems
        self.tiles = Tiles(weight.shape[1], place.chips)
        self.rows = weight.shape[0]

    def slots(self, chip, own):
        rows = rows_at(chip * self.rows, self.rows)
        least = self.tiles.least
        return self.out.at[rows, lanes_at(0 if own else least + 1, least)], self.out.at[rows, lanes_at(least, 1)]

    def sends(self, i):
        p = self.p
        chip = p.pair(i)
        (a, b), (c, d) = self.tiles.cut(self.w, chip, p.core), self.slots(p.me, True)
        return (
            remote(a, c, self.ms.at[i], self.mr.at[i], chip, p.core),
            remote(b, d, self.es.at[i], self.er.at[i], chip, p.core),
            self.tiles.more(chip, p.core),
        )

    def gets(self, i):
        p = self.p
        chip = p.pair(i)
        (a, b), (c, d) = self.tiles.cut(self.w, chip, p.core), self.slots(chip, True)
        return (
            remote(a, c, self.ms.at[i], self.mr.at[i], chip, p.core),
            remote(b, d, self.es.at[i], self.er.at[i], chip, p.core),
        )

    def passes(self, i):
        p = self.p
        chip = p.pair(i)
        a, b = self.slots(chip, True)
        if isinstance(i, int) and i == 0:
            a, b = self.tiles.cut(self.w, p.me, p.core)
        c, d = self.slots(chip, False)
        return (
            remote(a, c, self.fs.at[i], self.fr.at[i], p.me, 1 - p.core),
            remote(b, d, self.gs.at[i], self.gr.at[i], p.me, 1 - p.core),
        )

    def here(self):
        p = self.p
        (a, b), (c, d) = self.tiles.cut(self.w, p.me, p.core), self.slots(p.me, True)
        return pltpu.make_async_copy(a, c, self.ms.at[0]), pltpu.make_async_copy(b, d, self.es.at[0])

    def begin(self):
        p = self.p

        def send(i):
            main, extra, more = self.sends(i)
            main.start()
            pl.when(more)(extra.start)

        each(1, p.chips, send)
        own, pass_on = self.here(), self.passes(0)
        own[0].start()
        pass_on[0].start()

        @pl.when(self.tiles.more(p.me, p.core))
        def _():
            own[1].start()
            pass_on[1].start()

    def steps(self):
        return [self.hand_on]

    def hand_on(self):
        p = self.p
        mine = self.tiles.more(p.me, p.core)

        def hand(i):
            main, extra = self.gets(i)
            to_main, to_extra = self.passes(i)
            main.wait_recv()
            to_main.start()

            @pl.when(mine)
            def _():
                extra.wait_recv()
                to_extra.start()

        each(1, p.chips, hand)

    def end(self):
        p = self.p
        mine = self.tiles.more(p.me, p.core)
        theirs = self.tiles.more(p.me, 1 - p.core)
        own = self.here()
        own[0].wait()
        pl.when(mine)(own[1].wait)

        @pl.when(jnp.logical_not(mine | theirs))
        def _():
            self.nought[...] = jnp.zeros_like(self.nought)
            each(0, p.chips, lambda c: move(self.nought, self.slots(c, True)[1], self.es.at[0]))

        def sent(i):
            main, extra, more = self.sends(i)
            main.wait_send()
            pl.when(more)(extra.wait_send)

        each(1, p.chips, sent)

        def handed(i):
            main, extra = self.passes(i)
            main.wait()
            pl.when(mine)(extra.wait_send)
            pl.when(theirs)(extra.wait_recv)

        handed(0)
        each(1, p.chips, handed)


class Blocks:
    @staticmethod
    def shape(chips, a):
        return (chips * 2 * a.shape[1], a.shape[2])

    @staticmethod
    def scratch(chips, a):
        return [DMA((chips,))] * 4

    def __init__(self, place, blocks, out, sems):
        self.p, self.b, self.out = place, blocks, out
        self.s, self.r, self.fs, self.fr = sems
        self.rows = blocks.shape[1]

    def slot(self, chip, core):
        return self.out.at[rows_at((2 * chip + core) * self.rows, self.rows)]

    def sends(self, i):
        p = self.p
        chip = p.pair(i)
        return remote(self.b.at[chip], self.slot(p.me, p.core), self.s.at[i], self.r.at[i], chip, p.core)

    def passes(self, i):
        p = self.p
        part = self.slot(p.pair(i), p.core)
        mine = self.b.at[p.me] if isinstance(i, int) and i == 0 else part
        return remote(mine, part, self.fs.at[i], self.fr.at[i], p.me, 1 - p.core)

    def here(self):
        p = self.p
        return pltpu.make_async_copy(self.b.at[p.me], self.slot(p.me, p.core), self.s.at[0])

    def begin(self):
        each(1, self.p.chips, lambda i: self.sends(i).start())
        self.here().start()
        self.passes(0).start()

    def steps(self):
        return [self.hand_on]

    def hand_on(self):
        def hand(i):
            self.sends(i).wait_recv()
            self.passes(i).start()

        each(1, self.p.chips, hand)

    def end(self):
        p = self.p
        self.here().wait()
        each(1, p.chips, lambda i: self.sends(i).wait_send())
        self.passes(0).wait()
        each(1, p.chips, lambda i: self.passes(i).wait())


def drive(parts):
    for part in parts:
        part.begin()
    todo = [part.steps() for part in parts]
    total = max(len(steps) for steps in todo)
    for at in range(total):
        for steps in todo:
            index = at - (total - len(steps))
            if index >= 0:
                steps[index]()
    for part in parts:
        part.end()


def take(refs, counts):
    out, at = [], 0
    for count in counts:
        out.append(refs[at : at + count])
        at += count
    return out


def bring_kernel(chips, plan, *refs):
    n = len(plan)
    ins, outs, held = refs[:n], refs[n : 2 * n], refs[2 * n :]
    place = Place(chips)
    enter(place)
    held = take(held, [count for _, count in plan])
    drive([kind(place, a, o, h) for (kind, _), a, o, h in zip(plan, ins, outs, held)])


def bring(chips, number, name, *jobs):
    held = [kind.scratch(chips, a) for kind, a in jobs]
    return pl.pallas_call(
        functools.partial(bring_kernel, chips, [(kind, len(h)) for (kind, _), h in zip(jobs, held)]),
        in_specs=[ANY] * len(jobs),
        out_specs=[ANY] * len(jobs),
        out_shape=[jax.ShapeDtypeStruct(kind.shape(chips, a), a.dtype) for kind, a in jobs],
        scratch_shapes=[s for h in held for s in h],
        compiler_params=pltpu.CompilerParams(collective_id=number, has_side_effects=True, vmem_limit_bytes=16 << 20),
        name=name,
    )(*[a for _, a in jobs])


class Paired:
    @staticmethod
    def scratch(chips, shape, dtype):
        return [DMA((chips,))] * 5 + [pltpu.VMEM((chips, *shape), dtype)] * 2

    def __init__(self, place, held, views, gives=None, sums=None, comes=lambda j: None):
        self.p = place
        self.cs, self.cr, self.s, self.r, self.load, self.total, self.stage = held
        self.mine, self.theirs, self.target, self.source = views
        self.gives, self.sums, self.comes = gives, sums, comes

    def across(self, i):
        p = self.p
        return remote(self.theirs(p.pair(i)), self.stage.at[i], self.cs.at[i], self.cr.at[i], p.me, 1 - p.core)

    def fetch(self, i):
        return pltpu.make_async_copy(self.mine(self.p.pair(i)), self.total.at[i], self.load.at[i])

    def sends(self, i):
        p = self.p
        j = p.pair(i)
        return remote(self.total.at[i], self.target(j), self.s.at[i], self.r.at[i], j, p.core)

    def gets(self, i):
        p = self.p
        j = p.pair(i)
        return remote(self.total.at[i], self.source(j), self.s.at[i], self.r.at[i], j, p.core)

    def here(self):
        return pltpu.make_async_copy(self.total.at[0], self.source(self.p.me), self.s.at[0])

    def begin(self):
        chips = self.p.chips
        when(self.gives, lambda: each(0, chips, lambda i: self.across(i).start()))
        when(self.sums, lambda: each(0, chips, lambda i: self.fetch(i).start()))

    def add(self, i):
        self.fetch(i).wait()
        self.across(i).wait_recv()
        self.total[i] = (self.total[i].astype(F32) + self.stage[i].astype(F32)).astype(self.total.dtype)

    def some(self, first, last):
        def do(i):
            self.add(i)
            self.sends(i).start()

        when(self.sums, lambda: each(first, last, do))

    def own(self):
        def do():
            self.add(0)
            self.here().start()

        when(self.sums, do)

    def end(self):
        chips = self.p.chips
        when(self.gives, lambda: each(0, chips, lambda i: self.across(i).wait_send()))

        def sent():
            self.here().wait()
            each(1, chips, lambda i: self.sends(i).wait_send())

        when(self.sums, sent)

        def came(i):
            when(self.comes(self.p.pair(i)), lambda: self.gets(i).wait_recv())

        each(1, chips, came)

    def steps(self):
        chips = self.p.chips
        return [functools.partial(self.some, 1, chips), self.own]


class Scatter:
    @staticmethod
    def stages(chips, a):
        nz, _, n = grid_of(chips)
        _, t, d = a.shape
        h = t // 2
        return [(2, nz, n, n, h, d), (2, nz, n, h, d), (2, nz, n, h, d), (nz, t, d), (nz, t, d)]

    @staticmethod
    def scratch(chips, a):
        nz, _, n = grid_of(chips)
        _, t, d = a.shape
        h = t // 2
        most = max(n, nz)
        sems = [DMA((2, nz, n, n))] * 2 + [DMA((2, nz, n))] * 2 + [DMA((nz,))] * 2 + [DMA((most,)), DMA]
        return sems + [pltpu.VMEM((most, h, d), a.dtype), pltpu.VMEM((h, d), a.dtype)]

    def __init__(self, place, blocks, stages, held):
        self.p, self.b = place, blocks
        self.got1, self.sum1, self.got2, self.sum2, self.got3 = stages
        (self.s1, self.r1, self.s2, self.r2, self.s3, self.r3, self.load, self.store, self.parts, self.low) = held
        self.h = blocks.shape[1] // 2
        self.n = place.nx

    def chip(self, half, dz, du, dv):
        return self.p.at(dz, dv, du) if half == 0 else self.p.at(dz, du, dv)

    def rows(self, half):
        return pl.ds(half * self.h, self.h)

    def send1(self, half, dz, v, i):
        return remote(
            self.b.at[self.chip(half, dz, i, v), self.rows(half)],
            self.got1.at[half, dz, v, i],
            self.s1.at[half, dz, v, i],
            self.r1.at[half, dz, v, i],
            self.chip(half, 0, i, 0),
            self.p.core,
        )

    def send2(self, half, dz, v):
        return remote(
            self.sum1.at[half, dz, v],
            self.got2.at[half, dz, v],
            self.s2.at[half, dz, v],
            self.r2.at[half, dz, v],
            self.chip(half, 0, 0, v),
            self.p.core,
        )

    def send3(self, dz):
        return remote(
            self.sum2.at[dz], self.got3.at[dz], self.s3.at[dz], self.r3.at[dz], self.p.at(dz, 0, 0), self.p.core
        )

    def fetch(self, refs):
        loads = [pltpu.make_async_copy(r, self.parts.at[i], self.load.at[i]) for i, r in enumerate(refs)]
        for copy in loads:
            copy.start()
        for copy in loads:
            copy.wait()

    def add(self, refs, to):
        self.fetch(refs)
        total = self.parts[0].astype(F32)
        for i in range(1, len(refs)):
            total = total + self.parts[i].astype(F32)
        self.low[...] = total.astype(self.low.dtype)
        move(self.low, to, self.store)

    def order(self):
        nz = self.p.nz
        return [nz // 2] + [k for k in range(1, nz) if k != nz // 2] + [0]

    def begin(self):
        for dz in self.order():
            for half in (0, 1):
                for v in list(range(1, self.n)) + [0]:
                    for i in range(1, self.n):
                        self.send1(half, dz, v, i).start()

    def first(self, dz):
        for half in (0, 1):
            for v in list(range(1, self.n)) + [0]:
                for i in range(1, self.n):
                    self.send1(half, dz, v, i).wait_recv()
                mine = self.b.at[self.chip(half, dz, 0, v), self.rows(half)]
                self.add([mine] + [self.got1.at[half, dz, v, i] for i in range(1, self.n)], self.sum1.at[half, dz, v])
                if v:
                    self.send2(half, dz, v).start()

    def second(self, dz):
        for half in (0, 1):
            for v in range(1, self.n):
                self.send2(half, dz, v).wait_recv()
            parts = [self.sum1.at[half, dz, 0]] + [self.got2.at[half, dz, v] for v in range(1, self.n)]
            self.add(parts, self.sum2.at[dz, self.rows(half)])
        if dz:
            self.send3(dz).start()

    def last(self):
        for dz in range(1, self.p.nz):
            self.send3(dz).wait_recv()
        for half in (0, 1):
            rows = self.rows(half)
            self.fetch([self.sum2.at[0, rows]] + [self.got3.at[dz, rows] for dz in range(1, self.p.nz)])
            self.finish(half)

    def steps(self):
        order = self.order()
        steps = [functools.partial(self.first, order[0])]
        for old, new in zip(order[:-1], order[1:]):
            steps += [functools.partial(self.first, new), functools.partial(self.second, old)]
        return steps + [functools.partial(self.second, order[-1]), self.last]

    def end(self):
        for dz in range(self.p.nz):
            for half in (0, 1):
                for v in range(self.n):
                    for i in range(1, self.n):
                        self.send1(half, dz, v, i).wait_send()
                    if v:
                        self.send2(half, dz, v).wait_send()
            if dz:
                self.send3(dz).wait_send()


class NormBack(Scatter):
    @staticmethod
    def scratch(chips, a):
        d = a.shape[2]
        more = [pltpu.VMEM((2, 8, d), F32), pltpu.VMEM((2, d), F32), pltpu.VMEM((2, d), F32), pltpu.VMEM((chips, 2, d), F32)]
        return Scatter.scratch(chips, a) + more + [DMA((chips,))] * 2 + [DMA((3,))]

    def __init__(self, place, blocks, stages, held, operands, results, features):
        super().__init__(place, blocks, stages, held[:10])
        self.sums, self.mine, self.other, self.slots, self.ss, self.sr, self.pairs = held[10:]
        self.xhat, self.grad, self.gain, self.inverse = operands
        self.input_grad, self.stats = results
        self.features = features

    def begin(self):
        super().begin()
        self.sums[...] = jnp.zeros_like(self.sums)

    def finish(self, half):
        d = self.xhat.shape[1]

        def some(c):
            at = pl.multiple_of(c * 16, 16)
            total = self.parts[0, pl.ds(at, 16)].astype(F32)
            for i in range(1, self.p.nz):
                total = total + self.parts[i, pl.ds(at, 16)].astype(F32)
            rows = pl.ds(pl.multiple_of(half * self.h + c * 16, 16), 16)
            xhat = self.xhat[rows]
            both = total * xhat
            self.sums[0] += both[:8] + both[8:]
            self.sums[1] += total[:8] + total[8:]
            scaled = total * self.gain[...]
            mean = jnp.sum(scaled, 1, keepdims=True) / self.features
            slope = jnp.sum(scaled * xhat, 1, keepdims=True) / self.features
            change = (scaled - mean - xhat * slope) * self.inverse[rows]
            self.input_grad[rows] = self.grad[rows].astype(F32) + change

        each(0, self.h // 16, some)

    def swap_stats(self):
        p = self.p
        return remote(self.mine, self.other, self.pairs.at[0], self.pairs.at[1], p.me, 1 - p.core)

    def share_stats(self, i):
        p = self.p
        return remote(self.mine, self.slots.at[p.me], self.ss.at[i], self.sr.at[i], p.pair(i), p.core)

    def get_stats(self, i):
        p = self.p
        return remote(self.mine, self.slots.at[p.pair(i)], self.ss.at[i], self.sr.at[i], p.pair(i), p.core)

    def stats_out(self):
        self.mine[0:1] = jnp.sum(self.sums[0], 0, keepdims=True)
        self.mine[1:2] = jnp.sum(self.sums[1], 0, keepdims=True)
        self.swap_stats().start()
        self.swap_stats().wait()
        self.mine[...] += self.other[...]
        self.slots[self.p.me] = self.mine[...]
        each(1, self.p.chips, lambda i: self.share_stats(i).start())

    def steps(self):
        return super().steps() + [self.stats_out]

    def end(self):
        super().end()

        def done(i):
            self.share_stats(i).wait_send()
            self.get_stats(i).wait_recv()

        each(1, self.p.chips, done)
        self.stats[...] = self.slots[0]

        def more(c):
            self.stats[...] += self.slots[c]

        each(1, self.p.chips, more)


def return_parts(place, part, out, held):
    tiles = Tiles(out.shape[1], place.chips)
    least, rows, core, me = tiles.least, out.shape[0], place.core, place.me
    n = len(held) // 2

    def at(j, tile, count):
        return part.at[rows_at(j * rows, rows), lanes_at(tile, count)]

    main = Paired(
        place,
        held[:n],
        (
            lambda j: at(j, 0, least),
            lambda j: at(j, least + 1, least),
            lambda j: tiles.cut(out, me, core)[0],
            lambda j: tiles.cut(out, j, core)[0],
        ),
    )
    extra = Paired(
        place,
        held[n:],
        (
            lambda j: at(j, least, 1),
            lambda j: at(j, least, 1),
            lambda j: tiles.cut(out, me, core)[1],
            lambda j: tiles.cut(out, j, core)[1],
        ),
        tiles.more(me, 1 - core),
        tiles.more(me, core),
        lambda j: tiles.more(j, core),
    )
    return [main, extra]


def trade_parts(place, part, out, held):
    rows = out.shape[1]

    def at(j, core):
        return part.at[rows_at((2 * j + core) * rows, rows)]

    views = (
        lambda j: at(j, place.core),
        lambda j: at(j, 1 - place.core),
        lambda j: out.at[place.me],
        lambda j: out.at[j],
    )
    return [Paired(place, held, views)]


def send_kernel(chips, features, counts, *refs):
    blocks, wide, small, xhat, grad, gain, inverse = refs[:7]
    input_grad, stats, wide_out, small_out = refs[7:11]
    stages = refs[11:16]
    norm_held, wide_held, small_held = take(refs[16:], counts)
    place = Place(chips)
    enter(place)
    norm = NormBack(place, blocks, stages, norm_held, (xhat, grad, gain, inverse), (input_grad, stats), features)
    parts = return_parts(place, wide, wide_out, wide_held)
    parts += trade_parts(place, small, small_out, small_held)
    for part in [norm] + parts:
        part.begin()
    for part in parts + [norm]:
        for step in part.steps():
            step()
    for part in [norm] + parts:
        part.end()


def send(chips, number, features, blocks, wide, columns, small, xhat, grad, gain, inverse):
    _, tokens, d = blocks.shape
    rows = d // chips
    least, _ = tile_share(columns // LANES, chips)
    width = small.shape[1]
    held = [
        NormBack.scratch(chips, blocks),
        Paired.scratch(chips, (rows, least * LANES), BF16) + Paired.scratch(chips, (rows, LANES), BF16),
        Paired.scratch(chips, (rows // 2, width), BF16),
    ]
    low = lambda *shape: jax.ShapeDtypeStruct(shape, BF16)
    results = pl.pallas_call(
        functools.partial(send_kernel, chips, features, [len(h) for h in held]),
        in_specs=[ANY] * 3 + [WHOLE] * 4,
        out_specs=[WHOLE] * 2 + [ANY] * 7,
        out_shape=[
            jax.ShapeDtypeStruct((tokens, d), F32),
            jax.ShapeDtypeStruct((2, d), F32),
            low(rows, columns),
            low(chips, rows // 2, width),
        ]
        + [low(*s) for s in Scatter.stages(chips, blocks)],
        scratch_shapes=[s for h in held for s in h],
        compiler_params=pltpu.CompilerParams(collective_id=number, has_side_effects=True, vmem_limit_bytes=48 << 20),
        name="send",
    )(blocks, wide, small, xhat, grad, gain, inverse)
    return results[:4]


def untile_kernel(parts_ref, out_ref, low, high, load, main_sem, extra_sem):
    chips = parts_ref.shape[0]
    rows = out_ref.shape[0]
    core = lax.axis_index("fsdp")
    tiles = Tiles(out_ref.shape[1], chips)
    least = tiles.least

    def bring_in(chip, slot):
        return pltpu.make_async_copy(parts_ref.at[chip], low.at[slot], load.at[slot])

    def stores(chip, slot):
        main, extra = tiles.cut(out_ref, chip, core)
        return (
            pltpu.make_async_copy(high.at[slot, :, lanes_at(0, least)], main, main_sem.at[slot]),
            pltpu.make_async_copy(high.at[slot, :, lanes_at(least, 1)], extra, extra_sem.at[slot]),
        )

    def finish(chip, slot):
        main, extra = stores(chip, slot)
        main.wait()
        pl.when(tiles.more(chip, core))(extra.wait)

    bring_in(0, 0).start()

    def step(chip):
        slot = lax.rem(chip, 2)
        pl.when(chip + 1 < chips)(lambda: bring_in(chip + 1, 1 - slot).start())
        bring_in(chip, slot).wait()
        pl.when(chip >= 2)(lambda: finish(chip - 2, slot))
        high[slot] = low[slot, :rows].astype(F32)
        main, extra = stores(chip, slot)
        main.start()
        pl.when(tiles.more(chip, core))(extra.start)

    each(0, chips, step)
    finish(chips - 2, chips % 2)
    finish(chips - 1, 1 - chips % 2)


def untile(parts, rows, columns):
    _, high, width = parts.shape
    return pl.pallas_call(
        untile_kernel,
        in_specs=[ANY],
        out_specs=ANY,
        out_shape=jax.ShapeDtypeStruct((rows, columns), F32),
        scratch_shapes=[pltpu.VMEM((2, high, width), BF16), pltpu.VMEM((2, rows, width), F32)] + [DMA((2,))] * 3,
        compiler_params=pltpu.CompilerParams(vmem_limit_bytes=24 << 20),
        cost_estimate=pl.CostEstimate(flops=0, transcendentals=0, bytes_accessed=6 * rows * columns),
        name="untile",
    )(parts)


def rotate(values, cosines, sines):
    middle = values.shape[-1] // 2
    turned = jnp.concatenate([-values[..., middle:], values[..., :middle]], -1)
    return values * cosines + turned * sines


def rotate_back(values, cosines, sines):
    middle = values.shape[-1] // 2
    turned = jnp.concatenate([values[..., middle:], -values[..., :middle]], -1)
    return values * cosines + turned * sines


def attend_forward_kernel(lead, q_ref, k_ref, v_ref, low_ref, o_ref, lse_ref, acc, top):
    index = pl.program_id(0)
    heads, rows, _ = q_ref.shape
    outs = []
    for h in range(heads):
        q = q_ref[h]
        acc[...] = jnp.zeros_like(acc)
        top[...] = jnp.full_like(top, MASKED)

        def block(start, masked):
            s = dot(q, k_ref[pl.ds(start, rows), :], ROWS_COLS)
            if masked:
                key = lax.broadcasted_iota(jnp.int32, s.shape, 1)
                query = lax.broadcasted_iota(jnp.int32, s.shape, 0)
                s = jnp.where(key <= query, s, MASKED)
            old = top[...]
            new = jnp.maximum(old, jnp.max(s, 1, keepdims=True))
            p = jnp.exp(s - new).astype(BF16)
            acc[...] = acc[...] * jnp.exp(old - new) + dot(p, v_ref[pl.ds(start, rows), :])
            top[...] = new

        each(0, index, lambda i: block(pl.multiple_of(i * rows, rows), False))
        block(pl.multiple_of(index * rows, rows), True)
        total = acc[...]
        norm = total[:, HEAD : HEAD + 1]
        out = total[:, :HEAD] / norm
        o_ref[h] = out
        outs.append(out.astype(BF16))
        lse = jnp.broadcast_to(top[...] + jnp.log(norm), (rows, LANES))
        lse_ref[h] = lse.T[:1]
    if lead:
        outs = [jnp.zeros((rows, lead), BF16)] + outs
    low_ref[...] = jnp.concatenate(outs, 1)


def attend_forward(q, k, v, lead):
    heads, length, _ = q.shape
    rows = min(512, length)
    width = lead + heads * HEAD
    wide = jnp.concatenate([v, jnp.ones_like(v)], 1)
    return pl.pallas_call(
        functools.partial(attend_forward_kernel, lead),
        grid=(length // rows,),
        in_specs=[
            pl.BlockSpec((heads, rows, HEAD), lambda i: (0, i, 0)),
            pl.BlockSpec((length, HEAD), lambda i: (0, 0)),
            pl.BlockSpec((length, 2 * HEAD), lambda i: (0, 0)),
        ],
        out_specs=[
            pl.BlockSpec((rows, width), lambda i: (i, 0)),
            pl.BlockSpec((heads, rows, HEAD), lambda i: (0, i, 0)),
            pl.BlockSpec((heads, 1, rows), lambda i: (0, 0, i)),
        ],
        out_shape=[
            jax.ShapeDtypeStruct((length, width), BF16),
            jax.ShapeDtypeStruct((heads, length, HEAD), F32),
            jax.ShapeDtypeStruct((heads, 1, length), F32),
        ],
        scratch_shapes=[pltpu.VMEM((rows, 2 * HEAD), F32), pltpu.VMEM((rows, 1), F32)],
        compiler_params=pltpu.CompilerParams(vmem_limit_bytes=40 << 20),
        cost_estimate=pl.CostEstimate(
            flops=2 * heads * length * length * HEAD,
            transcendentals=heads * length * length // 2,
            bytes_accessed=8 * heads * length * HEAD,
        ),
        name="attend_forward",
    )(q, k, wide)


def attend_backward_kernel(q_ref, k_ref, v_ref, g_ref, o_ref, lse_ref, cos_ref, sin_ref, out_ref, acc, dk, dv):
    index = pl.program_id(0)
    heads, rows, _ = q_ref.shape
    scale = HEAD ** (-0.5)

    @pl.when(index == 0)
    def _():
        dk[...] = jnp.zeros_like(dk)
        dv[...] = jnp.zeros_like(dv)
        out_ref[...] = jnp.zeros_like(out_ref)

    here = pl.ds(pl.multiple_of(index * rows, rows), rows)
    cosines, sines = cos_ref[here], sin_ref[here]
    grads = []
    for h in range(heads):
        q = q_ref[h]
        g = g_ref[h]
        lse = lse_ref[h]
        delta = jnp.sum((g.astype(F32) * o_ref[h]).T, 0, keepdims=True)
        acc[...] = jnp.zeros_like(acc)

        def block(start, masked):
            at = pl.ds(start, rows)
            k = k_ref[at, :]
            p = jnp.exp(dot(k, q, ROWS_COLS) - lse)
            if masked:
                key = lax.broadcasted_iota(jnp.int32, p.shape, 0)
                query = lax.broadcasted_iota(jnp.int32, p.shape, 1)
                p = jnp.where(key <= query, p, 0.0)
            dp = dot(v_ref[at, :], g, ROWS_COLS)
            ds = (p * (dp - delta)).astype(BF16)
            dv[at, :] += dot(p.astype(BF16), g)
            dk[at, :] += dot(ds, q)
            acc[...] += dot(ds, k, ROWS_ROWS)

        each(0, index, lambda i: block(pl.multiple_of(i * rows, rows), False))
        block(pl.multiple_of(index * rows, rows), True)
        grads.append(rotate_back(acc[...] * scale, cosines, sines).astype(BF16))
    out_ref[here, : heads * HEAD] = jnp.concatenate(grads, 1)

    @pl.when(index == pl.num_programs(0) - 1)
    def _():
        keys = rotate_back(dk[...], cos_ref[...], sin_ref[...]).astype(BF16)
        both = jnp.concatenate([keys, dv[...].astype(BF16)], 1)
        out_ref[:, heads * HEAD : (heads + 2) * HEAD] = both


def attend_backward(q, k, v, g, o, lse, cosines, sines):
    heads, length, _ = q.shape
    rows = min(512, length)
    width = -(-(heads + 2) * HEAD // LANES) * LANES
    per_query = pl.BlockSpec((heads, rows, HEAD), lambda i: (0, i, 0))
    whole = pl.BlockSpec((length, HEAD), lambda i: (0, 0))
    return pl.pallas_call(
        attend_backward_kernel,
        grid=(length // rows,),
        in_specs=[
            per_query,
            whole,
            whole,
            per_query,
            per_query,
            pl.BlockSpec((heads, 1, rows), lambda i: (0, 0, i)),
            whole,
            whole,
        ],
        out_specs=pl.BlockSpec((length, width), lambda i: (0, 0)),
        out_shape=jax.ShapeDtypeStruct((length, width), BF16),
        scratch_shapes=[pltpu.VMEM((rows, HEAD), F32), pltpu.VMEM((length, HEAD), F32), pltpu.VMEM((length, HEAD), F32)],
        compiler_params=pltpu.CompilerParams(vmem_limit_bytes=56 << 20),
        cost_estimate=pl.CostEstimate(
            flops=5 * heads * length * length * HEAD,
            transcendentals=heads * length * length // 2,
            bytes_accessed=12 * heads * length * HEAD,
        ),
        name="attend_backward",
    )(q, k, v, g, o, lse, cosines, sines)


def flat(ref):
    return ref[...].reshape(ref.shape[0] * ref.shape[1], ref.shape[2])


def chunks(width, most):
    return [(at, min(most, width - at)) for at in range(0, width, most)]


def resident(shape, column=0):
    return pl.BlockSpec(shape, lambda i: (0, column), pipeline_mode=pl.Buffered(1))


def per_row(rows, width):
    return pl.BlockSpec((rows, width), lambda i: (i, 0))


def forward_in_kernel(x_ref, small_ref, wide_ref, cos_ref, sin_ref, q_ref, k_ref, v_ref, hidden_ref, slope_ref):
    x = flat(x_ref)
    cosines, sines = cos_ref[...], sin_ref[...]
    joined = dot(x, small_ref[...])
    heads = q_ref.shape[0]
    for h in range(heads):
        q = rotate(joined[:, h * HEAD : (h + 1) * HEAD], cosines, sines).astype(BF16)
        q_ref[h] = q * HEAD ** (-0.5)
    at = heads * HEAD
    k_ref[...] = rotate(joined[:, at : at + HEAD], cosines, sines).astype(BF16)
    v_ref[...] = joined[:, at + HEAD : at + 2 * HEAD].astype(BF16)
    for at, width in chunks(wide_ref.shape[1], 384):
        up = dot(x, wide_ref[:, at : at + width])
        bell = 0.5 + 0.5 * lax.erf(up * 0.5**0.5)
        hidden_ref[:, at : at + width] = (up * bell).astype(BF16)
        slope = bell + up * jnp.exp(up * up * -0.5) * (2 * jnp.pi) ** (-0.5)
        slope_ref[:, at : at + width] = slope.astype(BF16)


def forward_in(x, small, wide, cosines, sines, heads):
    chips, tokens, d = x.shape
    length = chips * tokens
    step = max(1, 512 // tokens)
    rows = step * tokens
    width = -(-(heads + 2) * HEAD // LANES) * LANES
    n = wide.shape[1]
    return pl.pallas_call(
        forward_in_kernel,
        grid=(chips // step,),
        in_specs=[
            pl.BlockSpec((step, tokens, d), lambda i: (i, 0, 0)),
            resident((d, width)),
            resident((d, n)),
            per_row(rows, HEAD),
            per_row(rows, HEAD),
        ],
        out_specs=[
            pl.BlockSpec((heads, rows, HEAD), lambda i: (0, i, 0)),
            per_row(rows, HEAD),
            per_row(rows, HEAD),
            per_row(rows, n),
            per_row(rows, n),
        ],
        out_shape=[
            jax.ShapeDtypeStruct((heads, length, HEAD), BF16),
            jax.ShapeDtypeStruct((length, HEAD), BF16),
            jax.ShapeDtypeStruct((length, HEAD), BF16),
            jax.ShapeDtypeStruct((length, n), BF16),
            jax.ShapeDtypeStruct((length, n), BF16),
        ],
        compiler_params=pltpu.CompilerParams(vmem_limit_bytes=56 << 20),
        cost_estimate=pl.CostEstimate(
            flops=2 * length * d * (n + width), transcendentals=2 * length * n, bytes_accessed=2 * length * d
        ),
        name="forward_in",
    )(x, small, wide, cosines, sines)


def back_in_kernel(lead, g_ref, dense_ref, down_ref, slope_ref, heads_ref, grad_ref):
    g = flat(g_ref)
    grad = dot(g, dense_ref[...]).astype(BF16)
    for h in range(heads_ref.shape[0]):
        heads_ref[h] = grad[:, lead + h * HEAD : lead + (h + 1) * HEAD]
    for at, width in chunks(down_ref.shape[1], 384):
        part = dot(g, down_ref[:, at : at + width])
        grad_ref[:, at : at + width] = (part * slope_ref[:, at : at + width].astype(F32)).astype(BF16)


def back_in(g, small, lead, heads, down, slope):
    chips, tokens, d = g.shape
    length = chips * tokens
    step = max(1, 512 // tokens)
    rows = step * tokens
    width = lead + heads * HEAD
    n = down.shape[1]
    return pl.pallas_call(
        functools.partial(back_in_kernel, lead),
        grid=(chips // step,),
        in_specs=[
            pl.BlockSpec((step, tokens, d), lambda i: (i, 0, 0)),
            resident((d, width), small.shape[1] // width - 1),
            resident((d, n)),
            per_row(rows, n),
        ],
        out_specs=[pl.BlockSpec((heads, rows, HEAD), lambda i: (0, i, 0)), per_row(rows, n)],
        out_shape=[jax.ShapeDtypeStruct((heads, length, HEAD), BF16), jax.ShapeDtypeStruct((length, n), BF16)],
        compiler_params=pltpu.CompilerParams(vmem_limit_bytes=56 << 20),
        cost_estimate=pl.CostEstimate(
            flops=2 * length * d * (n + width), transcendentals=0, bytes_accessed=2 * length * d
        ),
        name="back_in",
    )(g, small, down, slope)


def out_kernel(a_ref, b_ref, small_ref, wide_ref, out_ref):
    step, tokens, d = out_ref.shape
    a, b = a_ref[...], b_ref[...]
    for at, width in chunks(d, 512):
        part = dot(a, small_ref[at : at + width], ROWS_COLS) + dot(b, wide_ref[at : at + width], ROWS_COLS)
        out_ref[:, :, at : at + width] = part.astype(BF16).reshape(step, tokens, width)


def out_product(a, b, small, column, wide, chips, name):
    length, width = a.shape
    tokens, d = length // chips, small.shape[0]
    step = max(1, 512 // tokens)
    rows = step * tokens
    n = wide.shape[1]
    return pl.pallas_call(
        out_kernel,
        grid=(chips // step,),
        in_specs=[per_row(rows, width), per_row(rows, n), resident((d, width), column), resident((d, n))],
        out_specs=pl.BlockSpec((step, tokens, d), lambda i: (i, 0, 0)),
        out_shape=jax.ShapeDtypeStruct((chips, tokens, d), BF16),
        compiler_params=pltpu.CompilerParams(vmem_limit_bytes=56 << 20),
        cost_estimate=pl.CostEstimate(
            flops=2 * length * d * (n + width), transcendentals=0, bytes_accessed=2 * length * d
        ),
        name=name,
    )(a, b, small, wide)


def weight_kernel(x_ref, a_ref, b_ref, small_ref, wide_ref):
    chips, tokens, width = x_ref.shape
    x = x_ref[...].reshape(chips * tokens, width)
    small_ref[...] = dot(x, a_ref[...], ROWS_ROWS).astype(BF16)
    for at, n in chunks(wide_ref.shape[1], 384):
        wide_ref[:, at : at + n] = dot(x, b_ref[:, at : at + n], ROWS_ROWS).astype(BF16)


def weight_product(x, a, b, name):
    chips, tokens, d = x.shape
    length = chips * tokens
    width = 768 if d % 768 == 0 else 512
    return pl.pallas_call(
        weight_kernel,
        grid=(d // width,),
        in_specs=[pl.BlockSpec((chips, tokens, width), lambda i: (0, 0, i)), resident(a.shape), resident(b.shape)],
        out_specs=[per_row(width, a.shape[1]), per_row(width, b.shape[1])],
        out_shape=[jax.ShapeDtypeStruct((d, a.shape[1]), BF16), jax.ShapeDtypeStruct((d, b.shape[1]), BF16)],
        compiler_params=pltpu.CompilerParams(vmem_limit_bytes=56 << 20),
        cost_estimate=pl.CostEstimate(
            flops=2 * length * d * (a.shape[1] + b.shape[1]), transcendentals=0, bytes_accessed=2 * length * d
        ),
        name=name,
    )(x, a, b)


def share_heads(columns, chips):
    rows, width = columns.shape
    heads = width // HEAD
    most = -(-heads // chips)
    richer = heads - chips * (most - 1)
    cut = richer * most * HEAD
    first = jnp.moveaxis(columns[:, :cut].reshape(rows, richer, most * HEAD), 1, 0)
    if richer == chips:
        return first
    rest = jnp.moveaxis(columns[:, cut:].reshape(rows, chips - richer, (most - 1) * HEAD), 1, 0)
    return jnp.concatenate([first, jnp.pad(rest, ((0, 0), (0, 0), (0, HEAD)))], 0)


def join_heads(parts, heads):
    chips, rows, width = parts.shape
    most = width // HEAD
    richer = heads - chips * (most - 1)
    first = jnp.moveaxis(parts[:richer], 0, 1).reshape(rows, -1)
    if richer == chips:
        return first
    rest = jnp.moveaxis(parts[richer:, :, : width - HEAD], 0, 1).reshape(rows, -1)
    return jnp.concatenate([first, rest], 1)


def swap(values):
    return lax.ppermute(values, "fsdp", [(0, 1), (1, 0)])


def in_order(mine, other, core, axis):
    return jnp.where(
        core == 0,
        jnp.concatenate([mine, other], axis),
        jnp.concatenate([other, mine], axis),
    )


def half_of(values, core, axis):
    first, second = jnp.split(values, 2, axis)
    return jnp.where(core == 0, first, second), jnp.where(core == 0, second, first)


def angles(length):
    inverse_freq = ROPE_BASE ** (-jnp.arange(0, HEAD, 2).astype(F32) / HEAD)
    phases = jnp.arange(length, dtype=jnp.int32).astype(F32)[:, None] * inverse_freq[None, :]
    phases = jnp.concatenate([phases, phases], -1)
    return jnp.cos(phases), jnp.sin(phases)


def body(layer_input, cotangent, norm_gain, norm_bias, qkv_weight, up_weight, dense_weight, down_weight):
    chips = lax.axis_size("ctx")
    core = lax.axis_index("fsdp")
    inputs = layer_input[0].astype(F32)
    tokens, features = inputs.shape
    length = tokens * chips
    heads = features // HEAD
    most = -(-heads // chips)
    qwide = most * HEAD
    rows = qkv_weight.shape[0]
    high = padded_rows(rows)
    wide_columns = up_weight.shape[1]
    lead = (qwide + 2 * HEAD) % LANES

    def pad(values):
        apart = values.reshape(*values.shape[:-1], chips, rows)
        apart = jnp.pad(apart, [(0, 0)] * (apart.ndim - 1) + [(0, high - rows)])
        return apart.reshape(*values.shape[:-1], chips * high)

    def unpad(values):
        apart = values.reshape(*values.shape[:-1], chips, high)[..., :rows]
        return apart.reshape(*values.shape[:-1], features)

    def pad_rows(weight):
        return jnp.pad(weight, ((0, high - rows), (0, 0)))

    center = inputs - jnp.mean(inputs, -1, keepdims=True)
    inverse = lax.rsqrt(jnp.mean(center * center, -1, keepdims=True) + EPS)
    xhat = center * inverse
    normed_low = pad((xhat * norm_gain + norm_bias).astype(BF16))
    grad_low = pad(cotangent[0])

    mine, other = half_of(pad_rows(jnp.concatenate([qkv_weight, dense_weight], 1)), core, 0)
    other = swap(other)
    qkv_columns = qkv_weight.shape[1]
    qkv_rows = in_order(mine[:, :qkv_columns], other[:, :qkv_columns], core, 1)
    dense_rows = in_order(mine[:, qkv_columns:], other[:, qkv_columns:], core, 1)
    blocks = jnp.concatenate(
        [
            share_heads(qkv_rows[:, :features], chips),
            jnp.broadcast_to(qkv_rows[:, features:], (chips, high // 2, 2 * HEAD)),
            share_heads(dense_rows, chips),
        ],
        2,
    )
    normed_all, grad_all, up_cols, down_cols, small = bring(
        chips,
        0,
        "bring",
        (Gather, normed_low),
        (Gather, grad_low),
        (Columns, pad_rows(up_weight)),
        (Columns, pad_rows(down_weight)),
        (Blocks, blocks),
    )

    cosines, sines = angles(length)
    dense_block = small.shape[1] // (lead + qwide) - 1
    queries, keys, values, hidden_low, slope = forward_in(normed_all, small, up_cols, cosines, sines, most)
    attended_low, attention, log_sum = attend_forward(queries, keys, values, lead)
    branch = out_product(attended_low, hidden_low, small, dense_block, down_cols, chips, "forward_out")
    branch, grad_all = lax.optimization_barrier((branch, grad_all))
    branch = unpad(lax.psum_scatter(branch, "ctx", scatter_dimension=0, tiled=False))
    layer_output = (inputs + branch.astype(F32)).astype(BF16)

    least, _ = tile_share(wide_columns // LANES, chips)
    own_wide, one_wide = (least + 1) * LANES, least * LANES
    dense_part, down_part = weight_product(grad_all, attended_low, hidden_low, "late_weights")
    down_part, grad_all = lax.optimization_barrier((down_part, grad_all))
    other = jnp.concatenate([down_part[:, own_wide:], down_part[:, one_wide:own_wide]], 1)
    down_total = (down_part[:, :own_wide] + swap(other)).reshape(chips, high, own_wide)
    down_total = lax.all_to_all(down_total, "ctx", 0, 0, tiled=True)
    down_grad = untile(down_total, rows, wide_columns)
    grad_heads, grad_up = back_in(grad_all, small, lead, most, down_cols, slope)
    grad_joined = attend_backward(queries, keys, values, grad_heads, attention, log_sum, cosines, sines)
    qkv_part, up_part = weight_product(normed_all, grad_joined, grad_up, "early_weights")
    grad_normed = out_product(grad_joined, grad_up, small, 0, up_cols, chips, "back_out")

    small_part = jnp.concatenate([qkv_part[:, : qwide + 2 * HEAD], dense_part[:, lead:]], 1)
    input_grad, stats, up_grad, total = send(
        chips,
        1,
        features,
        grad_normed,
        up_part,
        wide_columns,
        small_part,
        pad(xhat),
        grad_low,
        pad(norm_gain[None]),
        inverse,
    )
    up_grad = up_grad[:rows].astype(F32)
    qkv_rows = jnp.concatenate(
        [
            join_heads(total[:, :, :qwide], heads),
            jnp.sum(total[:, :, qwide : qwide + 2 * HEAD].astype(F32), 0).astype(BF16),
        ],
        1,
    )
    dense_rows = join_heads(total[:, :, qwide + 2 * HEAD :], heads)

    def own_columns(values):
        mine, other = half_of(values, core, 1)
        return in_order(mine, swap(other), core, 0)[:rows].astype(F32)

    stats = unpad(stats)
    return (
        layer_output[None],
        unpad(input_grad)[None],
        stats[0],
        stats[1],
        own_columns(qkv_rows),
        up_grad,
        own_columns(dense_rows),
        down_grad,
    )


def solution(mesh):
    split = P("ctx", "fsdp")
    stream = P("fsdp", "ctx", None)
    return jax.shard_map(
        body,
        mesh=mesh,
        in_specs=(stream, stream, P(), P(), split, split, split, split),
        out_specs=(stream, stream, P(), P(), split, split, split, split),
        check_vma=False,
    )
```

time: 2220 us -> 1530 us (0.69)
  Pallas kernels: 99.4 us -> 1340 us
  waiting for transfers between devices: 1130 us -> 0.05 us
  matrix products: 310 us -> 0 us
  local copies, waits for them, and re-layouts: 387 us -> 84.2 us
  other arithmetic: 142 us -> 61 us
  starting transfers between devices: 79.6 us -> 16.7 us
  blocking collectives: 39.9 us -> 0 us
    pallas_call x2 -> x11, Pallas kernels: 99.4 us -> 1340 us  [the longest x1 514 us: bring(): pl.pallas_call(functools.partial(bring_kernel, chips, [(kind, len(h)) for...]
    all_to_all x6 -> x1, waiting for transfers between devices: 695 us -> 0.01 us  [body(): down_total = lax.all_to_all(down_total, 'ctx', 0, 0, tiled=True)]
    all_gather x2 -> x0, waiting for transfers between devices: 391 us -> none  [the longest x1 383 us: body(): grad_all = lax.all_gather(grad_low, 'ctx', axis=0, tiled=True)]
    dot_general x12 -> x0, matrix products: 310 us -> none  [the longest x8 189 us: dot(): return lax.dot_general(a, b, dims, preferred_element_type=F32)]
    reshape x19 -> x7, local copies, waits for them, and re-layouts: 149 us -> 6.75 us  [the longest x4 5.73 us: pad(): return apart.reshape(*values.shape[:-1], chips * high)]
    unnamed x70 -> x53, local copies, waits for them, and re-layouts: 89.8 us -> 19.6 us
    all_to_all x6 -> x1, starting transfers between devices: 69.2 us -> 4.87 us  [body(): down_total = lax.all_to_all(down_total, 'ctx', 0, 0, tiled=True)]
    convert_element_type x7 -> x2, local copies, waits for them, and re-layouts: 63.5 us -> 1.76 us  [the longest x1 1.53 us: body(): layer_output = (inputs + branch.astype(F32)).astype(BF16)]
  transfers between devices with their start and end apart: 20 -> 6, of which waited for: 12 -> 0; matrix products, arithmetic and copies ran while one was open for 26% -> 6% of each run, Pallas kernels for 0% -> 16%
where the time goes in v2:
time: 1530 us; the launch traced here: 1520 us
  Pallas kernels  1340 us (88%)
  local copies, waits for them, and re-layouts  84.2 us (6%)
  other arithmetic  61 us (4%)
  starting transfers between devices  16.7 us (1%)
    pallas_call x1, Pallas kernels, bring(): pl.pallas_call(functools.partial(bring_kernel, chips, [(kind, len(h)) for...  514 us
    pallas_call x1, Pallas kernels, send(): pl.pallas_call(functools.partial(send_kernel, chips, features, [len(h) fo...  432 us
    pallas_call x2, Pallas kernels, weight_product(): pl.pallas_call(weight_kernel, grid=(d // width,), in_specs=[pl.BlockSpec(...  90.6 us
    pallas_call x2, Pallas kernels, out_product(): pl.pallas_call(out_kernel, grid=(chips // step,), in_specs=[per_row(rows,...  86 us
    pallas_call x1, Pallas kernels, attend_forward(): pl.pallas_call(functools.partial(attend_forward_kernel, lead), grid=(leng...  58 us
    pallas_call x1, Pallas kernels, attend_backward(): pl.pallas_call(attend_backward_kernel, grid=(length // rows,), in_specs=[...  52.9 us
    pallas_call x1, Pallas kernels, forward_in(): pl.pallas_call(forward_in_kernel, grid=(chips // step,), in_specs=[pl.Blo...  50.5 us
    pallas_call x1, Pallas kernels, back_in(): pl.pallas_call(functools.partial(back_in_kernel, lead), grid=(chips // st...  47.9 us
  transfers between devices with their start and end apart: 6, of which 0 were waited for; matrix products, arithmetic and copies ran while one was open for 6% of the time, Pallas kernels for 16%

profile of v2, /device:TPU:15, one launch (start us, length us, event | category | flops | bytes accessed | tf_op | source)
XLA Modules:
  0.0 1520.2 jit_solution(16162193454963191470)
XLA Ops:
  7.2 2.5 pad_maximum_fusion.2
  9.8 2.2 broadcast_select_fusion.1
  13.5 2.2 slice.125
  15.7 2.0 slice.120
  20.6 3.4 add_convert_fusion
  27.2 1.7 copy.26.refs_1_.refs_4_
  28.9 5.3 pad.36.refs_2_
  34.2 2.7 pad.37.refs_3_
  37.3 4.8 fusion.17
  49.6 1.7 reshape.159
  51.2 2.6 reshape.157
  56.0 2.2 fusion.7.refs_4_
  58.2 2.5 copy-done
  60.7 514.5 %bring.1 = (bf16[16,128,4608]{2,1,0:T(8,128)(2,1)}, bf16[16,128,4608]{2,1,0:T(8,128)(2,1)}, bf16[4608,1152]{1,0:T(8,128)(2,1)S(1)}, bf16[4608,1152]{1,0:T(8,128)(2,1)}, bf16[4608,768]{1,0:T(8,128)(2,1)S(1)}) custom-call(bf16[128,4608]{1,0:T(8,128)(2,1)S(1)} %copy.25.refs_0_, bf16[128,4608]{1,0:T(8,128)(2,1)S(1)} %copy.26.refs_1_.refs_4_, ...), custom_call_target="tpu_custom_call" | custom-call | tf_op jit(solution)/shard_map/bring/pallas_call | solution.py:438
  575.2 3.9 copy-done.4
  579.1 3.0 copy-done.5
  582.0 50.5 %forward_in.1 = (bf16[5,2048,64]{2,1,0:T(8,128)(2,1)}, bf16[2048,64]{1,0:T(8,128)(2,1)}, bf16[2048,64]{1,0:T(8,128)(2,1)}, bf16[2048,1152]{1,0:T(8,128)(2,1)}, bf16[2048,1152]{1,0:T(8,128)(2,1)}) custom-call(bf16[16,128,4608]{2,1,0:T(8,128)(2,1)} %get-tuple-element.35.x_ref, bf16[4608,768]{1,0:T(8,128)(2,1)} %copy-done.5, bf16[4608,1152]{1,0:T(8,128)(2,1)} %copy-done.4, ...), custom_call_target="tpu_custom_call" | custom-call | flops 31406948352 | bytes 18874368 | tf_op jit(solution)/shard_map/forward_in/pallas_call | solution.py:1082
  633.7 1.7 copy-done.7
  636.5 58.0 %attend_forward.1 = (bf16[2048,384]{1,0:T(8,128)(2,1)S(1)}, f32[5,2048,64]{2,1,0:T(8,128)S(1)}, f32[5,1,2048]{2,1,0:T(1,128)S(1)}) custom-call(bf16[5,2048,64]{2,1,0:T(8,128)(2,1)S(1)} %copy-done.7, bf16[2048,64]{1,0:T(8,128)(2,1)S(1)} %copy-done.8, bf16[2048,128]{1,0:T(8,128)(2,1)S(1)} %concatenate.68.v_ref), custom_call_target="tpu_custom_call" | custom-call | flops 2684354560 | bytes 5242880 | tf_op jit(solution)/shard_map/attend_forward/pallas_call | solution.py:932
  694.5 2.3 copy-done.6
  698.6 42.8 %forward_out.1 = bf16[16,128,4608]{2,1,0:T(8,128)(2,1)} custom-call(bf16[2048,384]{1,0:T(8,128)(2,1)} %copy-done.9, bf16[2048,1152]{1,0:T(8,128)(2,1)} %get-tuple-element.42.b_ref, bf16[4608,768]{1,0:T(8,128)(2,1)} %copy-done.5, bf16[4608,1152]{1,0:T(8,128)(2,1)} %get-tuple-element.43.wide_ref.down_ref), custom_call_target="tpu_custom_call" | custom-call | flops 28991029248 | bytes 18874368 | tf_op jit(solution)/shard_map/forward_out/pallas_call | solution.py:1164
  741.4 45.2 %late_weights.1 = (bf16[4608,384]{1,0:T(8,128)(2,1)}, bf16[4608,1152]{1,0:T(8,128)(2,1)}) custom-call(bf16[16,128,4608]{2,1,0:T(8,128)(2,1)} %get-tuple-element.48.x_ref.g_ref, bf16[2048,384]{1,0:T(8,128)(2,1)} %copy-done.9, bf16[2048,1152]{1,0:T(8,128)(2,1)} %get-tuple-element.42.b_ref), custom_call_target="tpu_custom_call" | custom-call | flops 28991029248 | bytes 18874368 | tf_op jit(solution)/shard_map/late_weights/pallas_call | solution.py:1190
  788.1 2.7 slice.118
  790.8 3.1 pad_maximum_fusion.1
  793.9 10.5 collective-permute-start.3
  804.5 3.2 pad.41
  807.8 3.4 copy.28.refs_3_
  811.4 6.0 slice.105
  817.4 47.9 %back_in.1 = (bf16[5,2048,64]{2,1,0:T(8,128)(2,1)}, bf16[2048,1152]{1,0:T(8,128)(2,1)}) custom-call(bf16[16,128,4608]{2,1,0:T(8,128)(2,1)} %get-tuple-element.48.x_ref.g_ref, bf16[4608,768]{1,0:T(8,128)(2,1)} %copy-done.5, bf16[4608,1152]{1,0:T(8,128)(2,1)} %get-tuple-element.43.wide_ref.down_ref, bf16[2048,1152]{1,0:T(8,128)(2,1)} %get-tuple-element.49.slope_ref), custom_call_target="tpu_custom_call" | custom-call | flops 28991029248 | bytes 18874368 | tf_op jit(solution)/shard_map/back_in/pallas_call | solution.py:1131
  865.2 52.9 %attend_backward.1.a_ref = bf16[2048,512]{1,0:T(8,128)(2,1)} custom-call(bf16[5,2048,64]{2,1,0:T(8,128)(2,1)} %get-tuple-element.38.q_ref, bf16[2048,64]{1,0:T(8,128)(2,1)} %get-tuple-element.39.k_ref, bf16[2048,64]{1,0:T(8,128)(2,1)} %get-tuple-element.40.v_ref, bf16[5,2048,64]{2,1,0:T(8,128)(2,1)} %get-tuple-element.50.g_ref, f32[5,2048,64]{2,1,0:T(8,128)} %copy-done.6, ...), custom_call_target="tpu_custom_call" | custom-call | flops 6710886400 | bytes 7864320 | tf_op jit(solution)/shard_map/attend_backward/pallas_call | solution.py:1014
  918.2 7.7 slice_add_fusion
  925.9 4.9 all-to-all-start
  930.7 45.4 %early_weights.1 = (bf16[4608,512]{1,0:T(8,128)(2,1)}, bf16[4608,1152]{1,0:T(8,128)(2,1)}) custom-call(bf16[16,128,4608]{2,1,0:T(8,128)(2,1)} %get-tuple-element.35.x_ref, bf16[2048,512]{1,0:T(8,128)(2,1)} %attend_backward.1.a_ref, bf16[2048,1152]{1,0:T(8,128)(2,1)} %get-tuple-element.53.b_ref), custom_call_target="tpu_custom_call" | custom-call | flops 31406948352 | bytes 18874368 | tf_op jit(solution)/shard_map/early_weights/pallas_call | solution.py:1190
  976.1 8.3 pad_maximum_fusion.refs_2_
  984.4 43.2 %back_out.1.refs_0_ = bf16[16,128,4608]{2,1,0:T(8,128)(2,1)} custom-call(bf16[2048,512]{1,0:T(8,128)(2,1)} %attend_backward.1.a_ref, bf16[2048,1152]{1,0:T(8,128)(2,1)} %get-tuple-element.53.b_ref, bf16[4608,768]{1,0:T(8,128)(2,1)} %copy-done.5, bf16[4608,1152]{1,0:T(8,128)(2,1)} %copy-done.4), custom_call_target="tpu_custom_call" | custom-call | flops 31406948352 | bytes 18874368 | tf_op jit(solution)/shard_map/back_out/pallas_call | solution.py:1164
  1027.7 431.6 %send.1 = (f32[128,4608]{1,0:T(8,128)S(1)}, f32[2,4608]{1,0:T(2,128)S(1)}, bf16[288,9088]{1,0:T(8,128)(2,1)}, bf16[16,144,768]{2,1,0:T(8,128)(2,1)}, bf16[2,4,2,...) custom-call(bf16[16,128,4608]{2,1,0:T(8,128)(2,1)} %back_out.1.refs_, ...), custom_call_target="tpu_custom_call" | custom-call | tf_op jit(solution)/shard_map/send/pallas_call | solution.py:809
  1459.3 2.5 slice_bitcast_fusion.2
  1462.8 1.8 slice_bitcast_fusion
  1467.6 2.7 broadcast_select_fusion.3
  1473.2 7.4 slice_convert_fusion
  1480.6 1.9 copy.31
  1482.5 2.8 broadcast_in_dim_reshape.3
  1486.8 3.0 fusion.16
  1489.9 3.2 fusion.13
  1493.1 11.4 untile.1
  1504.5 2.4 copy.27
  1508.5 1.5 reshape.171
  1510.3 2.9 add_convert_fusion.1
  (106 shorter events, 33.4 us)
Async XLA Ops:
  7.2 1497.4 %reduce-scatter.2.cloned.1.call-start = ((), (), s32[]{:S(2)}) async-start(), calls=%async_computation.2 | async-start | bytes 20054016 | tf_op jit(solution)/shard_map/reduce_scatter | solution.py:1314
  7.2 2.5 copy-start.13
  7.2 2.6 copy-start.14
  9.8 2.9 copy-start.11
  12.0 30.1 %collective-permute-start = (bf16[144,4608]{1,0:T(8,128)(2,1)}, bf16[144,4608]{1,0:T(8,128)(2,1)}, u32[]{:S(2)}, u32[]{:S(2)}) collective-permute-start(bf16[144,4608]{1,0:T(8,128)(2,1)} %get-tuple-element.65), channel_id=1, source_target_pairs={{0,1},{1,0},{2,3},{3,2},{4,5},{5,4},{6,7},{7,6},{8,9},{9,8},{10,11... | collective-permute-start | bytes 3981320 | tf_op jit(solution)/shard_map/ppermute | solution.py:1229
  27.2 7.0 slice-start.3
  28.9 5.4 slice-start.4
  37.0 6.5 copy-start.20
  44.2 1.3 copy-start.15
  44.3 2.4 copy-start.18
  46.7 2.9 slice-start.2
  51.2 7.0 slice-start
  53.9 1.6 copy-start.16
  53.9 1.8 copy-start.17
  55.9 2.3 slice-start.1
  58.2 2.5 copy-start
  575.2 3.9 copy-start.4
  579.1 3.0 copy-start.5
  633.7 1.7 copy-start.7
  635.5 1.0 copy-start.8
  694.5 2.3 copy-start.6
  696.8 1.1 copy-start.9
  698.0 0.6 copy-start.10
  790.8 13.6 copy-start.21
  793.9 124.3 %collective-permute-start.3 = (bf16[4608,640]{1,0:T(8,128)(2,1)}, bf16[4608,640]{1,0:T(8,128)(2,1)}, u32[]{:S(2)}, u32[]{:S(2)}) collective-permute-start(bf16[4608,640]{1,0:T(8,128)(2,1)} %pad_maximum_fusion.1), channel_id=1, source_target_pairs={{0,1},{1,0},{2,3},{3,2},{4,5},{5,4},{6,7},{7,6},{8,9},{9,8},{10,11... | collective-permute-start | bytes 17694728 | tf_op jit(solution)/shard_map/ppermute | solution.py:1229
  925.9 567.2 %all-to-all-start = ((bf16[16,288,640]{2,1,0:T(8,128)(2,1)}), bf16[16,288,640]{2,1,0:T(8,128)(2,1)}, u32[]{:S(2)}, u32[]{:S(2)}) async-start(bf16[16,288,640]{2,1,0:T(8,128)(2,1)} %bitcast.52), calls=%async_computation.1 | async-start | bytes 11796480 | tf_op jit(solution)/shard_map/all_to_all | solution.py:1323
  984.4 43.2 %copy-start.1 = (f32[128,4608]{1,0:T(8,128)S(1)}, f32[128,4608]{1,0:T(8,128)}, u32[]{:S(2)}) copy-start(f32[128,4608]{1,0:T(8,128)} %copy.28.refs_3_) | copy-start | bytes 7077892
  1459.3 5.2 copy-start.2
  1470.2 19.7 %collective-permute-start.1 = (bf16[144,2336]{1,0:T(8,128)(2,1)}, bf16[144,2336]{1,0:T(8,128)(2,1)}, u32[]{:S(2)}, u32[]{:S(2)}) collective-permute-start(bf16[144,2336]{1,0:T(8,128)(2,1)} %get-tuple-element.71), channel_id=1, source_target_pairs={{0,1},{1,0},{2,3},{3,2},{4,5},{5,4},{6,7},{7,6},{8,9},{9,8},{10,11... | collective-permute-start | bytes 2018312 | tf_op jit(solution)/shard_map/ppermute | solution.py:1229
  1473.2 13.7 collective-permute-start.2
  1473.2 7.4 copy-start.3
  1482.5 4.3 copy-start.19
  1508.4 1.8 copy-start.12
Sparse Core Ops, SparseCore 0:
  741.5 456.8 reduce-scatter.1

commit v3 on v2

--- a/solution.py
+++ b/solution.py
@@ -887,75 +887,6 @@
     middle = values.shape[-1] // 2
     turned = jnp.concatenate([values[..., middle:], -values[..., :middle]], -1)
     return values * cosines + turned * sines
-
-
-def attend_forward_kernel(lead, q_ref, k_ref, v_ref, low_ref, o_ref, lse_ref, acc, top):
-    index = pl.program_id(0)
-    heads, rows, _ = q_ref.shape
-    outs = []
-    for h in range(heads):
-        q = q_ref[h]
-        acc[...] = jnp.zeros_like(acc)
-        top[...] = jnp.full_like(top, MASKED)
-
-        def block(start, masked):
-            s = dot(q, k_ref[pl.ds(start, rows), :], ROWS_COLS)
-            if masked:
-                key = lax.broadcasted_iota(jnp.int32, s.shape, 1)
-                query = lax.broadcasted_iota(jnp.int32, s.shape, 0)
-                s = jnp.where(key <= query, s, MASKED)
-            old = top[...]
-            new = jnp.maximum(old, jnp.max(s, 1, keepdims=True))
-            p = jnp.exp(s - new).astype(BF16)
-            acc[...] = acc[...] * jnp.exp(old - new) + dot(p, v_ref[pl.ds(start, rows), :])
-            top[...] = new
-
-        each(0, index, lambda i: block(pl.multiple_of(i * rows, rows), False))
-        block(pl.multiple_of(index * rows, rows), True)
-        total = acc[...]
-        norm = total[:, HEAD : HEAD + 1]
-        out = total[:, :HEAD] / norm
-        o_ref[h] = out
-        outs.append(out.astype(BF16))
-        lse = jnp.broadcast_to(top[...] + jnp.log(norm), (rows, LANES))
-        lse_ref[h] = lse.T[:1]
-    if lead:
-        outs = [jnp.zeros((rows, lead), BF16)] + outs
-    low_ref[...] = jnp.concatenate(outs, 1)
-
-
-def attend_forward(q, k, v, lead):
-    heads, length, _ = q.shape
-    rows = min(512, length)
-    width = lead + heads * HEAD
-    wide = jnp.concatenate([v, jnp.ones_like(v)], 1)
-    return pl.pallas_call(
-        functools.partial(attend_forward_kernel, lead),
-        grid=(length // rows,),
-        in_specs=[
-            pl.BlockSpec((heads, rows, HEAD), lambda i: (0, i, 0)),
-            pl.BlockSpec((length, HEAD), lambda i: (0, 0)),
-            pl.BlockSpec((length, 2 * HEAD), lambda i: (0, 0)),
-        ],
-        out_specs=[
-            pl.BlockSpec((rows, width), lambda i: (i, 0)),
-            pl.BlockSpec((heads, rows, HEAD), lambda i: (0, i, 0)),
-            pl.BlockSpec((heads, 1, rows), lambda i: (0, 0, i)),
-        ],
-        out_shape=[
-            jax.ShapeDtypeStruct((length, width), BF16),
-            jax.ShapeDtypeStruct((heads, length, HEAD), F32),
-            jax.ShapeDtypeStruct((heads, 1, length), F32),
-        ],
-        scratch_shapes=[pltpu.VMEM((rows, 2 * HEAD), F32), pltpu.VMEM((rows, 1), F32)],
-        compiler_params=pltpu.CompilerParams(vmem_limit_bytes=40 << 20),
-        cost_estimate=pl.CostEstimate(
-            flops=2 * heads * length * length * HEAD,
-            transcendentals=heads * length * length // 2,
-            bytes_accessed=8 * heads * length * HEAD,
-        ),
-        name="attend_forward",
-    )(q, k, wide)
 
 
 def attend_backward_kernel(q_ref, k_ref, v_ref, g_ref, o_ref, lse_ref, cos_ref, sin_ref, out_ref, acc, dk, dv):
@@ -1053,62 +984,172 @@
     return pl.BlockSpec((rows, width), lambda i: (i, 0))
 
 
-def forward_in_kernel(x_ref, small_ref, wide_ref, cos_ref, sin_ref, q_ref, k_ref, v_ref, hidden_ref, slope_ref):
-    x = flat(x_ref)
-    cosines, sines = cos_ref[...], sin_ref[...]
-    joined = dot(x, small_ref[...])
-    heads = q_ref.shape[0]
-    for h in range(heads):
-        q = rotate(joined[:, h * HEAD : (h + 1) * HEAD], cosines, sines).astype(BF16)
-        q_ref[h] = q * HEAD ** (-0.5)
-    at = heads * HEAD
-    k_ref[...] = rotate(joined[:, at : at + HEAD], cosines, sines).astype(BF16)
-    v_ref[...] = joined[:, at + HEAD : at + 2 * HEAD].astype(BF16)
-    for at, width in chunks(wide_ref.shape[1], 384):
-        up = dot(x, wide_ref[:, at : at + width])
-        bell = 0.5 + 0.5 * lax.erf(up * 0.5**0.5)
-        hidden_ref[:, at : at + width] = (up * bell).astype(BF16)
-        slope = bell + up * jnp.exp(up * up * -0.5) * (2 * jnp.pi) ** (-0.5)
-        slope_ref[:, at : at + width] = slope.astype(BF16)
-
-
-def forward_in(x, small, wide, cosines, sines, heads):
+def forward_kernel(chips, plan, lead, events, *refs):
+    n = len(plan)
+    x_ref, small_ref, wide_ref, cos_ref, sin_ref = refs[:5]
+    ins, refs = refs[5 : 5 + n], refs[5 + n :]
+    q_out, k_out, v_out, hidden_ref, slope_ref, low_ref, o_ref, lse_ref = refs[:8]
+    outs, refs = refs[8 : 8 + n], refs[8 + n :]
+    q_all, k_all, v_all, acc, top = refs[:5]
+    held = take(refs[5:], [count for _, count in plan])
+    step = pl.program_id(0)
+    half = pl.num_programs(0) // 2
+    heads, rows, _ = q_out.shape
+    place = Place(chips)
+    parts = [kind(place, a, o, h) for (kind, _), a, o, h in zip(plan, ins, outs, held)]
+
+    @pl.when(step == 0)
+    def _():
+        enter(place)
+        for part in parts:
+            part.begin()
+
+    @pl.when(step < half)
+    def _():
+        here = pl.ds(pl.multiple_of(step * rows, rows), rows)
+        x = flat(x_ref)
+        cosines, sines = cos_ref[...], sin_ref[...]
+        joined = dot(x, small_ref[...])
+        for h in range(heads):
+            q = rotate(joined[:, h * HEAD : (h + 1) * HEAD], cosines, sines).astype(BF16) * HEAD ** (-0.5)
+            q_out[h] = q
+            q_all[h, here] = q
+        at = heads * HEAD
+        k = rotate(joined[:, at : at + HEAD], cosines, sines).astype(BF16)
+        v = joined[:, at + HEAD : at + 2 * HEAD].astype(BF16)
+        k_out[...] = k
+        v_out[...] = v
+        k_all[here] = k
+        v_all[here] = jnp.concatenate([v, jnp.ones_like(v)], 1)
+        for at, width in chunks(wide_ref.shape[1], 384):
+            up = dot(x, wide_ref[:, at : at + width])
+            bell = 0.5 + 0.5 * lax.erf(up * 0.5**0.5)
+            hidden_ref[:, at : at + width] = (up * bell).astype(BF16)
+            slope = bell + up * jnp.exp(up * up * -0.5) * (2 * jnp.pi) ** (-0.5)
+            slope_ref[:, at : at + width] = slope.astype(BF16)
+
+    @pl.when(step >= half)
+    def _():
+        index = step - half
+        here = pl.ds(pl.multiple_of(index * rows, rows), rows)
+        lows = []
+        for h in range(heads):
+            q = q_all[h, here]
+            acc[...] = jnp.zeros_like(acc)
+            top[...] = jnp.full_like(top, MASKED)
+
+            def block(start, masked):
+                s = dot(q, k_all[pl.ds(start, rows), :], ROWS_COLS)
+                if masked:
+                    key = lax.broadcasted_iota(jnp.int32, s.shape, 1)
+                    query = lax.broadcasted_iota(jnp.int32, s.shape, 0)
+                    s = jnp.where(key <= query, s, MASKED)
+                old = top[...]
+                new = jnp.maximum(old, jnp.max(s, 1, keepdims=True))
+                p = jnp.exp(s - new).astype(BF16)
+                acc[...] = acc[...] * jnp.exp(old - new) + dot(p, v_all[pl.ds(start, rows), :])
+                top[...] = new
+
+            each(0, index, lambda i: block(pl.multiple_of(i * rows, rows), False))
+            block(pl.multiple_of(index * rows, rows), True)
+            total = acc[...]
+            norm = total[:, HEAD : HEAD + 1]
+            out = total[:, :HEAD] / norm
+            o_ref[h] = out
+            lows.append(out.astype(BF16))
+            lse = jnp.broadcast_to(top[...] + jnp.log(norm), (rows, LANES))
+            lse_ref[h] = lse.T[:1]
+        if lead:
+            lows = [jnp.zeros((rows, lead), BF16)] + lows
+        low_ref[...] = jnp.concatenate(lows, 1)
+
+    todo = []
+    longest = max(len(part.steps()) for part in parts)
+    for at in range(longest):
+        for part in parts:
+            steps = part.steps()
+            index = at - (longest - len(steps))
+            if index >= 0:
+                todo.append(steps[index])
+    cuts = [0, *[c for _, c in events], len(todo)]
+    for (back, _), first, last in zip([*events, (0, None)], cuts[:-1], cuts[1:]):
+
+        @pl.when(step == pl.num_programs(0) - 1 - back)
+        def _():
+            for do in todo[first:last]:
+                do()
+
+    @pl.when(step == pl.num_programs(0) - 1)
+    def _():
+        for part in parts:
+            part.end()
+
+
+def forward(x, small, wide, cosines, sines, heads, lead, number, jobs):
     chips, tokens, d = x.shape
     length = chips * tokens
     step = max(1, 512 // tokens)
     rows = step * tokens
+    half = chips // step
     width = -(-(heads + 2) * HEAD // LANES) * LANES
     n = wide.shape[1]
-    return pl.pallas_call(
-        forward_in_kernel,
-        grid=(chips // step,),
+    low = lead + heads * HEAD
+    held = [kind.scratch(chips, a) for kind, a in jobs]
+    plan = [(kind, len(h)) for (kind, _), h in zip(jobs, held)]
+    early = lambda i: jnp.minimum(i, half - 1)
+    late = lambda i: jnp.maximum(i - half, 0)
+    first = lambda w: pl.BlockSpec((rows, w), lambda i: (early(i), 0))
+    events = ((4, 1), (2, 3), (1, 4))
+    results = pl.pallas_call(
+        functools.partial(forward_kernel, chips, plan, lead, events),
+        grid=(2 * half,),
         in_specs=[
-            pl.BlockSpec((step, tokens, d), lambda i: (i, 0, 0)),
+            pl.BlockSpec((step, tokens, d), lambda i: (early(i), 0, 0)),
             resident((d, width)),
             resident((d, n)),
-            per_row(rows, HEAD),
-            per_row(rows, HEAD),
-        ],
+            first(HEAD),
+            first(HEAD),
+        ]
+        + [ANY] * len(jobs),
         out_specs=[
-            pl.BlockSpec((heads, rows, HEAD), lambda i: (0, i, 0)),
-            per_row(rows, HEAD),
-            per_row(rows, HEAD),
-            per_row(rows, n),
-            per_row(rows, n),
-        ],
+            pl.BlockSpec((heads, rows, HEAD), lambda i: (0, early(i), 0)),
+            first(HEAD),
+            first(HEAD),
+            first(n),
+            first(n),
+            pl.BlockSpec((rows, low), lambda i: (late(i), 0)),
+            pl.BlockSpec((heads, rows, HEAD), lambda i: (0, late(i), 0)),
+            pl.BlockSpec((heads, 1, rows), lambda i: (0, 0, late(i))),
+        ]
+        + [ANY] * len(jobs),
         out_shape=[
             jax.ShapeDtypeStruct((heads, length, HEAD), BF16),
             jax.ShapeDtypeStruct((length, HEAD), BF16),
             jax.ShapeDtypeStruct((length, HEAD), BF16),
             jax.ShapeDtypeStruct((length, n), BF16),
             jax.ShapeDtypeStruct((length, n), BF16),
-        ],
-        compiler_params=pltpu.CompilerParams(vmem_limit_bytes=56 << 20),
+            jax.ShapeDtypeStruct((length, low), BF16),
+            jax.ShapeDtypeStruct((heads, length, HEAD), F32),
+            jax.ShapeDtypeStruct((heads, 1, length), F32),
+        ]
+        + [jax.ShapeDtypeStruct(kind.shape(chips, a), a.dtype) for kind, a in jobs],
+        scratch_shapes=[
+            pltpu.VMEM((heads, length, HEAD), BF16),
+            pltpu.VMEM((length, HEAD), BF16),
+            pltpu.VMEM((length, 2 * HEAD), BF16),
+            pltpu.VMEM((rows, 2 * HEAD), F32),
+            pltpu.VMEM((rows, 1), F32),
+        ]
+        + [s for h in held for s in h],
+        compiler_params=pltpu.CompilerParams(collective_id=number, has_side_effects=True, vmem_limit_bytes=58 << 20),
         cost_estimate=pl.CostEstimate(
-            flops=2 * length * d * (n + width), transcendentals=2 * length * n, bytes_accessed=2 * length * d
+            flops=2 * length * d * (n + width) + 2 * heads * length * length * HEAD,
+            transcendentals=2 * length * n + heads * length * length // 2,
+            bytes_accessed=2 * length * d,
         ),
-        name="forward_in",
-    )(x, small, wide, cosines, sines)
+        name="forward",
+    )(x, small, wide, cosines, sines, *[a for _, a in jobs])
+    return results[:8], results[8:]
 
 
 def back_in_kernel(lead, g_ref, dense_ref, down_ref, slope_ref, heads_ref, grad_ref):
@@ -1294,21 +1335,23 @@
         ],
         2,
     )
-    normed_all, grad_all, up_cols, down_cols, small = bring(
-        chips,
-        0,
-        "bring",
-        (Gather, normed_low),
-        (Gather, grad_low),
-        (Columns, pad_rows(up_weight)),
-        (Columns, pad_rows(down_weight)),
-        (Blocks, blocks),
+    normed_all, up_cols, small = bring(
+        chips, 0, "bring", (Gather, normed_low), (Columns, pad_rows(up_weight)), (Blocks, blocks)
     )
 
     cosines, sines = angles(length)
     dense_block = small.shape[1] // (lead + qwide) - 1
-    queries, keys, values, hidden_low, slope = forward_in(normed_all, small, up_cols, cosines, sines, most)
-    attended_low, attention, log_sum = attend_forward(queries, keys, values, lead)
+    (queries, keys, values, hidden_low, slope, attended_low, attention, log_sum), (grad_all, down_cols) = forward(
+        normed_all,
+        small,
+        up_cols,
+        cosines,
+        sines,
+        most,
+        lead,
+        2,
+        [(Gather, grad_low), (Columns, pad_rows(down_weight))],
+    )
     branch = out_product(attended_low, hidden_low, small, dense_block, down_cols, chips, "forward_out")
     branch, grad_all = lax.optimization_barrier((branch, grad_all))
     branch = unpad(lax.psum_scatter(branch, "ctx", scatter_dimension=0, tiled=False))

time: 1530 us -> 1440 us (0.941)
  Pallas kernels: 1340 us -> 1280 us
    pallas_call x1, Pallas kernels: 514 us -> 299 us  [bring(): pl.pallas_call(functools.partial(bring_kernel, chips, [(kind, len(h)) for...]
    pallas_call x2 -> x1, Pallas kernels: 109 us -> 258 us  [forward(): pl.pallas_call(functools.partial(forward_kernel, chips, plan, lead, event...]
  transfers between devices with their start and end apart: 6 -> 6, of which waited for: 0 -> 0; matrix products, arithmetic and copies ran while one was open for 6% -> 7% of each run, Pallas kernels for 16% -> 17%
where the time goes in v3:
time: 1440 us; the launch traced here: 1430 us
  Pallas kernels  1280 us (89%)
  local copies, waits for them, and re-layouts  71.3 us (5%)
  other arithmetic  60.9 us (4%)
  between operations  14.7 us (1%)
    pallas_call x1, Pallas kernels, send(): pl.pallas_call(functools.partial(send_kernel, chips, features, [len(h) fo...  434 us
    pallas_call x1, Pallas kernels, bring(): pl.pallas_call(functools.partial(bring_kernel, chips, [(kind, len(h)) for...  299 us
    pallas_call x1, Pallas kernels, forward(): pl.pallas_call(functools.partial(forward_kernel, chips, plan, lead, event...  258 us
    pallas_call x2, Pallas kernels, weight_product(): pl.pallas_call(weight_kernel, grid=(d // width,), in_specs=[pl.BlockSpec(...  90.7 us
    pallas_call x2, Pallas kernels, out_product(): pl.pallas_call(out_kernel, grid=(chips // step,), in_specs=[per_row(rows,...  85.8 us
    pallas_call x1, Pallas kernels, attend_backward(): pl.pallas_call(attend_backward_kernel, grid=(length // rows,), in_specs=[...  53 us
    pallas_call x1, Pallas kernels, back_in(): pl.pallas_call(functools.partial(back_in_kernel, lead), grid=(chips // st...  47.8 us
  transfers between devices with their start and end apart: 6, of which 0 were waited for; matrix products, arithmetic and copies ran while one was open for 7% of the time, Pallas kernels for 17%

profile of v3, /device:TPU:15, one launch (start us, length us, event | category | flops | bytes accessed | tf_op | source)
XLA Modules:
  0.0 1434.0 jit_solution(821751256884709713)
XLA Ops:
  7.2 2.5 pad_maximum_fusion.2
  9.8 2.2 broadcast_select_fusion.1
  13.5 2.2 slice.125
  15.7 2.0 slice.120
  18.5 1.4 mul.58
  20.6 3.4 add_convert_fusion
  24.8 5.3 pad.34.refs_1_
  32.5 1.4 copy.26.refs_5_.refs_4_
  34.0 5.2 pad.39.refs_6_
  39.5 4.8 fusion.17
  52.4 2.7 reshape.156
  55.1 1.5 bitcast_bitcast_fusion
  56.9 2.2 fusion.7.refs_2_
  59.1 299.2 %bring.1 = (bf16[16,128,4608]{2,1,0:T(8,128)(2,1)}, bf16[4608,1152]{1,0:T(8,128)(2,1)S(1)}, bf16[4608,768]{1,0:T(8,128)(2,1)S(1)}) custom-call(bf16[128,4608]{1,0:T(8,128)(2,1)S(1)} %copy.25.refs_0_, bf16[288,9088]{1,0:T(8,128)(2,1)S(1)} %bitcast.51, bf16[16,144,768]{2,1,0:T(8,128)(2,1)S(1)} %fusion.7.refs_2_), custom_call_target="tpu_custom_call" | custom-call | tf_op jit(solution)/shard_map/bring/pallas_call | solution.py:438
  358.4 3.9 copy-done.3
  362.3 3.0 copy-done.4
  365.2 257.8 %forward.1 = (bf16[5,2048,64]{2,1,0:T(8,128)(2,1)}, bf16[2048,64]{1,0:T(8,128)(2,1)}, bf16[2048,64]{1,0:T(8,128)(2,1)}, bf16[2048,1152]{1,0:T(8,128)(2,1)}, bf16...) custom-call(bf16[16,128,4608]{2,1,0:T(8,128)(2,1)} %get-tuple-elemen, ...), custom_call_target="tpu_custom_call" | custom-call | flops 34091302912 | bytes 18874368 | tf_op jit(solution)/shard_map/forward/pallas_call | solution.py:1103
  623.1 42.7 %forward_out.1 = bf16[16,128,4608]{2,1,0:T(8,128)(2,1)} custom-call(bf16[2048,384]{1,0:T(8,128)(2,1)} %get-tuple-element.38.a_ref, bf16[2048,1152]{1,0:T(8,128)(2,1)} %get-tuple-element.39.b_ref, bf16[4608,768]{1,0:T(8,128)(2,1)} %copy-done.4, bf16[4608,1152]{1,0:T(8,128)(2,1)} %get-tuple-element.40.wide_ref.down_ref), custom_call_target="tpu_custom_call" | custom-call | flops 28991029248 | bytes 18874368 | tf_op jit(solution)/shard_map/forward_out/pallas_call | solution.py:1205
  665.8 45.3 %late_weights.1 = (bf16[4608,384]{1,0:T(8,128)(2,1)}, bf16[4608,1152]{1,0:T(8,128)(2,1)}) custom-call(bf16[16,128,4608]{2,1,0:T(8,128)(2,1)} %get-tuple-element.48.x_ref.g_ref, bf16[2048,384]{1,0:T(8,128)(2,1)} %get-tuple-element.38.a_ref, bf16[2048,1152]{1,0:T(8,128)(2,1)} %get-tuple-element.39.b_ref), custom_call_target="tpu_custom_call" | custom-call | flops 28991029248 | bytes 18874368 | tf_op jit(solution)/shard_map/late_weights/pallas_call | solution.py:1231
  712.4 2.7 slice.118
  715.1 3.1 pad_maximum_fusion.1
  718.2 1.4 collective-permute-start.3
  719.7 1.6 pad.40
  721.3 2.0 copy.28.refs_3_
  723.6 5.7 slice.105
  729.3 47.8 %back_in.1 = (bf16[5,2048,64]{2,1,0:T(8,128)(2,1)}, bf16[2048,1152]{1,0:T(8,128)(2,1)}) custom-call(bf16[16,128,4608]{2,1,0:T(8,128)(2,1)} %get-tuple-element.48.x_ref.g_ref, bf16[4608,768]{1,0:T(8,128)(2,1)} %copy-done.4, bf16[4608,1152]{1,0:T(8,128)(2,1)} %get-tuple-element.40.wide_ref.down_ref, bf16[2048,1152]{1,0:T(8,128)(2,1)} %get-tuple-element.49.slope_ref), custom_call_target="tpu_custom_call" | custom-call | flops 28991029248 | bytes 18874368 | tf_op jit(solution)/shard_map/back_in/pallas_call | solution.py:1172
  777.1 53.0 %attend_backward.1.a_ref = bf16[2048,512]{1,0:T(8,128)(2,1)} custom-call(bf16[5,2048,64]{2,1,0:T(8,128)(2,1)} %get-tuple-element.43.q_ref, bf16[2048,64]{1,0:T(8,128)(2,1)} %get-tuple-element.44.k_ref, bf16[2048,64]{1,0:T(8,128)(2,1)} %get-tuple-element.45.v_ref, bf16[5,2048,64]{2,1,0:T(8,128)(2,1)} %get-tuple-element.50.g_ref, ...), custom_call_target="tpu_custom_call" | custom-call | flops 6710886400 | bytes 7864320 | tf_op jit(solution)/shard_map/attend_backward/pallas_call | solution.py:945
  830.1 7.6 slice_add_fusion
  837.6 4.9 all-to-all-start
  842.5 45.4 %early_weights.1 = (bf16[4608,512]{1,0:T(8,128)(2,1)}, bf16[4608,1152]{1,0:T(8,128)(2,1)}) custom-call(bf16[16,128,4608]{2,1,0:T(8,128)(2,1)} %get-tuple-element.35.refs_0_.x_ref, bf16[2048,512]{1,0:T(8,128)(2,1)} %attend_backward.1.a_ref, bf16[2048,1152]{1,0:T(8,128)(2,1)} %get-tuple-element.53.b_ref), custom_call_target="tpu_custom_call" | custom-call | flops 31406948352 | bytes 18874368 | tf_op jit(solution)/shard_map/early_weights/pallas_call | solution.py:1231
  887.9 8.3 pad_maximum_fusion.refs_2_
  896.3 43.1 %back_out.1.refs_0_ = bf16[16,128,4608]{2,1,0:T(8,128)(2,1)} custom-call(bf16[2048,512]{1,0:T(8,128)(2,1)} %attend_backward.1.a_ref, bf16[2048,1152]{1,0:T(8,128)(2,1)} %get-tuple-element.53.b_ref, bf16[4608,768]{1,0:T(8,128)(2,1)} %copy-done.4, bf16[4608,1152]{1,0:T(8,128)(2,1)} %copy-done.3), custom_call_target="tpu_custom_call" | custom-call | flops 31406948352 | bytes 18874368 | tf_op jit(solution)/shard_map/back_out/pallas_call | solution.py:1205
  939.4 433.6 %send.1 = (f32[128,4608]{1,0:T(8,128)S(1)}, f32[2,4608]{1,0:T(2,128)S(1)}, bf16[288,9088]{1,0:T(8,128)(2,1)}, bf16[16,144,768]{2,1,0:T(8,128)(2,1)}, bf16[2,4,2,...) custom-call(bf16[16,128,4608]{2,1,0:T(8,128)(2,1)} %back_out.1.refs_, ...), custom_call_target="tpu_custom_call" | custom-call | tf_op jit(solution)/shard_map/send/pallas_call | solution.py:809
  1373.1 2.5 slice_bitcast_fusion.2
  1376.5 1.8 slice_bitcast_fusion
  1379.8 1.5 slice_reduce_fusion
  1381.3 2.7 broadcast_select_fusion.3
  1385.4 1.5 broadcast_select_fusion.5
  1386.9 7.4 slice_convert_fusion
  1394.3 1.9 copy.31
  1396.3 2.8 broadcast_in_dim_reshape.3
  1400.6 3.0 fusion.16
  1403.6 3.2 fusion.13
  1406.8 11.4 untile.1
  1418.3 2.4 copy.27
  1420.7 1.5 slice_convert_fusion.1
  1422.2 1.5 reshape.171
  1424.1 2.9 add_convert_fusion.1
  (86 shorter events, 22.4 us)
Async XLA Ops:
  7.2 1411.1 %reduce-scatter.2.cloned.1.call-start = ((), (), s32[]{:S(2)}) async-start(), calls=%async_computation.2 | async-start | bytes 20054016 | tf_op jit(solution)/shard_map/reduce_scatter | solution.py:1357
  7.2 2.5 copy-start.8
  7.2 2.6 copy-start.9
  9.8 2.9 copy-start.5
  12.0 32.4 %collective-permute-start = (bf16[144,4608]{1,0:T(8,128)(2,1)}, bf16[144,4608]{1,0:T(8,128)(2,1)}, u32[]{:S(2)}, u32[]{:S(2)}) collective-permute-start(bf16[144,4608]{1,0:T(8,128)(2,1)} %get-tuple-element.65), channel_id=1, source_target_pairs={{0,1},{1,0},{2,3},{3,2},{4,5},{5,4},{6,7},{7,6},{8,9},{9,8},{10,11... | collective-permute-start | bytes 3981320 | tf_op jit(solution)/shard_map/ppermute | solution.py:1270
  24.7 5.3 copy-start.14
  39.2 6.5 copy-start.13
  46.5 2.3 copy-start.11
  52.4 6.7 slice-start
  55.1 1.6 copy-start.10
  56.8 2.3 slice-start.1
  358.4 3.9 copy-start.3
  362.3 3.0 copy-start.4
  715.1 4.5 copy-start.15
  715.1 4.6 copy-start.7
  718.2 111.9 %collective-permute-start.3 = (bf16[4608,640]{1,0:T(8,128)(2,1)}, bf16[4608,640]{1,0:T(8,128)(2,1)}, u32[]{:S(2)}, u32[]{:S(2)}) collective-permute-start(bf16[4608,640]{1,0:T(8,128)(2,1)} %pad_maximum_fusion.1), channel_id=1, source_target_pairs={{0,1},{1,0},{2,3},{3,2},{4,5},{5,4},{6,7},{7,6},{8,9},{9,8},{10,11... | collective-permute-start | bytes 17694728 | tf_op jit(solution)/shard_map/ppermute | solution.py:1270
  837.6 569.2 %all-to-all-start = ((bf16[16,288,640]{2,1,0:T(8,128)(2,1)}), bf16[16,288,640]{2,1,0:T(8,128)(2,1)}, u32[]{:S(2)}, u32[]{:S(2)}) async-start(bf16[16,288,640]{2,1,0:T(8,128)(2,1)} %bitcast.52), calls=%async_computation.1 | async-start | bytes 11796480 | tf_op jit(solution)/shard_map/all_to_all | solution.py:1366
  896.3 43.2 %copy-start = (bf16[128,4608]{1,0:T(8,128)(2,1)S(1)}, bf16[128,4608]{1,0:T(8,128)(2,1)}, u32[]{:S(2)}) copy-start(bf16[128,4608]{1,0:T(8,128)(2,1)} %copy.26.refs_5_.refs_4_) | copy-start | bytes 3538948
  1373.1 5.2 copy-start.1
  1384.0 19.7 %collective-permute-start.1 = (bf16[144,2336]{1,0:T(8,128)(2,1)}, bf16[144,2336]{1,0:T(8,128)(2,1)}, u32[]{:S(2)}, u32[]{:S(2)}) collective-permute-start(bf16[144,2336]{1,0:T(8,128)(2,1)} %get-tuple-element.71), channel_id=1, source_target_pairs={{0,1},{1,0},{2,3},{3,2},{4,5},{5,4},{6,7},{7,6},{8,9},{9,8},{10,11... | collective-permute-start | bytes 2018312 | tf_op jit(solution)/shard_map/ppermute | solution.py:1270
  1386.9 13.7 collective-permute-start.2
  1386.9 7.4 copy-start.2
  1396.3 4.3 copy-start.12
  1422.2 1.8 copy-start.6
Sparse Core Ops, SparseCore 0:
  665.9 447.3 reduce-scatter.1

commit v4 on v3

--- a/solution.py
+++ b/solution.py
@@ -824,59 +824,6 @@
     return results[:4]
 
 
-def untile_kernel(parts_ref, out_ref, low, high, load, main_sem, extra_sem):
-    chips = parts_ref.shape[0]
-    rows = out_ref.shape[0]
-    core = lax.axis_index("fsdp")
-    tiles = Tiles(out_ref.shape[1], chips)
-    least = tiles.least
-
-    def bring_in(chip, slot):
-        return pltpu.make_async_copy(parts_ref.at[chip], low.at[slot], load.at[slot])
-
-    def stores(chip, slot):
-        main, extra = tiles.cut(out_ref, chip, core)
-        return (
-            pltpu.make_async_copy(high.at[slot, :, lanes_at(0, least)], main, main_sem.at[slot]),
-            pltpu.make_async_copy(high.at[slot, :, lanes_at(least, 1)], extra, extra_sem.at[slot]),
-        )
-
-    def finish(chip, slot):
-        main, extra = stores(chip, slot)
-        main.wait()
-        pl.when(tiles.more(chip, core))(extra.wait)
-
-    bring_in(0, 0).start()
-
-    def step(chip):
-        slot = lax.rem(chip, 2)
-        pl.when(chip + 1 < chips)(lambda: bring_in(chip + 1, 1 - slot).start())
-        bring_in(chip, slot).wait()
-        pl.when(chip >= 2)(lambda: finish(chip - 2, slot))
-        high[slot] = low[slot, :rows].astype(F32)
-        main, extra = stores(chip, slot)
-        main.start()
-        pl.when(tiles.more(chip, core))(extra.start)
-
-    each(0, chips, step)
-    finish(chips - 2, chips % 2)
-    finish(chips - 1, 1 - chips % 2)
-
-
-def untile(parts, rows, columns):
-    _, high, width = parts.shape
-    return pl.pallas_call(
-        untile_kernel,
-        in_specs=[ANY],
-        out_specs=ANY,
-        out_shape=jax.ShapeDtypeStruct((rows, columns), F32),
-        scratch_shapes=[pltpu.VMEM((2, high, width), BF16), pltpu.VMEM((2, rows, width), F32)] + [DMA((2,))] * 3,
-        compiler_params=pltpu.CompilerParams(vmem_limit_bytes=24 << 20),
-        cost_estimate=pl.CostEstimate(flops=0, transcendentals=0, bytes_accessed=6 * rows * columns),
-        name="untile",
-    )(parts)
-
-
 def rotate(values, cosines, sines):
     middle = values.shape[-1] // 2
     turned = jnp.concatenate([-values[..., middle:], values[..., :middle]], -1)
@@ -887,85 +834,6 @@
     middle = values.shape[-1] // 2
     turned = jnp.concatenate([values[..., middle:], -values[..., :middle]], -1)
     return values * cosines + turned * sines
-
-
-def attend_backward_kernel(q_ref, k_ref, v_ref, g_ref, o_ref, lse_ref, cos_ref, sin_ref, out_ref, acc, dk, dv):
-    index = pl.program_id(0)
-    heads, rows, _ = q_ref.shape
-    scale = HEAD ** (-0.5)
-
-    @pl.when(index == 0)
-    def _():
-        dk[...] = jnp.zeros_like(dk)
-        dv[...] = jnp.zeros_like(dv)
-        out_ref[...] = jnp.zeros_like(out_ref)
-
-    here = pl.ds(pl.multiple_of(index * rows, rows), rows)
-    cosines, sines = cos_ref[here], sin_ref[here]
-    grads = []
-    for h in range(heads):
-        q = q_ref[h]
-        g = g_ref[h]
-        lse = lse_ref[h]
-        delta = jnp.sum((g.astype(F32) * o_ref[h]).T, 0, keepdims=True)
-        acc[...] = jnp.zeros_like(acc)
-
-        def block(start, masked):
-            at = pl.ds(start, rows)
-            k = k_ref[at, :]
-            p = jnp.exp(dot(k, q, ROWS_COLS) - lse)
-            if masked:
-                key = lax.broadcasted_iota(jnp.int32, p.shape, 0)
-                query = lax.broadcasted_iota(jnp.int32, p.shape, 1)
-                p = jnp.where(key <= query, p, 0.0)
-            dp = dot(v_ref[at, :], g, ROWS_COLS)
-            ds = (p * (dp - delta)).astype(BF16)
-            dv[at, :] += dot(p.astype(BF16), g)
-            dk[at, :] += dot(ds, q)
-            acc[...] += dot(ds, k, ROWS_ROWS)
-
-        each(0, index, lambda i: block(pl.multiple_of(i * rows, rows), False))
-        block(pl.multiple_of(index * rows, rows), True)
-        grads.append(rotate_back(acc[...] * scale, cosines, sines).astype(BF16))
-    out_ref[here, : heads * HEAD] = jnp.concatenate(grads, 1)
-
-    @pl.when(index == pl.num_programs(0) - 1)
-    def _():
-        keys = rotate_back(dk[...], cos_ref[...], sin_ref[...]).astype(BF16)
-        both = jnp.concatenate([keys, dv[...].astype(BF16)], 1)
-        out_ref[:, heads * HEAD : (heads + 2) * HEAD] = both
-
-
-def attend_backward(q, k, v, g, o, lse, cosines, sines):
-    heads, length, _ = q.shape
-    rows = min(512, length)
-    width = -(-(heads + 2) * HEAD // LANES) * LANES
-    per_query = pl.BlockSpec((heads, rows, HEAD), lambda i: (0, i, 0))
-    whole = pl.BlockSpec((length, HEAD), lambda i: (0, 0))
-    return pl.pallas_call(
-        attend_backward_kernel,
-        grid=(length // rows,),
-        in_specs=[
-            per_query,
-            whole,
-            whole,
-            per_query,
-            per_query,
-            pl.BlockSpec((heads, 1, rows), lambda i: (0, 0, i)),
-            whole,
-            whole,
-        ],
-        out_specs=pl.BlockSpec((length, width), lambda i: (0, 0)),
-        out_shape=jax.ShapeDtypeStruct((length, width), BF16),
-        scratch_shapes=[pltpu.VMEM((rows, HEAD), F32), pltpu.VMEM((length, HEAD), F32), pltpu.VMEM((length, HEAD), F32)],
-        compiler_params=pltpu.CompilerParams(vmem_limit_bytes=56 << 20),
-        cost_estimate=pl.CostEstimate(
-            flops=5 * heads * length * length * HEAD,
-            transcendentals=heads * length * length // 2,
-            bytes_accessed=12 * heads * length * HEAD,
-        ),
-        name="attend_backward",
-    )(q, k, v, g, o, lse, cosines, sines)
 
 
 def flat(ref):
@@ -1152,62 +1020,185 @@
     return results[:8], results[8:]
 
 
-def back_in_kernel(lead, g_ref, dense_ref, down_ref, slope_ref, heads_ref, grad_ref):
-    g = flat(g_ref)
-    grad = dot(g, dense_ref[...]).astype(BF16)
-    for h in range(heads_ref.shape[0]):
-        heads_ref[h] = grad[:, lead + h * HEAD : lead + (h + 1) * HEAD]
-    for at, width in chunks(down_ref.shape[1], 384):
-        part = dot(g, down_ref[:, at : at + width])
-        grad_ref[:, at : at + width] = (part * slope_ref[:, at : at + width].astype(F32)).astype(BF16)
-
-
-def back_in(g, small, lead, heads, down, slope):
+def backward_kernel(chips, lead, counts, *refs):
+    g_ref, dense_ref, down_ref, slope_ref, q_ref, k_ref, v_ref, o_ref, lse_ref, cos_ref, sin_ref = refs[:11]
+    wide, small = refs[11:13]
+    grad_ref, out_ref, wide_out, small_out = refs[13:17]
+    g_all, acc, dk, dv = refs[17:21]
+    wide_held, small_held = take(refs[21:], counts)
+    heads, rows, _ = q_ref.shape
+    length = g_all.shape[1]
+    count = pl.num_programs(0) - length // rows
+    step = pl.program_id(0)
+    scale = HEAD ** (-0.5)
+    place = Place(chips)
+    parts = return_parts(place, wide, wide_out, wide_held) + trade_parts(place, small, small_out, small_held)
+
+    @pl.when(step == 0)
+    def _():
+        enter(place)
+        for part in parts:
+            part.begin()
+
+    @pl.when(step < count)
+    def _():
+        g = flat(g_ref)
+        low = g.shape[0]
+        here = pl.ds(pl.multiple_of(step * low, low), low)
+        grad = dot(g, dense_ref[...]).astype(BF16)
+        for h in range(heads):
+            g_all[h, here] = grad[:, lead + h * HEAD : lead + (h + 1) * HEAD]
+        for at, width in chunks(down_ref.shape[1], 384):
+            part = dot(g, down_ref[:, at : at + width])
+            grad_ref[:, at : at + width] = (part * slope_ref[:, at : at + width].astype(F32)).astype(BF16)
+
+    @pl.when(step == count)
+    def _():
+        dk[...] = jnp.zeros_like(dk)
+        dv[...] = jnp.zeros_like(dv)
+        out_ref[...] = jnp.zeros_like(out_ref)
+
+    @pl.when(step >= count)
+    def _():
+        index = step - count
+        here = pl.ds(pl.multiple_of(index * rows, rows), rows)
+        cosines, sines = cos_ref[here], sin_ref[here]
+        grads = []
+        for h in range(heads):
+            q = q_ref[h]
+            g = g_all[h, here]
+            lse = lse_ref[h]
+            delta = jnp.sum((g.astype(F32) * o_ref[h]).T, 0, keepdims=True)
+            acc[...] = jnp.zeros_like(acc)
+
+            def block(start, masked):
+                at = pl.ds(start, rows)
+                k = k_ref[at, :]
+                p = jnp.exp(dot(k, q, ROWS_COLS) - lse)
+                if masked:
+                    key = lax.broadcasted_iota(jnp.int32, p.shape, 0)
+                    query = lax.broadcasted_iota(jnp.int32, p.shape, 1)
+                    p = jnp.where(key <= query, p, 0.0)
+                dp = dot(v_ref[at, :], g, ROWS_COLS)
+                ds = (p * (dp - delta)).astype(BF16)
+                dv[at, :] += dot(p.astype(BF16), g)
+                dk[at, :] += dot(ds, q)
+                acc[...] += dot(ds, k, ROWS_ROWS)
+
+            each(0, index, lambda i: block(pl.multiple_of(i * rows, rows), False))
+            block(pl.multiple_of(index * rows, rows), True)
+            grads.append(rotate_back(acc[...] * scale, cosines, sines).astype(BF16))
+        out_ref[here, : heads * HEAD] = jnp.concatenate(grads, 1)
+
+    @pl.when(step == 1)
+    def _():
+        for part in parts:
+            for do in part.steps():
+                do()
+
+    @pl.when(step == pl.num_programs(0) - 1)
+    def _():
+        keys = rotate_back(dk[...], cos_ref[...], sin_ref[...]).astype(BF16)
+        both = jnp.concatenate([keys, dv[...].astype(BF16)], 1)
+        out_ref[:, heads * HEAD : (heads + 2) * HEAD] = both
+        for part in parts:
+            part.end()
+
+
+def backward(g, small, lead, down, slope, q, k, v, o, lse, cosines, sines, number, down_part, dense_part, columns):
     chips, tokens, d = g.shape
-    length = chips * tokens
-    step = max(1, 512 // tokens)
-    rows = step * tokens
+    heads, length, _ = q.shape
+    group = max(1, 256 // tokens)
+    low = group * tokens
+    count = chips // group
+    rows = min(512, length)
     width = lead + heads * HEAD
     n = down.shape[1]
+    out_width = -(-(heads + 2) * HEAD // LANES) * LANES
+    high = d // chips
+    least, _ = tile_share(columns // LANES, chips)
+    held = [
+        Paired.scratch(chips, (high, least * LANES), BF16) + Paired.scratch(chips, (high, LANES), BF16),
+        Paired.scratch(chips, (high // 2, width), BF16),
+    ]
+    early = lambda i: jnp.minimum(i, count - 1)
+    late = lambda i: jnp.maximum(i - count, 0)
+    first = pl.BlockSpec((low, n), lambda i: (early(i), 0))
+    per_query = pl.BlockSpec((heads, rows, HEAD), lambda i: (0, late(i), 0))
+    whole = resident((length, HEAD))
     return pl.pallas_call(
-        functools.partial(back_in_kernel, lead),
-        grid=(chips // step,),
+        functools.partial(backward_kernel, chips, lead, [len(h) for h in held]),
+        grid=(count + length // rows,),
         in_specs=[
-            pl.BlockSpec((step, tokens, d), lambda i: (i, 0, 0)),
+            pl.BlockSpec((group, tokens, d), lambda i: (early(i), 0, 0)),
             resident((d, width), small.shape[1] // width - 1),
             resident((d, n)),
-            per_row(rows, n),
+            first,
+            per_query,
+            whole,
+            whole,
+            per_query,
+            pl.BlockSpec((heads, 1, rows), lambda i: (0, 0, late(i))),
+            whole,
+            whole,
+            ANY,
+            ANY,
         ],
-        out_specs=[pl.BlockSpec((heads, rows, HEAD), lambda i: (0, i, 0)), per_row(rows, n)],
-        out_shape=[jax.ShapeDtypeStruct((heads, length, HEAD), BF16), jax.ShapeDtypeStruct((length, n), BF16)],
-        compiler_params=pltpu.CompilerParams(vmem_limit_bytes=56 << 20),
+        out_specs=[first, resident((length, out_width)), ANY, ANY],
+        out_shape=[
+            jax.ShapeDtypeStruct((length, n), BF16),
+            jax.ShapeDtypeStruct((length, out_width), BF16),
+            jax.ShapeDtypeStruct((high, columns), BF16),
+            jax.ShapeDtypeStruct((chips, high // 2, width), BF16),
+        ],
+        scratch_shapes=[
+            pltpu.VMEM((heads, length, HEAD), BF16),
+            pltpu.VMEM((rows, HEAD), F32),
+            pltpu.VMEM((length, HEAD), F32),
+            pltpu.VMEM((length, HEAD), F32),
+        ]
+        + [s for h in held for s in h],
+        compiler_params=pltpu.CompilerParams(collective_id=number, has_side_effects=True, vmem_limit_bytes=60 << 20),
         cost_estimate=pl.CostEstimate(
-            flops=2 * length * d * (n + width), transcendentals=0, bytes_accessed=2 * length * d
+            flops=2 * length * d * (n + width) + 5 * heads * length * length * HEAD,
+            transcendentals=heads * length * length // 2,
+            bytes_accessed=2 * length * d,
         ),
-        name="back_in",
-    )(g, small, down, slope)
+        name="backward",
+    )(g, small, down, slope, q, k, v, o, lse, cosines, sines, down_part, dense_part)
 
 
 def out_kernel(a_ref, b_ref, small_ref, wide_ref, out_ref):
-    step, tokens, d = out_ref.shape
+    tokens, d = out_ref.shape[-2:]
+    step = a_ref.shape[0] // tokens
     a, b = a_ref[...], b_ref[...]
     for at, width in chunks(d, 512):
         part = dot(a, small_ref[at : at + width], ROWS_COLS) + dot(b, wide_ref[at : at + width], ROWS_COLS)
-        out_ref[:, :, at : at + width] = part.astype(BF16).reshape(step, tokens, width)
-
-
-def out_product(a, b, small, column, wide, chips, name):
+        part = part.astype(BF16).reshape(step, tokens, width)
+        if out_ref.ndim == 4:
+            out_ref[:, 0, :, at : at + width] = part
+        else:
+            out_ref[:, :, at : at + width] = part
+
+
+def out_product(a, b, small, column, wide, chips, name, by_plane=False):
     length, width = a.shape
     tokens, d = length // chips, small.shape[0]
     step = max(1, 512 // tokens)
     rows = step * tokens
     n = wide.shape[1]
+    shape, spec = (chips, tokens, d), pl.BlockSpec((step, tokens, d), lambda i: (i, 0, 0))
+    if by_plane:
+        nz, ny, nx = grid_of(chips)
+        per = ny * nx // step
+        shape = (ny * nx, nz, tokens, d)
+        spec = pl.BlockSpec((step, 1, tokens, d), lambda i: (lax.rem(i, per), i // per, 0, 0))
     return pl.pallas_call(
         out_kernel,
         grid=(chips // step,),
         in_specs=[per_row(rows, width), per_row(rows, n), resident((d, width), column), resident((d, n))],
-        out_specs=pl.BlockSpec((step, tokens, d), lambda i: (i, 0, 0)),
-        out_shape=jax.ShapeDtypeStruct((chips, tokens, d), BF16),
+        out_specs=spec,
+        out_shape=jax.ShapeDtypeStruct(shape, BF16),
         compiler_params=pltpu.CompilerParams(vmem_limit_bytes=56 << 20),
         cost_estimate=pl.CostEstimate(
             flops=2 * length * d * (n + width), transcendentals=0, bytes_accessed=2 * length * d
@@ -1352,25 +1343,40 @@
         2,
         [(Gather, grad_low), (Columns, pad_rows(down_weight))],
     )
-    branch = out_product(attended_low, hidden_low, small, dense_block, down_cols, chips, "forward_out")
+    branch = out_product(attended_low, hidden_low, small, dense_block, down_cols, chips, "forward_out", True)
     branch, grad_all = lax.optimization_barrier((branch, grad_all))
-    branch = unpad(lax.psum_scatter(branch, "ctx", scatter_dimension=0, tiled=False))
-    layer_output = (inputs + branch.astype(F32)).astype(BF16)
-
-    least, _ = tile_share(wide_columns // LANES, chips)
-    own_wide, one_wide = (least + 1) * LANES, least * LANES
+    nz, ny, nx = grid_of(chips)
+    planes = [[z * ny * nx + i for i in range(ny * nx)] for z in range(nz)]
+    lines = [[z * ny * nx + i for z in range(nz)] for i in range(ny * nx)]
+    branch = branch.reshape(ny * nx, nz * tokens, -1)
+    branch = lax.psum_scatter(branch, "ctx", scatter_dimension=0, axis_index_groups=planes, tiled=False)
+
     dense_part, down_part = weight_product(grad_all, attended_low, hidden_low, "late_weights")
-    down_part, grad_all = lax.optimization_barrier((down_part, grad_all))
-    other = jnp.concatenate([down_part[:, own_wide:], down_part[:, one_wide:own_wide]], 1)
-    down_total = (down_part[:, :own_wide] + swap(other)).reshape(chips, high, own_wide)
-    down_total = lax.all_to_all(down_total, "ctx", 0, 0, tiled=True)
-    down_grad = untile(down_total, rows, wide_columns)
-    grad_heads, grad_up = back_in(grad_all, small, lead, most, down_cols, slope)
-    grad_joined = attend_backward(queries, keys, values, grad_heads, attention, log_sum, cosines, sines)
+    grad_up, grad_joined, down_grad, dense_total = backward(
+        grad_all,
+        small,
+        lead,
+        down_cols,
+        slope,
+        queries,
+        keys,
+        values,
+        attention,
+        log_sum,
+        cosines,
+        sines,
+        3,
+        down_part,
+        dense_part,
+        wide_columns,
+    )
+    branch, grad_joined = lax.optimization_barrier((branch, grad_joined))
+    branch = branch.reshape(nz, tokens, -1)
+    branch = lax.psum_scatter(branch, "ctx", scatter_dimension=0, axis_index_groups=lines, tiled=False)
+    layer_output = (inputs + unpad(branch).astype(F32)).astype(BF16)
+    grad_normed = out_product(grad_joined, grad_up, small, 0, up_cols, chips, "back_out")
     qkv_part, up_part = weight_product(normed_all, grad_joined, grad_up, "early_weights")
-    grad_normed = out_product(grad_joined, grad_up, small, 0, up_cols, chips, "back_out")
-
-    small_part = jnp.concatenate([qkv_part[:, : qwide + 2 * HEAD], dense_part[:, lead:]], 1)
+
     input_grad, stats, up_grad, total = send(
         chips,
         1,
@@ -1378,13 +1384,14 @@
         grad_normed,
         up_part,
         wide_columns,
-        small_part,
+        qkv_part,
         pad(xhat),
         grad_low,
         pad(norm_gain[None]),
         inverse,
     )
     up_grad = up_grad[:rows].astype(F32)
+    down_grad = down_grad[:rows].astype(F32)
     qkv_rows = jnp.concatenate(
         [
             join_heads(total[:, :, :qwide], heads),
@@ -1392,7 +1399,7 @@
         ],
         1,
     )
-    dense_rows = join_heads(total[:, :, qwide + 2 * HEAD :], heads)
+    dense_rows = join_heads(dense_total[:, :, lead:], heads)
 
     def own_columns(values):
         mine, other = half_of(values, core, 1)

time: 1440 us -> 1390 us (0.965)
  Pallas kernels: 1280 us -> 1240 us
    pallas_call x1, Pallas kernels: 434 us -> 336 us  [send(): pl.pallas_call(functools.partial(send_kernel, chips, features, [len(h) fo...]
    pallas_call x3 -> x1, Pallas kernels: 112 us -> 179 us  [backward(): pl.pallas_call(functools.partial(backward_kernel, chips, lead, [len(h) fo...]
  transfers between devices with their start and end apart: 6 -> 5, of which waited for: 0 -> 1; matrix products, arithmetic and copies ran while one was open for 7% -> 5% of each run, Pallas kernels for 17% -> 23%
where the time goes in v4:
time: 1390 us; the launch traced here: 1370 us
  Pallas kernels  1240 us (89%)
  local copies, waits for them, and re-layouts  63.4 us (5%)
  other arithmetic  46.8 us (3%)
  between operations  14.6 us (1%)
    pallas_call x1, Pallas kernels, send(): pl.pallas_call(functools.partial(send_kernel, chips, features, [len(h) fo...  336 us
    pallas_call x1, Pallas kernels, bring(): pl.pallas_call(functools.partial(bring_kernel, chips, [(kind, len(h)) for...  299 us
    pallas_call x1, Pallas kernels, forward(): pl.pallas_call(functools.partial(forward_kernel, chips, plan, lead, event...  246 us
    pallas_call x1, Pallas kernels, backward(): pl.pallas_call(functools.partial(backward_kernel, chips, lead, [len(h) fo...  179 us
    pallas_call x2, Pallas kernels, weight_product(): pl.pallas_call(weight_kernel, grid=(d // width,), in_specs=[pl.BlockSpec(...  91.4 us
    pallas_call x2, Pallas kernels, out_product(): pl.pallas_call(out_kernel, grid=(chips // step,), in_specs=[per_row(rows,...  85.9 us
  transfers between devices with their start and end apart: 5, of which 1 were waited for; matrix products, arithmetic and copies ran while one was open for 5% of the time, Pallas kernels for 23%

profile of v4, /device:TPU:15, one launch (start us, length us, event | category | flops | bytes accessed | tf_op | source)
XLA Modules:
  0.0 1372.1 jit_solution(10286240872061848519)
XLA Ops:
  7.2 2.5 pad_maximum_fusion
  9.8 2.2 broadcast_select_fusion.1
  13.5 2.2 slice.109
  15.7 2.0 slice.104
  18.6 1.4 mul.58
  20.6 3.4 add_convert_fusion
  24.8 5.3 pad.34.refs_1_
  30.1 1.1 reshape_squeeze.3
  31.2 1.4 pad.38
  32.5 1.4 copy.41.refs_5_.refs_4_
  34.0 5.2 pad.39.refs_6_
  39.5 4.8 fusion.17
  44.3 1.3 slice.110
  46.5 1.1 slice.112
  47.6 1.2 slice.105
  49.6 1.1 slice.107
  52.4 2.7 reshape.159
  55.1 1.5 bitcast_bitcast_fusion
  56.9 2.2 fusion.7.refs_2_
  59.1 299.2 %bring.1 = (bf16[16,128,4608]{2,1,0:T(8,128)(2,1)}, bf16[4608,1152]{1,0:T(8,128)(2,1)S(1)}, bf16[4608,768]{1,0:T(8,128)(2,1)S(1)}) custom-call(bf16[128,4608]{1,0:T(8,128)(2,1)S(1)} %copy.40.refs_0_, bf16[288,9088]{1,0:T(8,128)(2,1)S(1)} %bitcast.53, bf16[16,144,768]{2,1,0:T(8,128)(2,1)S(1)} %fusion.7.refs_2_), custom_call_target="tpu_custom_call" | custom-call | tf_op jit(solution)/shard_map/bring/pallas_call | solution.py:438
  358.4 3.9 copy-done.2
  362.3 3.0 copy-done.3
  365.2 245.9 %forward.1 = (bf16[5,2048,64]{2,1,0:T(8,128)(2,1)}, bf16[2048,64]{1,0:T(8,128)(2,1)}, bf16[2048,64]{1,0:T(8,128)(2,1)}, bf16[2048,1152]{1,0:T(8,128)(2,1)}, bf16...) custom-call(bf16[16,128,4608]{2,1,0:T(8,128)(2,1)} %get-tuple-elemen, ...), custom_call_target="tpu_custom_call" | custom-call | flops 34091302912 | bytes 18874368 | tf_op jit(solution)/shard_map/forward/pallas_call | solution.py:971
  611.1 42.8 %forward_out.1 = bf16[4,4,128,4608]{3,2,1,0:T(8,128)(2,1)} custom-call(bf16[2048,384]{1,0:T(8,128)(2,1)} %get-tuple-element.40.a_ref, bf16[2048,1152]{1,0:T(8,128)(2,1)} %get-tuple-element.41.b_ref, bf16[4608,768]{1,0:T(8,128)(2,1)} %copy-done.3, bf16[4608,1152]{1,0:T(8,128)(2,1)} %get-tuple-element.42.wide_ref.refs_2_), custom_call_target="tpu_custom_call" | custom-call | flops 28991029248 | bytes 18874368 | tf_op jit(solution)/shard_map/forward_out/pallas_call | solution.py:1196
  655.6 1.6 pad.40
  657.1 3.0 copy.43.refs_3_
  660.4 45.8 %late_weights.1 = (bf16[4608,384]{1,0:T(8,128)(2,1)}, bf16[4608,1152]{1,0:T(8,128)(2,1)}) custom-call(bf16[16,128,4608]{2,1,0:T(8,128)(2,1)} %get-tuple-element.45.x_ref.refs_0_, bf16[2048,384]{1,0:T(8,128)(2,1)} %get-tuple-element.40.a_ref, bf16[2048,1152]{1,0:T(8,128)(2,1)} %get-tuple-element.41.b_ref), custom_call_target="tpu_custom_call" | custom-call | flops 28991029248 | bytes 18874368 | tf_op jit(solution)/shard_map/late_weights/pallas_call | solution.py:1222
  706.2 179.4 %backward.1 = (bf16[2048,1152]{1,0:T(8,128)(2,1)}, bf16[2048,512]{1,0:T(8,128)(2,1)}, bf16[288,9088]{1,0:T(8,128)(2,1)}, bf16[16,144,384]{2,1,0:T(8,128)(2,1)}) custom-call(bf16[16,128,4608]{2,1,0:T(8,128)(2,1)} %get-tuple-element.45.x_ref.refs_0_, bf16[4608,768]{1,0:T(8,128)(2,1)} %copy-done.3, bf16[4608,1152]{1,0:T(8,128)(2,1)} %get-tuple-element.42.wide_ref.refs_2_, ...), custom_call_target="tpu_custom_call" | custom-call | flops 35701915648 | bytes 18874368 | tf_op jit(solution)/shard_map/backward/pallas_call | solution.py:1129
  885.6 1.5 slice_bitcast_fusion.2
  887.2 1.5 slice_bitcast_fusion
  889.9 7.5 slice_convert_fusion
  897.4 1.7 fusion.16
  899.1 8.6 reduce-scatter.7.cloned.1.call-done
  907.7 43.1 %back_out.1.refs_0_ = bf16[16,128,4608]{2,1,0:T(8,128)(2,1)} custom-call(bf16[2048,512]{1,0:T(8,128)(2,1)} %get-tuple-element.56.a_ref, bf16[2048,1152]{1,0:T(8,128)(2,1)} %get-tuple-element.57.b_ref, bf16[4608,768]{1,0:T(8,128)(2,1)} %copy-done.3, bf16[4608,1152]{1,0:T(8,128)(2,1)} %copy-done.2), custom_call_target="tpu_custom_call" | custom-call | flops 31406948352 | bytes 18874368 | tf_op jit(solution)/shard_map/back_out/pallas_call | solution.py:1196
  950.8 45.6 %early_weights.1 = (bf16[4608,512]{1,0:T(8,128)(2,1)}, bf16[4608,1152]{1,0:T(8,128)(2,1)}) custom-call(bf16[16,128,4608]{2,1,0:T(8,128)(2,1)} %get-tuple-element.37.refs_0_.x_ref, bf16[2048,512]{1,0:T(8,128)(2,1)} %get-tuple-element.56.a_ref, bf16[2048,1152]{1,0:T(8,128)(2,1)} %get-tuple-element.57.b_ref), custom_call_target="tpu_custom_call" | custom-call | flops 31406948352 | bytes 18874368 | tf_op jit(solution)/shard_map/early_weights/pallas_call | solution.py:1222
  996.4 335.5 %send.1 = (f32[128,4608]{1,0:T(8,128)S(1)}, f32[2,4608]{1,0:T(2,128)S(1)}, bf16[288,9088]{1,0:T(8,128)(2,1)}, bf16[16,144,512]{2,1,0:T(8,128)(2,1)S(1)}, bf16[2,...) custom-call(bf16[16,128,4608]{2,1,0:T(8,128)(2,1)} %back_out.1.refs_, ...), custom_call_target="tpu_custom_call" | custom-call | tf_op jit(solution)/shard_map/send/pallas_call | solution.py:809
  1332.0 1.0 copy.53
  1333.9 1.3 reshape.170
  1335.2 1.5 slice_reduce_fusion
  1336.7 2.7 broadcast_select_fusion.3
  1339.8 7.2 slice_convert_fusion.1
  1347.1 1.9 copy.46
  1349.0 2.7 broadcast_in_dim_reshape.3
  1353.3 3.1 fusion.13
  1356.4 2.4 copy.42
  1358.8 1.5 slice_convert_fusion.2
  1360.3 1.5 reshape.175
  1362.1 2.9 add_convert_fusion.1
  (76 shorter events, 14.2 us)
Async XLA Ops:
  7.2 900.5 %reduce-scatter.7.cloned.1.call-start = ((), (), s32[]{:S(2)}) async-start(), calls=%async_computation.3 | async-start | bytes 23592960
  7.2 2.5 copy-start.7
  7.2 2.6 copy-start.8
  9.8 2.9 copy-start.4
  12.0 32.3 %collective-permute-start = (bf16[144,4608]{1,0:T(8,128)(2,1)}, bf16[144,4608]{1,0:T(8,128)(2,1)}, u32[]{:S(2)}, u32[]{:S(2)}) collective-permute-start(bf16[144,4608]{1,0:T(8,128)(2,1)} %get-tuple-element.69), channel_id=1, source_target_pairs={{0,1},{1,0},{2,3},{3,2},{4,5},{5,4},{6,7},{7,6},{8,9},{9,8},{10,11... | collective-permute-start | bytes 3981320 | tf_op jit(solution)/shard_map/ppermute | solution.py:1261
  24.8 5.3 copy-start.12
  39.5 6.2 copy-start.11
  46.4 2.3 copy-start.10
  52.4 6.7 slice-start
  55.1 1.6 copy-start.9
  56.8 2.3 slice-start.1
  358.4 3.9 copy-start.2
  362.3 3.0 copy-start.3
  653.9 0.7 copy-start.13
  653.9 1.7 copy-start.6
  653.9 702.5 %reduce-scatter.5.cloned.1.call-start = ((), (), s32[]{:S(2)}) async-start(), calls=%async_computation.2 | async-start | bytes 5898240 | tf_op jit(solution)/shard_map/reduce_scatter | solution.py:1375
  889.8 7.6 collective-permute-start.2
  950.8 45.6 %copy-start = (bf16[128,4608]{1,0:T(8,128)(2,1)S(1)}, bf16[128,4608]{1,0:T(8,128)(2,1)}, u32[]{:S(2)}) copy-start(bf16[128,4608]{1,0:T(8,128)(2,1)} %copy.41.refs_5_.refs_4_) | copy-start | bytes 3538948
  1332.0 1.6 copy-start.1
  1339.4 13.9 %collective-permute-start.1 = (bf16[144,2336]{1,0:T(8,128)(2,1)}, bf16[144,2336]{1,0:T(8,128)(2,1)}, u32[]{:S(2)}, u32[]{:S(2)}) collective-permute-start(bf16[144,2336]{1,0:T(8,128)(2,1)} %get-tuple-element.71), channel_id=1, source_target_pairs={{0,1},{1,0},{2,3},{3,2},{4,5},{5,4},{6,7},{7,6},{8,9},{9,8},{10,11... | collective-permute-start | bytes 2018312 | tf_op jit(solution)/shard_map/ppermute | solution.py:1261
  1360.3 1.8 copy-start.5
Sparse Core Ops, SparseCore 0:
  654.0 253.6 reduce-scatter.6
  910.1 85.6 reduce-scatter.4

commit v5 on v4

--- a/solution.py
+++ b/solution.py
@@ -136,27 +136,45 @@
     @staticmethod
     def scratch(chips, a):
         nz, ny, nx = grid_of(chips)
-        return [DMA((nz,))] * 2 + [DMA((nz, nx))] * 2 + [DMA((nz, ny))] * 2 + [DMA((nz, nx, ny))] * 4 + [DMA]
+        return [DMA((nz,))] * 2 + [DMA((nz, nx))] * 2 + [DMA((nz, ny))] * 2 + [DMA((nz, nx, ny))] * 4 + [DMA, DMA((nz,))]
 
     def __init__(self, place, mine, out, sems):
         self.p, self.mine, self.out = place, mine, out
-        (self.sl, self.rl, self.sx, self.rx, self.sy, self.ry, self.s1, self.r1, self.s2, self.r2, self.own) = sems
+        (self.sl, self.rl, self.sx, self.rx, self.sy, self.ry, self.s1, self.r1, self.s2, self.r2, self.own, self.sr) = sems
         self.half = mine.shape[0] // 2
 
     def line(self, k):
         p = self.p
         return remote(self.mine, self.out.at[p.me], self.sl.at[k], self.rl.at[k], p.at(k, 0, 0), p.core)
 
+    def direct(self, k):
+        p = self.p
+        to = lax.rem(p.z + k, p.nz)
+        middle = p.nz // 2
+        far = ((to == p.nz - 1) & (p.z < middle)) | ((to == 0) & (p.z >= middle))
+        return jnp.logical_not(far)
+
+    def relay(self, k):
+        p = self.p
+        source = lax.rem(p.z - k + p.nz, p.nz)
+        middle = p.nz // 2
+        up = (p.z == p.nz - 2) & (source < middle)
+        down = (p.z == 1) & (source >= middle)
+        b = p.at(-k, 0, 0)
+        index = jnp.where(up, k + 1, k - 1)
+        copy = remote(self.out.at[b], self.out.at[b], self.sr.at[k], self.rl.at[index], p.at(jnp.where(up, 1, -1), 0, 0), p.core)
+        return copy, up | down
+
     def across(self, k, i):
         p = self.p
         b = p.at(-k, 0, 0)
-        src = self.mine if k == 0 else self.out.at[b]
+        src = self.mine if isinstance(k, int) and k == 0 else self.out.at[b]
         return remote(src, self.out.at[b], self.sx.at[k, i], self.rx.at[k, i], p.at(0, 0, i), p.core)
 
     def along(self, k, j):
         p = self.p
         b = p.at(-k, 0, 0)
-        src = self.mine if k == 0 else self.out.at[b]
+        src = self.mine if isinstance(k, int) and k == 0 else self.out.at[b]
         return remote(src, self.out.at[b], self.sy.at[k, j], self.ry.at[k, j], p.at(0, j, 0), p.core)
 
     def corner1(self, k, i, j):
@@ -177,7 +195,7 @@
 
     def begin(self):
         for k in range(1, self.p.nz):
-            self.line(k).start()
+            pl.when(self.direct(k))(self.line(k).start)
         self.spread(0)
         pltpu.make_async_copy(self.mine, self.out.at[self.p.me], self.own).start()
 
@@ -193,11 +211,16 @@
                 self.corner2(k, i, j).start()
 
     def steps(self):
-        nz = self.p.nz
-        order = [1, nz - 1] + list(range(2, nz - 1))
+        p = self.p
+        assert p.nz == 4
+        first = jnp.where(p.z == 0, 3, 1)
+        last = jnp.where(p.z == 0, 1, jnp.where(p.z == 3, 3, 2))
+        order = [first, 6 - first - last, last]
 
         def come(k):
             self.line(k).wait_recv()
+            copy, needed = self.relay(k)
+            pl.when(needed)(copy.start)
             self.spread(k)
 
         return (
@@ -211,7 +234,9 @@
         pltpu.make_async_copy(self.mine, self.out.at[p.me], self.own).wait()
         for k in range(p.nz):
             if k:
-                self.line(k).wait_send()
+                pl.when(self.direct(k))(self.line(k).wait_send)
+                copy, needed = self.relay(k)
+                pl.when(needed)(copy.wait_send)
             for i in range(1, p.nx):
                 self.across(k, i).wait_send()
             for j in range(1, p.ny):
@@ -777,50 +802,109 @@
 
 
 def send_kernel(chips, features, counts, *refs):
-    blocks, wide, small, xhat, grad, gain, inverse = refs[:7]
-    input_grad, stats, wide_out, small_out = refs[7:11]
-    stages = refs[11:16]
-    norm_held, wide_held, small_held = take(refs[16:], counts)
+    x_ref, a_ref, b_ref, blocks, xhat, grad, gain, inverse = refs[:8]
+    input_grad, stats, wide_out, small_out, wide, small = refs[8:14]
+    stages = refs[14:19]
+    wide_tile, small_tile, stored = refs[19:22]
+    norm_held, wide_held, small_held = take(refs[22:], counts)
+    step = pl.program_id(0)
+    count = pl.num_programs(0) - 1
+    width = x_ref.shape[2]
     place = Place(chips)
-    enter(place)
     norm = NormBack(place, blocks, stages, norm_held, (xhat, grad, gain, inverse), (input_grad, stats), features)
     parts = return_parts(place, wide, wide_out, wide_held)
     parts += trade_parts(place, small, small_out, small_held)
-    for part in [norm] + parts:
-        part.begin()
-    for part in parts + [norm]:
-        for step in part.steps():
-            step()
-    for part in [norm] + parts:
-        part.end()
-
-
-def send(chips, number, features, blocks, wide, columns, small, xhat, grad, gain, inverse):
+
+    def stores(at):
+        slot = lax.rem(at, 2)
+        rows = rows_at(at * width, width)
+        return (
+            pltpu.make_async_copy(wide_tile.at[slot], wide.at[rows], stored.at[0, slot]),
+            pltpu.make_async_copy(small_tile.at[slot], small.at[rows], stored.at[1, slot]),
+        )
+
+    def done(at):
+        for copy in stores(at):
+            copy.wait()
+
+    @pl.when(step == 0)
+    def _():
+        enter(place)
+        norm.begin()
+
+    @pl.when(step < count)
+    def _():
+        slot = lax.rem(step, 2)
+        pl.when(step >= 2)(lambda: done(step - 2))
+        x = flat(x_ref)
+        small_tile[slot] = dot(x, a_ref[...], ROWS_ROWS).astype(BF16)
+        for at, n in chunks(b_ref.shape[1], 384):
+            wide_tile[slot, :, at : at + n] = dot(x, b_ref[:, at : at + n], ROWS_ROWS).astype(BF16)
+        for copy in stores(step):
+            copy.start()
+
+    @pl.when(step == count)
+    def _():
+        done(step - 2)
+        done(step - 1)
+        for part in parts:
+            part.begin()
+        ahead, *rest = norm.steps()
+        ahead()
+        for part in parts:
+            for do in part.steps():
+                do()
+        for do in rest:
+            do()
+        for part in [norm] + parts:
+            part.end()
+
+
+def send(chips, number, features, blocks, x, a, b, columns, xhat, grad, gain, inverse):
     _, tokens, d = blocks.shape
+    length = chips * tokens
     rows = d // chips
     least, _ = tile_share(columns // LANES, chips)
-    width = small.shape[1]
+    low, wide = a.shape[1], b.shape[1]
+    width = 768 if d % 768 == 0 else 512
+    count = d // width
     held = [
         NormBack.scratch(chips, blocks),
         Paired.scratch(chips, (rows, least * LANES), BF16) + Paired.scratch(chips, (rows, LANES), BF16),
-        Paired.scratch(chips, (rows // 2, width), BF16),
+        Paired.scratch(chips, (rows // 2, low), BF16),
     ]
-    low = lambda *shape: jax.ShapeDtypeStruct(shape, BF16)
+    half = lambda *shape: jax.ShapeDtypeStruct(shape, BF16)
     results = pl.pallas_call(
         functools.partial(send_kernel, chips, features, [len(h) for h in held]),
-        in_specs=[ANY] * 3 + [WHOLE] * 4,
-        out_specs=[WHOLE] * 2 + [ANY] * 7,
+        grid=(count + 1,),
+        in_specs=[
+            pl.BlockSpec((chips, tokens, width), lambda i: (0, 0, jnp.minimum(i, count - 1))),
+            resident(a.shape),
+            resident(b.shape),
+            ANY,
+            resident(xhat.shape),
+            resident(grad.shape),
+            resident(gain.shape),
+            resident(inverse.shape),
+        ],
+        out_specs=[resident((tokens, d)), resident((2, d))] + [ANY] * 9,
         out_shape=[
             jax.ShapeDtypeStruct((tokens, d), F32),
             jax.ShapeDtypeStruct((2, d), F32),
-            low(rows, columns),
-            low(chips, rows // 2, width),
+            half(rows, columns),
+            half(chips, rows // 2, low),
+            half(d, wide),
+            half(d, low),
         ]
-        + [low(*s) for s in Scatter.stages(chips, blocks)],
-        scratch_shapes=[s for h in held for s in h],
-        compiler_params=pltpu.CompilerParams(collective_id=number, has_side_effects=True, vmem_limit_bytes=48 << 20),
+        + [half(*s) for s in Scatter.stages(chips, blocks)],
+        scratch_shapes=[pltpu.VMEM((2, width, wide), BF16), pltpu.VMEM((2, width, low), BF16), DMA((2, 2))]
+        + [s for h in held for s in h],
+        compiler_params=pltpu.CompilerParams(collective_id=number, has_side_effects=True, vmem_limit_bytes=60 << 20),
+        cost_estimate=pl.CostEstimate(
+            flops=2 * length * d * (low + wide), transcendentals=0, bytes_accessed=2 * length * d
+        ),
         name="send",
-    )(blocks, wide, small, xhat, grad, gain, inverse)
+    )(x, a, b, blocks, xhat, grad, gain, inverse)
     return results[:4]
 
 
@@ -1375,16 +1459,16 @@
     branch = lax.psum_scatter(branch, "ctx", scatter_dimension=0, axis_index_groups=lines, tiled=False)
     layer_output = (inputs + unpad(branch).astype(F32)).astype(BF16)
     grad_normed = out_product(grad_joined, grad_up, small, 0, up_cols, chips, "back_out")
-    qkv_part, up_part = weight_product(normed_all, grad_joined, grad_up, "early_weights")
 
     input_grad, stats, up_grad, total = send(
         chips,
         1,
         features,
         grad_normed,
-        up_part,
+        normed_all,
+        grad_joined,
+        grad_up,
         wide_columns,
-        qkv_part,
         pad(xhat),
         grad_low,
         pad(norm_gain[None]),

time: 1390 us -> 1360 us (0.978)
  Pallas kernels: 1240 us -> 1210 us
    pallas_call x1, Pallas kernels: 299 us -> 252 us  [bring(): pl.pallas_call(functools.partial(bring_kernel, chips, [(kind, len(h)) for...]
    pallas_call x2 -> x1, Pallas kernels: 91.4 us -> 46 us  [weight_product(): pl.pallas_call(weight_kernel, grid=(d // width,), in_specs=[pl.BlockSpec(...]
    pallas_call x1, Pallas kernels: 246 us -> 286 us  [forward(): pl.pallas_call(functools.partial(forward_kernel, chips, plan, lead, event...]
    pallas_call x1, Pallas kernels: 336 us -> 360 us  [send(): pl.pallas_call(functools.partial(send_kernel, chips, features, [len(h) fo...]
  transfers between devices with their start and end apart: 5 -> 5, of which waited for: 1 -> 1; matrix products, arithmetic and copies ran while one was open for 5% -> 5% of each run, Pallas kernels for 23% -> 20%
where the time goes in v5:
time: 1360 us; the launch traced here: 1350 us
  Pallas kernels  1210 us (89%)
  local copies, waits for them, and re-layouts  63.5 us (5%)
  other arithmetic  45.3 us (3%)
  waiting for transfers between devices  15.6 us (1%)
  between operations  14.6 us (1%)
    pallas_call x1, Pallas kernels, send(): pl.pallas_call(functools.partial(send_kernel, chips, features, [len(h) fo...  360 us
    pallas_call x1, Pallas kernels, forward(): pl.pallas_call(functools.partial(forward_kernel, chips, plan, lead, event...  286 us
    pallas_call x1, Pallas kernels, bring(): pl.pallas_call(functools.partial(bring_kernel, chips, [(kind, len(h)) for...  252 us
    pallas_call x1, Pallas kernels, backward(): pl.pallas_call(functools.partial(backward_kernel, chips, lead, [len(h) fo...  181 us
    pallas_call x2, Pallas kernels, out_product(): pl.pallas_call(out_kernel, grid=(chips // step,), in_specs=[per_row(rows,...  85.9 us
    pallas_call x1, Pallas kernels, weight_product(): pl.pallas_call(weight_kernel, grid=(d // width,), in_specs=[pl.BlockSpec(...  46 us
  transfers between devices with their start and end apart: 5, of which 1 were waited for; matrix products, arithmetic and copies ran while one was open for 5% of the time, Pallas kernels for 20%

profile of v5, /device:TPU:15, one launch (start us, length us, event | category | flops | bytes accessed | tf_op | source)
XLA Modules:
  0.0 1351.0 jit_solution(1478438360485979073)
XLA Ops:
  7.2 2.5 pad_maximum_fusion
  9.8 2.2 broadcast_select_fusion.1
  13.5 2.2 slice.109
  15.7 2.0 slice.104
  18.6 1.4 mul.58
  20.6 3.4 add_convert_fusion
  24.8 5.3 pad.34.refs_1_
  30.1 1.1 reshape_squeeze.3
  31.2 1.4 pad.38
  32.6 1.4 copy.41.refs_5_
  34.0 5.2 pad.39.refs_6_
  39.5 4.8 fusion.17
  44.3 1.3 slice.110
  46.5 1.1 slice.112
  47.7 1.2 slice.105
  49.6 1.1 slice.107
  50.7 0.9 slice.106
  52.4 2.7 reshape.159
  55.1 1.5 bitcast_bitcast_fusion
  56.9 2.2 fusion.7.refs_2_
  59.1 251.9 %bring.1 = (bf16[16,128,4608]{2,1,0:T(8,128)(2,1)}, bf16[4608,1152]{1,0:T(8,128)(2,1)S(1)}, bf16[4608,768]{1,0:T(8,128)(2,1)S(1)}) custom-call(bf16[128,4608]{1,0:T(8,128)(2,1)S(1)} %copy.40.refs_0_, bf16[288,9088]{1,0:T(8,128)(2,1)S(1)} %bitcast.53, bf16[16,144,768]{2,1,0:T(8,128)(2,1)S(1)} %fusion.7.refs_2_), custom_call_target="tpu_custom_call" | custom-call | tf_op jit(solution)/shard_map/bring/pallas_call | solution.py:463
  311.1 3.9 copy-done
  314.9 3.0 copy-done.1
  317.9 285.8 %forward.1 = (bf16[5,2048,64]{2,1,0:T(8,128)(2,1)}, bf16[2048,64]{1,0:T(8,128)(2,1)}, bf16[2048,64]{1,0:T(8,128)(2,1)}, bf16[2048,1152]{1,0:T(8,128)(2,1)}, bf16...) custom-call(bf16[16,128,4608]{2,1,0:T(8,128)(2,1)} %get-tuple-elemen, ...), custom_call_target="tpu_custom_call" | custom-call | flops 34091302912 | bytes 18874368 | tf_op jit(solution)/shard_map/forward/pallas_call | solution.py:1055
  603.7 42.8 %forward_out.1 = bf16[4,4,128,4608]{3,2,1,0:T(8,128)(2,1)} custom-call(bf16[2048,384]{1,0:T(8,128)(2,1)} %get-tuple-element.38.a_ref, bf16[2048,1152]{1,0:T(8,128)(2,1)} %get-tuple-element.39.b_ref, bf16[4608,768]{1,0:T(8,128)(2,1)} %copy-done.1, bf16[4608,1152]{1,0:T(8,128)(2,1)} %get-tuple-element.40.wide_ref.refs_2_), custom_call_target="tpu_custom_call" | custom-call | flops 28991029248 | bytes 18874368 | tf_op jit(solution)/shard_map/forward_out/pallas_call | solution.py:1280
  648.2 1.6 pad.40
  649.7 3.0 copy.43.refs_4_
  654.2 46.0 %late_weights.1 = (bf16[4608,384]{1,0:T(8,128)(2,1)}, bf16[4608,1152]{1,0:T(8,128)(2,1)}) custom-call(bf16[16,128,4608]{2,1,0:T(8,128)(2,1)} %get-tuple-element.43.x_ref.refs_0_, bf16[2048,384]{1,0:T(8,128)(2,1)} %get-tuple-element.38.a_ref, bf16[2048,1152]{1,0:T(8,128)(2,1)} %get-tuple-element.39.b_ref), custom_call_target="tpu_custom_call" | custom-call | flops 28991029248 | bytes 18874368 | tf_op jit(solution)/shard_map/late_weights/pallas_call | solution.py:1306
  700.2 181.5 %backward.1 = (bf16[2048,1152]{1,0:T(8,128)(2,1)}, bf16[2048,512]{1,0:T(8,128)(2,1)}, bf16[288,9088]{1,0:T(8,128)(2,1)}, bf16[16,144,384]{2,1,0:T(8,128)(2,1)}) custom-call(bf16[16,128,4608]{2,1,0:T(8,128)(2,1)} %get-tuple-element.43.x_ref.refs_0_, bf16[4608,768]{1,0:T(8,128)(2,1)} %copy-done.1, bf16[4608,1152]{1,0:T(8,128)(2,1)} %get-tuple-element.40.wide_ref.refs_2_, ...), custom_call_target="tpu_custom_call" | custom-call | flops 35701915648 | bytes 18874368 | tf_op jit(solution)/shard_map/backward/pallas_call | solution.py:1213
  881.7 1.6 slice_bitcast_fusion.2
  883.4 1.5 slice_bitcast_fusion
  886.1 7.3 slice_convert_fusion
  893.4 1.7 fusion.16
  895.1 15.5 %reduce-scatter.7.cloned.1.call-done = bf16[1,512,4608]{2,1,0:T(8,128)(2,1)} async-done(((bf16[4,512,4608]{2,1,0:T(8,128)(2,1)}), bf16[1,512,4608]{2,1,0:T(8,128)(2,1)}) %reduce-scatter.7.cloned.1.call-update) | async-done | bytes 4718608
  910.7 43.1 %back_out.1.refs_3_ = bf16[16,128,4608]{2,1,0:T(8,128)(2,1)} custom-call(bf16[2048,512]{1,0:T(8,128)(2,1)} %get-tuple-element.54.a_ref.refs_1_, bf16[2048,1152]{1,0:T(8,128)(2,1)} %get-tuple-element.55.b_ref.refs_2_, bf16[4608,768]{1,0:T(8,128)(2,1)} %copy-done.1, bf16[4608,1152]{1,0:T(8,128)(2,1)} %copy-done), custom_call_target="tpu_custom_call" | custom-call | flops 31406948352 | bytes 18874368 | tf_op jit(solution)/shard_map/back_out/pallas_call | solution.py:1280
  953.8 359.5 %send.1 = (f32[128,4608]{1,0:T(8,128)}, f32[2,4608]{1,0:T(2,128)}, bf16[288,9088]{1,0:T(8,128)(2,1)}, bf16[16,144,512]{2,1,0:T(8,128)(2,1)}, bf16[4608,1152]{1,0...) custom-call(bf16[16,128,4608]{2,1,0:T(8,128)(2,1)} %get-tuple-elemen, ...), custom_call_target="tpu_custom_call" | custom-call | flops 31406948352 | bytes 18874368 | tf_op jit(solution)/shard_map/send/pallas_call | solution.py:877
  1313.3 1.1 slice_bitcast_fusion.3
  1314.5 1.2 slice_bitcast_fusion.1
  1316.4 1.5 slice_reduce_fusion
  1317.9 1.4 broadcast_select_fusion.3
  1320.0 7.2 slice_convert_fusion.1
  1327.2 2.0 copy.46
  1329.2 1.5 broadcast_in_dim_reshape.3
  1332.3 3.1 fusion.13
  1335.4 2.4 copy.42
  1337.8 1.5 slice_convert_fusion.2
  1339.3 1.5 reshape.175
  1341.1 2.9 add_convert_fusion.1
  (73 shorter events, 14.5 us)
Async XLA Ops:
  7.2 903.5 %reduce-scatter.7.cloned.1.call-start = ((), (), s32[]{:S(2)}) async-start(), calls=%async_computation.3 | async-start | bytes 23592960
  7.2 2.5 copy-start.5
  7.2 2.6 copy-start.6
  9.8 2.9 copy-start.2
  12.0 32.4 %collective-permute-start = (bf16[144,4608]{1,0:T(8,128)(2,1)}, bf16[144,4608]{1,0:T(8,128)(2,1)}, u32[]{:S(2)}, u32[]{:S(2)}) collective-permute-start(bf16[144,4608]{1,0:T(8,128)(2,1)} %get-tuple-element.65), channel_id=1, source_target_pairs={{0,1},{1,0},{2,3},{3,2},{4,5},{5,4},{6,7},{7,6},{8,9},{9,8},{10,11... | collective-permute-start | bytes 3981320 | tf_op jit(solution)/shard_map/ppermute | solution.py:1345
  24.8 5.3 copy-start.10
  39.5 6.2 copy-start.9
  46.5 2.4 copy-start.8
  52.4 6.7 slice-start
  55.1 1.6 copy-start.7
  56.8 2.3 slice-start.1
  311.1 3.9 copy-start
  314.9 3.0 copy-start.1
  646.5 0.7 copy-start.11
  646.5 1.7 copy-start.4
  646.5 688.9 %reduce-scatter.5.cloned.1.call-start = ((), (), s32[]{:S(2)}) async-start(), calls=%async_computation.2 | async-start | bytes 5898240 | tf_op jit(solution)/shard_map/reduce_scatter | solution.py:1459
  886.0 7.4 collective-permute-start.2
  1319.3 13.0 collective-permute-start.1
  1329.2 1.5 copy-start.12
  1339.3 1.8 copy-start.3
Sparse Core Ops, SparseCore 0:
  646.6 263.9 reduce-scatter.6
  913.1 84.1 reduce-scatter.4

commit v6 on v5

--- a/solution.py
+++ b/solution.py
@@ -596,10 +596,28 @@
             self.p.core,
         )
 
-    def send3(self, dz):
-        return remote(
-            self.sum2.at[dz], self.got3.at[dz], self.s3.at[dz], self.r3.at[dz], self.p.at(dz, 0, 0), self.p.core
-        )
+    def beside(self):
+        return jnp.where(lax.rem(self.p.z, 2) == 0, 1, self.p.nz - 1)
+
+    def beyond(self, side):
+        other = jnp.where(self.p.z < 2, 2, 0) + side
+        return lax.rem(other - self.p.z + self.p.nz, self.p.nz)
+
+    def inner(self):
+        return (self.p.z == 1) | (self.p.z == 2)
+
+    def near(self):
+        p, dz = self.p, self.beside()
+        return remote(self.sum2.at[dz], self.got3.at[0], self.s3.at[0], self.r3.at[0], p.at(dz, 0, 0), p.core)
+
+    def lift(self, side):
+        p, dz = self.p, self.beyond(side)
+        to = p.at(self.beside(), 0, 0)
+        return remote(self.sum2.at[dz], self.got3.at[2 + side], self.s3.at[1 + side], self.r3.at[2 + side], to, p.core)
+
+    def far(self, side):
+        p, dz = self.p, self.beyond(side)
+        return remote(self.sum2.at[dz], self.got3.at[1], self.s3.at[1 + side], self.r3.at[1], p.at(dz, 0, 0), p.core)
 
     def fetch(self, refs):
         loads = [pltpu.make_async_copy(r, self.parts.at[i], self.load.at[i]) for i, r in enumerate(refs)]
@@ -644,22 +662,35 @@
             parts = [self.sum1.at[half, dz, 0]] + [self.got2.at[half, dz, v] for v in range(1, self.n)]
             self.add(parts, self.sum2.at[dz, self.rows(half)])
         if dz:
-            self.send3(dz).start()
+            pl.when(self.beside() == dz)(self.near().start)
+            for side in (0, 1):
+                pl.when((self.beyond(side) == dz) & jnp.logical_not(self.inner()))(self.lift(side).start)
+
+    def relay(self):
+        @pl.when(self.inner())
+        def _():
+            for side in (0, 1):
+                self.lift(side).wait_recv()
+                for half in (0, 1):
+                    mine = self.sum2.at[self.beyond(side), self.rows(half)]
+                    self.add([mine, self.got3.at[2 + side, self.rows(half)]], mine)
+                self.far(side).start()
 
     def last(self):
-        for dz in range(1, self.p.nz):
-            self.send3(dz).wait_recv()
+        self.near().wait_recv()
+        self.far(0).wait_recv()
         for half in (0, 1):
             rows = self.rows(half)
-            self.fetch([self.sum2.at[0, rows]] + [self.got3.at[dz, rows] for dz in range(1, self.p.nz)])
+            self.fetch([self.sum2.at[0, rows], self.got3.at[0, rows], self.got3.at[1, rows]])
             self.finish(half)
 
     def steps(self):
+        assert self.p.nz == 4
         order = self.order()
         steps = [functools.partial(self.first, order[0])]
         for old, new in zip(order[:-1], order[1:]):
             steps += [functools.partial(self.first, new), functools.partial(self.second, old)]
-        return steps + [functools.partial(self.second, order[-1]), self.last]
+        return steps + [self.relay, functools.partial(self.second, order[-1]), self.last]
 
     def end(self):
         for dz in range(self.p.nz):
@@ -669,8 +700,11 @@
                         self.send1(half, dz, v, i).wait_send()
                     if v:
                         self.send2(half, dz, v).wait_send()
-            if dz:
-                self.send3(dz).wait_send()
+        self.near().wait_send()
+        inner = self.inner()
+        for side in (0, 1):
+            pl.when(inner)(self.far(side).wait_send)
+            pl.when(jnp.logical_not(inner))(self.lift(side).wait_send)
 
 
 class NormBack(Scatter):
@@ -697,7 +731,7 @@
         def some(c):
             at = pl.multiple_of(c * 16, 16)
             total = self.parts[0, pl.ds(at, 16)].astype(F32)
-            for i in range(1, self.p.nz):
+            for i in (1, 2):
                 total = total + self.parts[i, pl.ds(at, 16)].astype(F32)
             rows = pl.ds(pl.multiple_of(half * self.h + c * 16, 16), 16)
             xhat = self.xhat[rows]
@@ -1051,7 +1085,7 @@
     early = lambda i: jnp.minimum(i, half - 1)
     late = lambda i: jnp.maximum(i - half, 0)
     first = lambda w: pl.BlockSpec((rows, w), lambda i: (early(i), 0))
-    events = ((4, 1), (2, 3), (1, 4))
+    events = ((6, 2), (5, 3), (4, 4), (3, 5), (2, 6), (1, 7)) if half == 4 else ((4, 1), (2, 3), (1, 4))
     results = pl.pallas_call(
         functools.partial(forward_kernel, chips, plan, lead, events),
         grid=(2 * half,),

time: 1360 us -> 1330 us (0.978); the launches traced: 1350 us -> 1300 us
  Pallas kernels: 1210 us -> 1170 us
    pallas_call x1, Pallas kernels: 360 us -> 326 us  [send(): pl.pallas_call(functools.partial(send_kernel, chips, features, [len(h) fo...]
    pallas_call x1, Pallas kernels: 286 us -> 266 us  [forward(): pl.pallas_call(functools.partial(forward_kernel, chips, plan, lead, event...]
    pallas_call x1, Pallas kernels: 181 us -> 196 us  [backward(): pl.pallas_call(functools.partial(backward_kernel, chips, lead, [len(h) fo...]
  transfers between devices with their start and end apart: 5 -> 5, of which waited for: 1 -> 1; matrix products, arithmetic and copies ran while one was open for 5% -> 6% of each run, Pallas kernels for 20% -> 22%
where the time goes in v6:
time: 1330 us; the launch traced here: 1300 us
  Pallas kernels  1170 us (88%)
  local copies, waits for them, and re-layouts  63.4 us (5%)
  other arithmetic  45.3 us (3%)
  between operations  14.7 us (1%)
    pallas_call x1, Pallas kernels, send(): pl.pallas_call(functools.partial(send_kernel, chips, features, [len(h) fo...  326 us
    pallas_call x1, Pallas kernels, forward(): pl.pallas_call(functools.partial(forward_kernel, chips, plan, lead, event...  266 us
    pallas_call x1, Pallas kernels, bring(): pl.pallas_call(functools.partial(bring_kernel, chips, [(kind, len(h)) for...  252 us
    pallas_call x1, Pallas kernels, backward(): pl.pallas_call(functools.partial(backward_kernel, chips, lead, [len(h) fo...  196 us
    pallas_call x2, Pallas kernels, out_product(): pl.pallas_call(out_kernel, grid=(chips // step,), in_specs=[per_row(rows,...  85.9 us
    pallas_call x1, Pallas kernels, weight_product(): pl.pallas_call(weight_kernel, grid=(d // width,), in_specs=[pl.BlockSpec(...  45.2 us
  transfers between devices with their start and end apart: 5, of which 1 were waited for; matrix products, arithmetic and copies ran while one was open for 6% of the time, Pallas kernels for 22%

profile of v6, /device:TPU:15, one launch (start us, length us, event | category | flops | bytes accessed | tf_op | source)
XLA Modules:
  0.0 1303.6 jit_solution(4321120941859219799)
XLA Ops:
  7.2 2.5 pad_maximum_fusion
  9.8 2.2 broadcast_select_fusion.1
  13.5 2.2 slice.109
  15.7 2.0 slice.104
  18.6 1.4 mul.58
  20.6 3.4 add_convert_fusion
  24.8 5.3 pad.34.refs_1_
  30.1 1.1 reshape_squeeze.3
  31.2 1.4 pad.38
  32.6 1.4 copy.41.refs_5_
  34.0 5.2 pad.39.refs_6_
  39.5 4.8 fusion.17
  44.3 1.3 slice.110
  46.5 1.1 slice.112
  47.7 1.2 slice.105
  49.6 1.1 slice.107
  52.4 2.7 reshape.159
  55.1 1.5 bitcast_bitcast_fusion
  56.9 2.2 fusion.7.refs_2_
  59.1 251.9 %bring.1 = (bf16[16,128,4608]{2,1,0:T(8,128)(2,1)}, bf16[4608,1152]{1,0:T(8,128)(2,1)S(1)}, bf16[4608,768]{1,0:T(8,128)(2,1)S(1)}) custom-call(bf16[128,4608]{1,0:T(8,128)(2,1)S(1)} %copy.40.refs_0_, bf16[288,9088]{1,0:T(8,128)(2,1)S(1)} %bitcast.53, bf16[16,144,768]{2,1,0:T(8,128)(2,1)S(1)} %fusion.7.refs_2_), custom_call_target="tpu_custom_call" | custom-call | tf_op jit(solution)/shard_map/bring/pallas_call | solution.py:463
  311.1 3.9 copy-done
  314.9 3.0 copy-done.1
  317.9 266.4 %forward.1 = (bf16[5,2048,64]{2,1,0:T(8,128)(2,1)}, bf16[2048,64]{1,0:T(8,128)(2,1)}, bf16[2048,64]{1,0:T(8,128)(2,1)}, bf16[2048,1152]{1,0:T(8,128)(2,1)}, bf16...) custom-call(bf16[16,128,4608]{2,1,0:T(8,128)(2,1)} %get-tuple-elemen, ...), custom_call_target="tpu_custom_call" | custom-call | flops 34091302912 | bytes 18874368 | tf_op jit(solution)/shard_map/forward/pallas_call | solution.py:1089
  584.3 42.8 %forward_out.1 = bf16[4,4,128,4608]{3,2,1,0:T(8,128)(2,1)} custom-call(bf16[2048,384]{1,0:T(8,128)(2,1)} %get-tuple-element.38.a_ref, bf16[2048,1152]{1,0:T(8,128)(2,1)} %get-tuple-element.39.b_ref, bf16[4608,768]{1,0:T(8,128)(2,1)} %copy-done.1, bf16[4608,1152]{1,0:T(8,128)(2,1)} %get-tuple-element.40.wide_ref.refs_2_), custom_call_target="tpu_custom_call" | custom-call | flops 28991029248 | bytes 18874368 | tf_op jit(solution)/shard_map/forward_out/pallas_call | solution.py:1314
  628.8 1.6 pad.40
  630.3 3.0 copy.43.refs_4_
  634.8 45.2 %late_weights.1 = (bf16[4608,384]{1,0:T(8,128)(2,1)}, bf16[4608,1152]{1,0:T(8,128)(2,1)}) custom-call(bf16[16,128,4608]{2,1,0:T(8,128)(2,1)} %get-tuple-element.43.x_ref.refs_0_, bf16[2048,384]{1,0:T(8,128)(2,1)} %get-tuple-element.38.a_ref, bf16[2048,1152]{1,0:T(8,128)(2,1)} %get-tuple-element.39.b_ref), custom_call_target="tpu_custom_call" | custom-call | flops 28991029248 | bytes 18874368 | tf_op jit(solution)/shard_map/late_weights/pallas_call | solution.py:1340
  680.0 195.9 %backward.1 = (bf16[2048,1152]{1,0:T(8,128)(2,1)}, bf16[2048,512]{1,0:T(8,128)(2,1)}, bf16[288,9088]{1,0:T(8,128)(2,1)}, bf16[16,144,384]{2,1,0:T(8,128)(2,1)}) custom-call(bf16[16,128,4608]{2,1,0:T(8,128)(2,1)} %get-tuple-element.43.x_ref.refs_0_, bf16[4608,768]{1,0:T(8,128)(2,1)} %copy-done.1, bf16[4608,1152]{1,0:T(8,128)(2,1)} %get-tuple-element.40.wide_ref.refs_2_, ...), custom_call_target="tpu_custom_call" | custom-call | flops 35701915648 | bytes 18874368 | tf_op jit(solution)/shard_map/backward/pallas_call | solution.py:1247
  875.9 1.5 slice_bitcast_fusion.2
  877.5 1.5 slice_bitcast_fusion
  880.2 7.3 slice_convert_fusion
  887.5 1.7 fusion.16
  889.2 6.9 reduce-scatter.7.cloned.1.call-done
  896.1 43.1 %back_out.1.refs_3_ = bf16[16,128,4608]{2,1,0:T(8,128)(2,1)} custom-call(bf16[2048,512]{1,0:T(8,128)(2,1)} %get-tuple-element.54.a_ref.refs_1_, bf16[2048,1152]{1,0:T(8,128)(2,1)} %get-tuple-element.55.b_ref.refs_2_, bf16[4608,768]{1,0:T(8,128)(2,1)} %copy-done.1, bf16[4608,1152]{1,0:T(8,128)(2,1)} %copy-done), custom_call_target="tpu_custom_call" | custom-call | flops 31406948352 | bytes 18874368 | tf_op jit(solution)/shard_map/back_out/pallas_call | solution.py:1314
  939.3 326.4 %send.1 = (f32[128,4608]{1,0:T(8,128)}, f32[2,4608]{1,0:T(2,128)}, bf16[288,9088]{1,0:T(8,128)(2,1)}, bf16[16,144,512]{2,1,0:T(8,128)(2,1)}, bf16[4608,1152]{1,0...) custom-call(bf16[16,128,4608]{2,1,0:T(8,128)(2,1)} %get-tuple-elemen, ...), custom_call_target="tpu_custom_call" | custom-call | flops 31406948352 | bytes 18874368 | tf_op jit(solution)/shard_map/send/pallas_call | solution.py:911
  1265.6 1.1 slice_bitcast_fusion.3
  1266.8 1.2 slice_bitcast_fusion.1
  1268.7 1.5 slice_reduce_fusion
  1270.2 1.4 broadcast_select_fusion.3
  1271.6 0.9 collective-permute-start.1
  1272.5 7.2 slice_convert_fusion.1
  1279.8 2.0 copy.46
  1281.8 1.5 broadcast_in_dim_reshape.3
  1284.8 3.1 fusion.13
  1287.9 2.4 copy.42
  1290.3 1.5 slice_convert_fusion.2
  1291.8 1.5 reshape.175
  1293.7 2.9 add_convert_fusion.1
  (73 shorter events, 14.7 us)
Async XLA Ops:
  7.2 888.9 %reduce-scatter.7.cloned.1.call-start = ((), (), s32[]{:S(2)}) async-start(), calls=%async_computation.3 | async-start | bytes 23592960
  7.2 2.5 copy-start.5
  7.2 2.6 copy-start.6
  9.8 2.9 copy-start.2
  12.0 32.4 %collective-permute-start = (bf16[144,4608]{1,0:T(8,128)(2,1)}, bf16[144,4608]{1,0:T(8,128)(2,1)}, u32[]{:S(2)}, u32[]{:S(2)}) collective-permute-start(bf16[144,4608]{1,0:T(8,128)(2,1)} %get-tuple-element.65), channel_id=1, source_target_pairs={{0,1},{1,0},{2,3},{3,2},{4,5},{5,4},{6,7},{7,6},{8,9},{9,8},{10,11... | collective-permute-start | bytes 3981320 | tf_op jit(solution)/shard_map/ppermute | solution.py:1379
  24.8 5.3 copy-start.10
  39.5 6.2 copy-start.9
  46.5 2.4 copy-start.8
  52.4 6.7 slice-start
  55.1 1.6 copy-start.7
  56.8 2.3 slice-start.1
  311.1 3.9 copy-start
  314.9 3.0 copy-start.1
  627.1 0.7 copy-start.11
  627.1 1.7 copy-start.4
  627.1 660.8 %reduce-scatter.5.cloned.1.call-start = ((), (), s32[]{:S(2)}) async-start(), calls=%async_computation.2 | async-start | bytes 5898240 | tf_op jit(solution)/shard_map/reduce_scatter | solution.py:1493
  880.2 7.4 collective-permute-start.2
  1271.6 13.2 %collective-permute-start.1 = (bf16[144,2336]{1,0:T(8,128)(2,1)}, bf16[144,2336]{1,0:T(8,128)(2,1)}, u32[]{:S(2)}, u32[]{:S(2)}) collective-permute-start(bf16[144,2336]{1,0:T(8,128)(2,1)} %get-tuple-element.67), channel_id=1, source_target_pairs={{0,1},{1,0},{2,3},{3,2},{4,5},{5,4},{6,7},{7,6},{8,9},{9,8},{10,11... | collective-permute-start | bytes 2018312 | tf_op jit(solution)/shard_map/ppermute | solution.py:1379
  1281.8 1.5 copy-start.12
  1291.8 1.8 copy-start.3
Sparse Core Ops, SparseCore 0:
  627.2 268.8 reduce-scatter.6
  898.5 85.9 reduce-scatter.4

commit v7 on v6

--- a/solution.py
+++ b/solution.py
@@ -872,7 +872,7 @@
         pl.when(step >= 2)(lambda: done(step - 2))
         x = flat(x_ref)
         small_tile[slot] = dot(x, a_ref[...], ROWS_ROWS).astype(BF16)
-        for at, n in chunks(b_ref.shape[1], 384):
+        for at, n in chunks(b_ref.shape[1], 1152):
             wide_tile[slot, :, at : at + n] = dot(x, b_ref[:, at : at + n], ROWS_ROWS).astype(BF16)
         for copy in stores(step):
             copy.start()
@@ -1329,7 +1329,7 @@
     chips, tokens, width = x_ref.shape
     x = x_ref[...].reshape(chips * tokens, width)
     small_ref[...] = dot(x, a_ref[...], ROWS_ROWS).astype(BF16)
-    for at, n in chunks(wide_ref.shape[1], 384):
+    for at, n in chunks(wide_ref.shape[1], 1152):
         wide_ref[:, at : at + n] = dot(x, b_ref[:, at : at + n], ROWS_ROWS).astype(BF16)
 
 

time: 1330 us -> 1330 us (level)
  transfers between devices with their start and end apart: 5 -> 5, of which waited for: 1 -> 1; matrix products, arithmetic and copies ran while one was open for 6% -> 6% of each run, Pallas kernels for 22% -> 21%
where the time goes in v7:
time: 1330 us; the launch traced here: 1300 us
  Pallas kernels  1170 us (88%)
  local copies, waits for them, and re-layouts  63.3 us (5%)
  other arithmetic  45.5 us (3%)
  between operations  14.7 us (1%)
    pallas_call x1, Pallas kernels, send(): pl.pallas_call(functools.partial(send_kernel, chips, features, [len(h) fo...  328 us
    pallas_call x1, Pallas kernels, forward(): pl.pallas_call(functools.partial(forward_kernel, chips, plan, lead, event...  266 us
    pallas_call x1, Pallas kernels, bring(): pl.pallas_call(functools.partial(bring_kernel, chips, [(kind, len(h)) for...  252 us
    pallas_call x1, Pallas kernels, backward(): pl.pallas_call(functools.partial(backward_kernel, chips, lead, [len(h) fo...  196 us
    pallas_call x2, Pallas kernels, out_product(): pl.pallas_call(out_kernel, grid=(chips // step,), in_specs=[per_row(rows,...  85.9 us
    pallas_call x1, Pallas kernels, weight_product(): pl.pallas_call(weight_kernel, grid=(d // width,), in_specs=[pl.BlockSpec(...  40.4 us
  transfers between devices with their start and end apart: 5, of which 1 were waited for; matrix products, arithmetic and copies ran while one was open for 6% of the time, Pallas kernels for 21%

profile of v7, /device:TPU:15, one launch (start us, length us, event | category | flops | bytes accessed | tf_op | source)
XLA Modules:
  0.0 1302.8 jit_solution(16191813162298213854)
XLA Ops:
  7.2 2.5 pad_maximum_fusion
  9.8 2.2 broadcast_select_fusion.1
  13.5 2.2 slice.109
  15.7 2.0 slice.104
  18.6 1.4 mul.58
  20.6 3.4 add_convert_fusion
  24.8 5.3 pad.34.refs_1_
  30.1 1.1 reshape_squeeze.3
  31.2 1.4 pad.38
  32.6 1.4 copy.41.refs_5_
  34.0 5.2 pad.39.refs_6_
  39.5 4.8 fusion.17
  44.3 1.3 slice.110
  46.5 1.1 slice.112
  47.7 1.2 slice.105
  49.6 1.1 slice.107
  50.7 0.9 slice.106
  52.4 2.7 reshape.159
  55.1 1.5 bitcast_bitcast_fusion
  56.9 2.2 fusion.7.refs_2_
  59.1 251.9 %bring.1 = (bf16[16,128,4608]{2,1,0:T(8,128)(2,1)}, bf16[4608,1152]{1,0:T(8,128)(2,1)S(1)}, bf16[4608,768]{1,0:T(8,128)(2,1)S(1)}) custom-call(bf16[128,4608]{1,0:T(8,128)(2,1)S(1)} %copy.40.refs_0_, bf16[288,9088]{1,0:T(8,128)(2,1)S(1)} %bitcast.53, bf16[16,144,768]{2,1,0:T(8,128)(2,1)S(1)} %fusion.7.refs_2_), custom_call_target="tpu_custom_call" | custom-call | tf_op jit(solution)/shard_map/bring/pallas_call | solution.py:463
  311.1 3.9 copy-done
  314.9 3.0 copy-done.1
  317.9 266.4 %forward.1 = (bf16[5,2048,64]{2,1,0:T(8,128)(2,1)}, bf16[2048,64]{1,0:T(8,128)(2,1)}, bf16[2048,64]{1,0:T(8,128)(2,1)}, bf16[2048,1152]{1,0:T(8,128)(2,1)}, bf16...) custom-call(bf16[16,128,4608]{2,1,0:T(8,128)(2,1)} %get-tuple-elemen, ...), custom_call_target="tpu_custom_call" | custom-call | flops 34091302912 | bytes 18874368 | tf_op jit(solution)/shard_map/forward/pallas_call | solution.py:1089
  584.3 42.8 %forward_out.1 = bf16[4,4,128,4608]{3,2,1,0:T(8,128)(2,1)} custom-call(bf16[2048,384]{1,0:T(8,128)(2,1)} %get-tuple-element.38.a_ref, bf16[2048,1152]{1,0:T(8,128)(2,1)} %get-tuple-element.39.b_ref, bf16[4608,768]{1,0:T(8,128)(2,1)} %copy-done.1, bf16[4608,1152]{1,0:T(8,128)(2,1)} %get-tuple-element.40.wide_ref.refs_2_), custom_call_target="tpu_custom_call" | custom-call | flops 28991029248 | bytes 18874368 | tf_op jit(solution)/shard_map/forward_out/pallas_call | solution.py:1314
  628.8 1.6 pad.40
  630.3 3.0 copy.43.refs_4_
  634.8 40.4 %late_weights.1 = (bf16[4608,384]{1,0:T(8,128)(2,1)}, bf16[4608,1152]{1,0:T(8,128)(2,1)}) custom-call(bf16[16,128,4608]{2,1,0:T(8,128)(2,1)} %get-tuple-element.43.x_ref.refs_0_, bf16[2048,384]{1,0:T(8,128)(2,1)} %get-tuple-element.38.a_ref, bf16[2048,1152]{1,0:T(8,128)(2,1)} %get-tuple-element.39.b_ref), custom_call_target="tpu_custom_call" | custom-call | flops 28991029248 | bytes 18874368 | tf_op jit(solution)/shard_map/late_weights/pallas_call | solution.py:1340
  675.2 196.1 %backward.1 = (bf16[2048,1152]{1,0:T(8,128)(2,1)}, bf16[2048,512]{1,0:T(8,128)(2,1)}, bf16[288,9088]{1,0:T(8,128)(2,1)}, bf16[16,144,384]{2,1,0:T(8,128)(2,1)}) custom-call(bf16[16,128,4608]{2,1,0:T(8,128)(2,1)} %get-tuple-element.43.x_ref.refs_0_, bf16[4608,768]{1,0:T(8,128)(2,1)} %copy-done.1, bf16[4608,1152]{1,0:T(8,128)(2,1)} %get-tuple-element.40.wide_ref.refs_2_, ...), custom_call_target="tpu_custom_call" | custom-call | flops 35701915648 | bytes 18874368 | tf_op jit(solution)/shard_map/backward/pallas_call | solution.py:1247
  871.3 1.5 slice_bitcast_fusion.2
  872.8 1.5 slice_bitcast_fusion
  875.6 7.5 slice_convert_fusion
  883.1 1.7 fusion.16
  884.8 8.5 reduce-scatter.7.cloned.1.call-done
  893.4 43.1 %back_out.1.refs_3_ = bf16[16,128,4608]{2,1,0:T(8,128)(2,1)} custom-call(bf16[2048,512]{1,0:T(8,128)(2,1)} %get-tuple-element.54.a_ref.refs_1_, bf16[2048,1152]{1,0:T(8,128)(2,1)} %get-tuple-element.55.b_ref.refs_2_, bf16[4608,768]{1,0:T(8,128)(2,1)} %copy-done.1, bf16[4608,1152]{1,0:T(8,128)(2,1)} %copy-done), custom_call_target="tpu_custom_call" | custom-call | flops 31406948352 | bytes 18874368 | tf_op jit(solution)/shard_map/back_out/pallas_call | solution.py:1314
  936.5 328.4 %send.1 = (f32[128,4608]{1,0:T(8,128)}, f32[2,4608]{1,0:T(2,128)}, bf16[288,9088]{1,0:T(8,128)(2,1)}, bf16[16,144,512]{2,1,0:T(8,128)(2,1)}, bf16[4608,1152]{1,0...) custom-call(bf16[16,128,4608]{2,1,0:T(8,128)(2,1)} %get-tuple-elemen, ...), custom_call_target="tpu_custom_call" | custom-call | flops 31406948352 | bytes 18874368 | tf_op jit(solution)/shard_map/send/pallas_call | solution.py:911
  1264.9 1.1 slice_bitcast_fusion.3
  1266.1 1.2 slice_bitcast_fusion.1
  1268.0 1.5 slice_reduce_fusion
  1269.5 1.4 broadcast_select_fusion.3
  1271.7 7.2 slice_convert_fusion.1
  1278.9 2.0 copy.46
  1281.0 1.5 broadcast_in_dim_reshape.3
  1284.0 3.1 fusion.13
  1287.1 2.4 copy.42
  1289.5 1.5 slice_convert_fusion.2
  1291.0 1.5 reshape.175
  1292.8 2.9 add_convert_fusion.1
  (73 shorter events, 14.7 us)
Async XLA Ops:
  7.2 886.2 %reduce-scatter.7.cloned.1.call-start = ((), (), s32[]{:S(2)}) async-start(), calls=%async_computation.3 | async-start | bytes 23592960
  7.2 2.5 copy-start.5
  7.2 2.6 copy-start.6
  9.8 2.9 copy-start.2
  12.0 32.4 %collective-permute-start = (bf16[144,4608]{1,0:T(8,128)(2,1)}, bf16[144,4608]{1,0:T(8,128)(2,1)}, u32[]{:S(2)}, u32[]{:S(2)}) collective-permute-start(bf16[144,4608]{1,0:T(8,128)(2,1)} %get-tuple-element.65), channel_id=1, source_target_pairs={{0,1},{1,0},{2,3},{3,2},{4,5},{5,4},{6,7},{7,6},{8,9},{9,8},{10,11... | collective-permute-start | bytes 3981320 | tf_op jit(solution)/shard_map/ppermute | solution.py:1379
  24.8 5.3 copy-start.10
  39.5 6.2 copy-start.9
  46.5 2.4 copy-start.8
  52.4 6.7 slice-start
  55.1 1.6 copy-start.7
  56.8 2.3 slice-start.1
  311.1 3.9 copy-start
  314.9 3.0 copy-start.1
  627.1 0.7 copy-start.11
  627.1 1.7 copy-start.4
  627.1 660.0 %reduce-scatter.5.cloned.1.call-start = ((), (), s32[]{:S(2)}) async-start(), calls=%async_computation.2 | async-start | bytes 5898240 | tf_op jit(solution)/shard_map/reduce_scatter | solution.py:1493
  875.5 7.6 collective-permute-start.2
  1270.8 13.1 %collective-permute-start.1 = (bf16[144,2336]{1,0:T(8,128)(2,1)}, bf16[144,2336]{1,0:T(8,128)(2,1)}, u32[]{:S(2)}, u32[]{:S(2)}) collective-permute-start(bf16[144,2336]{1,0:T(8,128)(2,1)} %get-tuple-element.67), channel_id=1, source_target_pairs={{0,1},{1,0},{2,3},{3,2},{4,5},{5,4},{6,7},{7,6},{8,9},{9,8},{10,11... | collective-permute-start | bytes 2018312 | tf_op jit(solution)/shard_map/ppermute | solution.py:1379
  1280.9 1.5 copy-start.12
  1291.0 1.8 copy-start.3
Sparse Core Ops, SparseCore 0:
  627.2 266.0 reduce-scatter.6
  895.7 85.4 reduce-scatter.4
